TPU v7x, 32 devices: a whole 2x2x4 slice. The times are simulated.
32 devices in a mesh: dp: 8 (over z, y), seq: 4 (over x, core).
Axes of the slice: x: 2, y: 2, z: 4, core: 2. Of those that a mesh axis runs over, the one named last changes fastest.
Arguments:
- tokens: bfloat16 [16, 1024, 1536], P(None, ('dp', 'seq')), may hold values from -6 to 6
- cotangent: bfloat16 [16, 1024, 1536], P(None, ('dp', 'seq')), may hold values from -6 to 6
- routes: int32 [16, 1024, 8], P(None, ('dp', 'seq')), may hold values from 0 to 11, as said below
- lengths: int32 [16], replicated, may hold values from 128 to 1024, as said below
- deal_order: int32 [16], replicated, may hold values from 0 to 15, as said below
- attn_gain: float32 [1536], P('dp'), may hold values from 0.5 to 1.5
- query_weight: float32 [1536, 1536], P('dp'), may hold values from -0.15625 to 0.15625
- key_matrix: float32 [1536, 512], P('dp'), may hold values from -0.15625 to 0.15625
- value_matrix: float32 [1536, 512], P('dp'), may hold values from -0.15625 to 0.15625
- out_weight: float32 [1536, 1536], P('dp'), may hold values from -1.75 to 1.75
- moe_gain: float32 [1536], P('dp'), may hold values from 0.5 to 1.5
- router_weight: float32 [1536, 12], P('dp'), may hold values from -0.078125 to 0.078125
- expert_weight: float32 [1536, 12, 1536], P('dp'), may hold values from -0.3125 to 0.3125
Outputs:
- output: float32 [16, 1024, 1536], P(None, ('dp', 'seq'))
- grad_tokens: float32 [16, 1024, 1536], P(None, ('dp', 'seq'))
- grad_attn_gain: float32 [1536], P('dp')
- grad_query: float32 [1536, 1536], P('dp')
- grad_key: float32 [1536, 512], P('dp')
- grad_value: float32 [1536, 512], P('dp')
- grad_out: float32 [1536, 1536], P('dp')
- grad_moe_gain: float32 [1536], P('dp')
- grad_router: float32 [1536, 12], P('dp')
- grad_experts: float32 [1536, 12, 1536], P('dp')
Inputs may be any that keep to these rules, and one draw needn't show every extreme that they name: Every length is a multiple of 128; lengths[deal_order[2k]] + lengths[deal_order[2k+1]] = 1152 for every k; some length equals 1024. `deal_order`: A permutation of the sequences. `routes`: each row names 8 different experts. For each g < 8 and s < 4, take the slots p < length of the sequences deal_order[2g] and deal_order[2g + 1] with (p // 32) % 4 == s: among these rows each expert is named at most 216 times, and some expert exactly 216 times.
All inputs are finite; a program needn't handle non-finite values.
Results may differ from a plain program's by a relative error of at most 0.023.
Values may be sent and summed in bfloat16 or wider, within the bound.
No kernel may reach another device: no remote copies, remote signals or barrier semaphores. Data moves between devices by JAX's collectives and lax.ppermute only.
A program may use at most 640 MiB of HBM per device.

v0:
```python
import jax
import jax.numpy as jnp
from jax import lax
from jax.sharding import PartitionSpec as P

QUERY_HEADS = 24
KEY_VALUE_HEADS = 8
HEAD_SIZE = 64
PAIR_TOK = 1152


eps_norm = 1e-06
rope_base = 10000.0
score_scale = 0.125


def norm_scale(values, gain):
    inverse = lax.rsqrt(jnp.mean(values * values, axis=-1, keepdims=True) + eps_norm)
    return values * inverse * gain


def norm_back(values, gain, upstream):
    inverse = lax.rsqrt(jnp.mean(values * values, axis=-1, keepdims=True) + eps_norm)
    normed = values * inverse
    scaled = upstream * gain
    grad_values = inverse * (scaled - normed * jnp.mean(scaled * normed, axis=-1, keepdims=True))
    return (grad_values, jnp.sum(upstream * normed, axis=0))


def rotate(values, cosine, sine):
    middle = values.shape[-1] // 2
    first = values[..., :middle]
    second = values[..., middle:]
    return jnp.concatenate(
        [first * cosine - second * sine, second * cosine + first * sine], axis=-1
    )


def body(
    tokens,
    cotangent,
    routes,
    lengths,
    deal_order,
    attn_gain,
    query_weight,
    key_matrix,
    value_matrix,
    out_weight,
    moe_gain,
    router_weight,
    expert_weight,
):
    n_data = lax.axis_size("dp")
    member_count = lax.axis_size("seq")
    group = lax.axis_index("dp")
    member = lax.axis_index("seq")
    width = tokens.shape[2]
    block = tokens.shape[1]
    slots = tokens.shape[0] // n_data
    n_pairs = slots // 2
    quarter_tok = PAIR_TOK // member_count
    tokens_per_device = n_pairs * quarter_tok
    slot_rows = n_data * block
    q_width = QUERY_HEADS * HEAD_SIZE
    key_value_width = KEY_VALUE_HEADS * HEAD_SIZE
    heads_local = QUERY_HEADS // member_count
    key_value_local = KEY_VALUE_HEADS // member_count
    queries_per_group = QUERY_HEADS // KEY_VALUE_HEADS
    n_expert = router_weight.shape[1]
    hidden_units = expert_weight.shape[2] // 3
    local_rows = expert_weight.shape[0]
    half_members = member_count // 2
    q_rows = half_members * quarter_tok
    key_count = member_count * quarter_tok
    n_blocks = n_pairs * 2 * key_value_local
    sent = (tokens[deal_order], cotangent[deal_order], routes[deal_order].astype(jnp.bfloat16))
    dealt_x, dealt_cot, dealt_routes = (
        lax.all_to_all(sent[0], "dp", split_axis=0, concat_axis=1, tiled=True),
        lax.all_to_all(sent[1], "dp", split_axis=0, concat_axis=1, tiled=True),
        lax.all_to_all(sent[2], "dp", split_axis=0, concat_axis=1, tiled=True),
    )
    slot_ids = lax.dynamic_slice_in_dim(deal_order, group * slots, slots)
    slot_len = lengths[slot_ids] // member_count
    first_len = slot_len[0::2]
    row_ids = jnp.arange(quarter_tok, dtype=jnp.int32)
    is_later = (row_ids[None, :] >= first_len[:, None]).astype(jnp.int32)
    slot_of = 2 * jnp.arange(n_pairs, dtype=jnp.int32)[:, None] + is_later
    local_row = row_ids[None, :] - first_len[:, None] * is_later
    flat_index = (slot_of * slot_rows + local_row).reshape(tokens_per_device)
    base_pos = local_row // block * member_count * block + local_row % block
    all_pos = base_pos[None] + (jnp.arange(member_count, dtype=jnp.int32) * block)[:, None, None]
    all_seg = jnp.broadcast_to(slot_of[None], all_pos.shape)
    own_pos = (base_pos + member * block).reshape(tokens_per_device)
    x_rows = dealt_x.reshape(slots * slot_rows, width)[flat_index]
    cot_rows = dealt_cot.reshape(slots * slot_rows, width)[flat_index]
    route_rows = dealt_routes.reshape(slots * slot_rows, dealt_routes.shape[2])[flat_index].astype(
        jnp.int32
    )
    gain_a, full_query, full_key, full_value, full_out = (
        lax.all_gather(attn_gain.astype(jnp.bfloat16), "dp", axis=0, tiled=True),
        lax.all_gather(query_weight.astype(jnp.bfloat16), "dp", axis=0, tiled=True),
        lax.all_gather(key_matrix.astype(jnp.bfloat16), "dp", axis=0, tiled=True),
        lax.all_gather(value_matrix.astype(jnp.bfloat16), "dp", axis=0, tiled=True),
        lax.all_gather(out_weight.astype(jnp.bfloat16), "dp", axis=0, tiled=True),
    )
    gain_a_float = gain_a.astype(jnp.float32)
    x_float = x_rows.astype(jnp.float32)
    attention_normed = norm_scale(x_float, gain_a_float).astype(jnp.bfloat16)
    query_linear = jnp.dot(
        attention_normed, full_query, preferred_element_type=jnp.float32
    ).reshape(tokens_per_device, QUERY_HEADS, HEAD_SIZE)
    key_linear = jnp.dot(attention_normed, full_key, preferred_element_type=jnp.float32).reshape(
        tokens_per_device, KEY_VALUE_HEADS, HEAD_SIZE
    )
    value_linear = jnp.dot(attention_normed, full_value, preferred_element_type=jnp.float32)
    freq = rope_base ** (-(jnp.arange(HEAD_SIZE // 2, dtype=jnp.float32) * 2.0 / HEAD_SIZE))
    angle = own_pos.astype(jnp.float32)[:, None] * freq[None, :]
    cosine = jnp.cos(angle)[:, None, :]
    sine = jnp.sin(angle)[:, None, :]
    query_rotated = (
        rotate(query_linear, cosine, sine).astype(jnp.bfloat16).reshape(tokens_per_device, q_width)
    )
    key_rotated = rotate(key_linear, cosine, sine).astype(jnp.bfloat16)
    key_value_packed = jnp.stack(
        [
            key_rotated,
            value_linear.astype(jnp.bfloat16).reshape(
                tokens_per_device, KEY_VALUE_HEADS, HEAD_SIZE
            ),
        ],
        axis=2,
    )
    key_value_packed = key_value_packed.reshape(tokens_per_device, 2 * key_value_width)
    query_heads, kv_heads = (
        lax.all_to_all(query_rotated, "seq", split_axis=1, concat_axis=0, tiled=True),
        lax.all_to_all(key_value_packed, "seq", split_axis=1, concat_axis=0, tiled=True),
    )

    def to_blocks(values):
        shaped = values.reshape(
            2, half_members, n_pairs, quarter_tok, key_value_local, queries_per_group, HEAD_SIZE
        )
        return shaped.transpose(2, 0, 4, 5, 1, 3, 6).reshape(
            n_blocks, queries_per_group, q_rows, HEAD_SIZE
        )

    def from_blocks(values):
        shaped = values.reshape(
            n_pairs, 2, key_value_local, queries_per_group, half_members, quarter_tok, HEAD_SIZE
        )
        return shaped.transpose(1, 4, 0, 5, 2, 3, 6).reshape(
            member_count * tokens_per_device, heads_local * HEAD_SIZE
        )

    query_blocks = to_blocks(query_heads)
    kv_shaped = kv_heads.reshape(member_count, n_pairs, quarter_tok, key_value_local, 2, HEAD_SIZE)
    kv_shaped = kv_shaped.transpose(1, 3, 0, 2, 4, 5).reshape(
        n_pairs * key_value_local, key_count, 2, HEAD_SIZE
    )
    key_blocks = kv_shaped[:, :, 0]
    value_blocks = kv_shaped[:, :, 1]
    query_pos = (
        all_pos.reshape(2, half_members, n_pairs, quarter_tok)
        .transpose(2, 0, 1, 3)
        .reshape(n_pairs * 2, q_rows)
    )
    query_seg = (
        all_seg.reshape(2, half_members, n_pairs, quarter_tok)
        .transpose(2, 0, 1, 3)
        .reshape(n_pairs * 2, q_rows)
    )
    key_pos = all_pos.transpose(1, 0, 2).reshape(n_pairs, key_count)
    key_seg = all_seg.transpose(1, 0, 2).reshape(n_pairs, key_count)

    def block_scores(index):
        pair_idx = index // (2 * key_value_local)
        row_set = index // key_value_local
        kv_idx = pair_idx * key_value_local + index % key_value_local
        keys_here = key_blocks[kv_idx]
        scores = (
            jnp.einsum(
                "hrd,kd->hrk", query_blocks[index], keys_here, preferred_element_type=jnp.float32
            )
            * score_scale
        )
        allowed = (query_seg[row_set][:, None] == key_seg[pair_idx][None, :]) & (
            key_pos[pair_idx][None, :] <= query_pos[row_set][:, None]
        )
        return (jnp.where(allowed[None], scores, -jnp.inf), keys_here, value_blocks[kv_idx])

    def attend(index):
        scores, keys_here, values_here = block_scores(index)
        row_max = jnp.max(scores, axis=-1, keepdims=True)
        exponent = jnp.exp(scores - row_max)
        row_total = jnp.sum(exponent, axis=-1, keepdims=True)
        probability = (exponent / row_total).astype(jnp.bfloat16)
        mixed = jnp.einsum(
            "hrk,kd->hrd", probability, values_here, preferred_element_type=jnp.float32
        )
        return (mixed.astype(jnp.bfloat16), (row_max + jnp.log(row_total))[..., 0])

    block_ids = jnp.arange(n_blocks, dtype=jnp.int32)
    attended, log_total = lax.map(attend, block_ids)
    head_out = lax.all_to_all(from_blocks(attended), "seq", split_axis=0, concat_axis=1, tiled=True)
    middle = x_float + jnp.dot(head_out, full_out, preferred_element_type=jnp.float32)
    expert_local = (
        expert_weight.reshape(local_rows, n_expert, 3, hidden_units)
        .transpose(1, 2, 0, 3)
        .astype(jnp.bfloat16)
    )
    gain_m, full_router, full_experts = (
        lax.all_gather(moe_gain.astype(jnp.bfloat16), "dp", axis=0, tiled=True),
        lax.all_gather(router_weight.astype(jnp.bfloat16), "dp", axis=0, tiled=True),
        lax.all_gather(expert_local, "dp", axis=2, tiled=True),
    )
    gate_weights = full_experts[:, :2]
    down_weights = full_experts[:, 2]
    gain_m_float = gain_m.astype(jnp.float32)
    normed_m = norm_scale(middle, gain_m_float).astype(jnp.bfloat16)
    logits = jnp.dot(normed_m, full_router, preferred_element_type=jnp.float32)
    expert_ids = jnp.arange(n_expert, dtype=jnp.int32)
    chosen = jnp.sum(
        (route_rows[:, :, None] == expert_ids[None, None, :]).astype(jnp.int32), axis=1
    )
    gate_probs = jax.nn.softmax(jnp.where(chosen > 0, logits, -jnp.inf), axis=-1)
    capacity = 3 * tokens_per_device // 4
    slot_rank = jnp.cumsum(chosen, axis=0) - 1
    target = jnp.where(chosen > 0, slot_rank, capacity)
    token_ids = jnp.broadcast_to(
        jnp.arange(tokens_per_device, dtype=jnp.int32)[:, None], chosen.shape
    )
    dispatch = (
        jnp.zeros((n_expert, capacity), jnp.int32)
        .at[expert_ids[None, :], target]
        .set(token_ids, mode="drop")
    )
    used = (
        jnp.zeros((n_expert, capacity), jnp.float32)
        .at[expert_ids[None, :], target]
        .set(1.0, mode="drop")
    )
    expert_gate = gate_probs[dispatch, expert_ids[:, None]] * used
    disp_in = normed_m[dispatch]
    gate_up = jnp.einsum(
        "ecd,ekdf->eckf", disp_in, gate_weights, preferred_element_type=jnp.float32
    )
    gate_part = gate_up[:, :, 0]
    up_part = gate_up[:, :, 1]
    hidden_b = (jax.nn.silu(gate_part) * up_part).astype(jnp.bfloat16)
    branch = jnp.einsum("ecf,edf->ecd", hidden_b, down_weights, preferred_element_type=jnp.float32)
    disp_cot = cot_rows[dispatch]
    grad_gate = jnp.sum(disp_cot.astype(jnp.float32) * branch, axis=-1) * used
    combined = (
        jnp.zeros((tokens_per_device, width), jnp.float32)
        .at[dispatch]
        .add(expert_gate[..., None] * branch)
    )
    result = middle + combined
    scaled_cot = (expert_gate[..., None] * disp_cot.astype(jnp.float32)).astype(jnp.bfloat16)
    grad_hidden = jnp.einsum(
        "ecd,edf->ecf", scaled_cot, down_weights, preferred_element_type=jnp.float32
    )
    sigmoid_gate = jax.nn.sigmoid(gate_part)
    grad_gate_part = grad_hidden * up_part * sigmoid_gate * (1.0 + gate_part * (1.0 - sigmoid_gate))
    grad_up_part = grad_hidden * jax.nn.silu(gate_part)
    grad_gate_up = jnp.stack([grad_gate_part, grad_up_part], axis=2).astype(jnp.bfloat16)
    grad_disp_in = jnp.einsum(
        "eckf,ekdf->ecd", grad_gate_up, gate_weights, preferred_element_type=jnp.float32
    )
    grad_gate_flat = grad_gate_up.reshape(n_expert, capacity, 2 * hidden_units)
    grad_probs = (
        jnp.zeros((tokens_per_device, n_expert), jnp.float32)
        .at[dispatch, expert_ids[:, None]]
        .add(grad_gate)
    )
    grad_logits = (
        gate_probs * (grad_probs - jnp.sum(gate_probs * grad_probs, axis=-1, keepdims=True))
    ).astype(jnp.bfloat16)
    grad_normed_m = (
        jnp.zeros((tokens_per_device, width), jnp.float32).at[dispatch].add(grad_disp_in)
    )
    grad_normed_m = grad_normed_m + jnp.einsum(
        "te,de->td", grad_logits, full_router, preferred_element_type=jnp.float32
    )
    grad_router_term = jnp.einsum(
        "td,te->de", normed_m, grad_logits, preferred_element_type=jnp.float32
    )
    grad_mid_norm, grad_gain_m = norm_back(middle, gain_m_float, grad_normed_m)
    grad_mid = cot_rows.astype(jnp.float32) + grad_mid_norm
    grad_mix = grad_mid.astype(jnp.bfloat16)
    grad_out_term = jnp.einsum("tq,td->qd", head_out, grad_mix, preferred_element_type=jnp.float32)
    grad_head = jnp.einsum(
        "td,qd->tq", grad_mix, full_out, preferred_element_type=jnp.float32
    ).astype(jnp.bfloat16)
    grad_heads_here = lax.all_to_all(grad_head, "seq", split_axis=1, concat_axis=0, tiled=True)
    grad_blocks = to_blocks(grad_heads_here)

    def attend_back(index):
        scores, keys_here, values_here = block_scores(index)
        probability = jnp.exp(scores - log_total[index][..., None])
        grad_here = grad_blocks[index]
        grad_prob = jnp.einsum(
            "hrd,kd->hrk", grad_here, values_here, preferred_element_type=jnp.float32
        )
        row_delta = jnp.sum(grad_prob * probability, axis=-1, keepdims=True)
        grad_scores = (probability * (grad_prob - row_delta)).astype(jnp.bfloat16)
        grad_query_blk = (
            jnp.einsum("hrk,kd->hrd", grad_scores, keys_here, preferred_element_type=jnp.float32)
            * score_scale
        )
        grad_key_blk = (
            jnp.einsum(
                "hrk,hrd->kd", grad_scores, query_blocks[index], preferred_element_type=jnp.float32
            )
            * score_scale
        )
        grad_value_blk = jnp.einsum(
            "hrk,hrd->kd",
            probability.astype(jnp.bfloat16),
            grad_here,
            preferred_element_type=jnp.float32,
        )
        return (grad_query_blk, jnp.stack([grad_key_blk, grad_value_blk], axis=1))

    grad_query_blocks, grad_kv_blocks = lax.map(attend_back, block_ids)
    grad_kv_sum = jnp.sum(
        grad_kv_blocks.reshape(n_pairs, 2, key_value_local, key_count, 2, HEAD_SIZE), axis=1
    )
    grad_kv_sum = grad_kv_sum.reshape(
        n_pairs, key_value_local, member_count, quarter_tok, 2, HEAD_SIZE
    ).transpose(2, 0, 3, 1, 4, 5)
    grad_kv_send = grad_kv_sum.reshape(
        member_count * tokens_per_device, key_value_local * 2 * HEAD_SIZE
    ).astype(jnp.bfloat16)
    grad_query_send = from_blocks(grad_query_blocks).astype(jnp.bfloat16)
    grad_query_rows, key_value_grad_rows = (
        lax.all_to_all(grad_query_send, "seq", split_axis=0, concat_axis=1, tiled=True),
        lax.all_to_all(grad_kv_send, "seq", split_axis=0, concat_axis=1, tiled=True),
    )
    grad_query_lin = rotate(
        grad_query_rows.astype(jnp.float32).reshape(tokens_per_device, QUERY_HEADS, HEAD_SIZE),
        cosine,
        -sine,
    )
    grad_query_lin = grad_query_lin.astype(jnp.bfloat16).reshape(tokens_per_device, q_width)
    key_value_grad_parts = key_value_grad_rows.reshape(
        tokens_per_device, KEY_VALUE_HEADS, 2, HEAD_SIZE
    )
    grad_key_lin = (
        rotate(key_value_grad_parts[:, :, 0].astype(jnp.float32), cosine, -sine)
        .astype(jnp.bfloat16)
        .reshape(tokens_per_device, key_value_width)
    )
    grad_value_lin = key_value_grad_parts[:, :, 1].reshape(tokens_per_device, key_value_width)
    grad_query_term = jnp.einsum(
        "td,tq->dq", attention_normed, grad_query_lin, preferred_element_type=jnp.float32
    )
    grad_key_term = jnp.einsum(
        "td,tq->dq", attention_normed, grad_key_lin, preferred_element_type=jnp.float32
    )
    grad_value_term = jnp.einsum(
        "td,tq->dq", attention_normed, grad_value_lin, preferred_element_type=jnp.float32
    )
    grad_normed_a = jnp.einsum(
        "tq,dq->td", grad_query_lin, full_query, preferred_element_type=jnp.float32
    )
    grad_normed_a = grad_normed_a + jnp.einsum(
        "tq,dq->td", grad_key_lin, full_key, preferred_element_type=jnp.float32
    )
    grad_normed_a = grad_normed_a + jnp.einsum(
        "tq,dq->td", grad_value_lin, full_value, preferred_element_type=jnp.float32
    )
    grad_x_norm, grad_gain_a = norm_back(x_float, gain_a_float, grad_normed_a)
    grad_input = grad_mid + grad_x_norm
    up_term = jnp.einsum(
        "ecd,ecf->def", disp_in, grad_gate_flat, preferred_element_type=jnp.float32
    )
    down_term = jnp.einsum("ecd,ecf->def", scaled_cot, hidden_b, preferred_element_type=jnp.float32)
    expert_share = lax.psum_scatter(
        jnp.concatenate([up_term, down_term], axis=2).astype(jnp.bfloat16),
        "dp",
        scatter_dimension=0,
        tiled=True,
    )
    small_share = (
        lax.psum_scatter(
            grad_gain_a.astype(jnp.bfloat16), "dp", scatter_dimension=0, tiled=True
        ).astype(jnp.float32),
        lax.psum_scatter(
            grad_gain_m.astype(jnp.bfloat16), "dp", scatter_dimension=0, tiled=True
        ).astype(jnp.float32),
        lax.psum_scatter(
            grad_query_term.astype(jnp.bfloat16), "dp", scatter_dimension=0, tiled=True
        ).astype(jnp.float32),
        lax.psum_scatter(
            grad_key_term.astype(jnp.bfloat16), "dp", scatter_dimension=0, tiled=True
        ).astype(jnp.float32),
        lax.psum_scatter(
            grad_value_term.astype(jnp.bfloat16), "dp", scatter_dimension=0, tiled=True
        ).astype(jnp.float32),
        lax.psum_scatter(
            grad_out_term.astype(jnp.bfloat16), "dp", scatter_dimension=0, tiled=True
        ).astype(jnp.float32),
        lax.psum_scatter(
            grad_router_term.astype(jnp.bfloat16), "dp", scatter_dimension=0, tiled=True
        ).astype(jnp.float32),
    )
    summed = (
        lax.psum(small_share[0].astype(jnp.bfloat16), "seq").astype(jnp.float32),
        lax.psum(small_share[2].astype(jnp.bfloat16), "seq").astype(jnp.float32),
        lax.psum(small_share[3].astype(jnp.bfloat16), "seq").astype(jnp.float32),
        lax.psum(small_share[4].astype(jnp.bfloat16), "seq").astype(jnp.float32),
        lax.psum(small_share[5].astype(jnp.bfloat16), "seq").astype(jnp.float32),
        lax.psum(small_share[1].astype(jnp.bfloat16), "seq").astype(jnp.float32),
        lax.psum(small_share[6].astype(jnp.bfloat16), "seq").astype(jnp.float32),
        lax.psum(expert_share, "seq").astype(jnp.float32),
    )

    def unpack(row_values):
        filled = jnp.zeros((slots * slot_rows, width), jnp.float32).at[flat_index].set(row_values)
        return filled.reshape(slots, slot_rows, width)

    back_out, back_grad = (
        lax.all_to_all(
            unpack(result).astype(jnp.bfloat16), "dp", split_axis=1, concat_axis=0, tiled=True
        ).astype(jnp.float32),
        lax.all_to_all(
            unpack(grad_input).astype(jnp.bfloat16), "dp", split_axis=1, concat_axis=0, tiled=True
        ).astype(jnp.float32),
    )
    output = jnp.zeros_like(back_out).at[deal_order].set(back_out)
    grad_tokens = jnp.zeros_like(back_grad).at[deal_order].set(back_grad)
    return (
        output,
        grad_tokens,
        summed[0],
        summed[1],
        summed[2],
        summed[3],
        summed[4],
        summed[5],
        summed[6],
        summed[7],
    )


def solution(mesh):
    placed = (
        P(None, ("dp", "seq"), None),
        P(None, ("dp", "seq"), None),
        P(None, ("dp", "seq"), None),
        P(),
        P(),
        P("dp"),
        P("dp", None),
        P("dp", None),
        P("dp", None),
        P("dp", None),
        P("dp"),
        P("dp", None),
        P("dp", None, None),
    )
    return jax.shard_map(
        body,
        mesh=mesh,
        in_specs=placed,
        out_specs=(
            P(None, ("dp", "seq"), None),
            P(None, ("dp", "seq"), None),
            P("dp"),
            P("dp", None),
            P("dp", None),
            P("dp", None),
            P("dp", None),
            P("dp"),
            P("dp", None),
            P("dp", None, None),
        ),
        check_vma=False,
    )
```

profile of v0, /device:TPU:1, one launch (start us, length us, event | category | flops | bytes accessed | tf_op | source)
XLA Modules:
  0.0 3182.5 jit_solution(17394966877893169736)
XLA Ops:
  14.1 8.9 convert_element_type.315
  23.1 6.7 copy.266
  31.9 6.4 all-to-all-start.4
  52.3 37.8 %all-reduce.6 = (bf16[1536]{0:T(1024)(128)(2,1)S(1)}, bf16[1536]{0:T(1024)(128)(2,1)S(1)}) all-reduce(bf16[1536]{0:T(1024)(128)(2,1)S(1)} %dynamic-update-slice, bf16[1536]{0:T(1024)(128)(2,1)S(1)} %dynamic-update-slice.1), channel_id=1, replica_groups=mesh['dp'=8,'seq'=4] {'dp'}, use_global_device_ids=true, to_apply=%add.1 | all-reduce | flops 3072 | bytes 12288
  90.3 34.8 %all-gather = bf16[8,192,12]{1,2,0:T(8,128)(2,1)S(1)} all-gather(bf16[1,192,12]{1,2,0:T(8,128)(2,1)S(1)} %convert_bitcast_fusion.5), channel_id=1, replica_groups=mesh['dp'=8,'seq'=4] {'dp'}, dimensions={0}, use_global_device_ids=true | all-gather | bytes 41472 | tf_op jit(solution)/shard_map/all_gather | solution.py:214
  130.9 17.0 scatter_custom_fusion.6
  157.0 14.9 all-to-all-start.2
  171.9 25.4 all-gather.7.cloned.1.call-done
  203.9 5.1 all-to-all-start.1
  211.5 9.5 all-to-all-done.1
  232.3 56.2 %while.32 = (s32[]{:T(128)}, bf16[4,3,576,64]{2,3,1,0:T(8,128)(2,1)}, f32[4,3,576]{2,1,0:T(4,128)}, s32[4]{0:T(128)S(1)}, s32[2,576]{1,0:T(2,128)S(1)}, /*index=...) while((s32[]{:T(128)}, ...), condition=%wide.region_4.5_spmd.clone, body=%wide.region_1.4_spmd.clone.sunk | while | flops 535596512 | bytes 28627092 | solution.py:204
  302.9 17.0 scatter_custom_fusion.7
  323.9 10.2 gather_fusion.9
  341.3 10.1 gather_fusion.6
  351.8 1020.7 %all-gather.15.cloned.1.call-done = bf16[12,3,1536,512]{3,2,1,0:T(8,128)(2,1)} async-done(((bf16[12,3,192,512]{3,2,1,0:T(8,128)(2,1)}), bf16[12,3,1536,512]{3,2,1,0:T(8,128)(2,1)}) %all-gather.15.cloned.1.call-update) | async-done | bytes 56623120 | tf_op jit(solution)/shard_map/all_gather | solution.py:215
  1372.5 20.7 fusion.122
  1393.1 5.0 multiply_convert_fusion.1
  1398.1 18.4 fusion.59
  1416.7 19.8 scatter_custom_fusion.8
  1436.6 20.4 gather_fusion.5
  1457.2 12.7 convert_bitcast_fusion.1
  1469.9 17.2 multiply_bitcast_fusion.1
  1493.1 19.6 convert_bitcast_fusion
  1512.7 38.6 %pad_maximum_fusion = bf16[1536,12,1536]{0,2,1:T(8,128)(2,1)} fusion(bf16[1536,12,512]{0,2,1:T(8,128)(2,1)} %convert_bitcast_fusion.1, bf16[1536,12,1024]{0,2,1:T(8,128)(2,1)} %convert_bitcast_fusion), kind=kLoop, calls=%fused_computation.89 | loop fusion | flops 113246208 | bytes 113246208 | tf_op jit(solution)/shard_map/concatenate | solution.py:381
  1551.3 72.8 %copy.253 = bf16[1536,18432]{1,0:T(8,128)(2,1)} copy(bf16[1536,18432]{0,1:T(8,128)(2,1)} %bitcast.341) | data formatting | bytes 113246208
  1625.3 23.7 fusion.55
  1649.0 32.2 %scatter_fusion.2 = f32[288,1536]{1,0:T(8,128)S(1)} fusion(f32[288,1536]{1,0:T(8,128)S(1)} %fusion.130, s32[2592]{0:T(1024)S(1)} %copy-done.45, f32[2592,1536]{1,0:T(8,128)} %bitcast.354), kind=kCustom, calls=%fused_computation.13 | custom fusion | flops 3981312 | bytes 47786112 | tf_op jit(solution)/shard_map/scatter-add | solution.py:281
  1694.1 11.9 all-to-all-done.7
  1713.1 68.2 %while.33 = (s32[]{:T(128)}, bf16[4,3,576,64]{2,3,1,0:T(8,128)(2,1)}, f32[4,1152,2,64]{1,3,2,0:T(8,128)}, s32[4]{0:T(128)S(1)}, s32[2,576]{1,0:T(2,128)S(1)}, /*...) while((s32[]{:T(128)}, ...), condition=%wide.region_23.24_spmd.clone, body=%wide.region_21.23_spmd.clone.sunk | while | flops 1294257664 | bytes 74258696 | solution.py:326
  1784.6 13.2 all_to_all.150
  1806.1 6.5 convolution_convert_fusion
  1820.6 15.0 all_to_all.151
  1848.4 11.3 broadcast_multiply_fusion
  1859.7 32.5 %scatter_fusion = f32[288,1536]{1,0:T(8,128)S(1)} fusion(f32[288,1536]{1,0:T(8,128)S(1)} %copy-done.3, s32[2592]{0:T(1024)S(1)} %copy-done.45, f32[2592,1536]{1,0:T(8,128)} %bitcast.345), kind=kCustom, calls=%fused_computation.10 | custom fusion | flops 3981312 | bytes 47786112 | tf_op jit(solution)/shard_map/scatter-add | solution.py:257
  1906.7 5.1 fusion.131
  1911.8 630.9 %reduce-scatter.21.cloned.1.call-done = bf16[192,18432]{1,0:T(8,128)(2,1)} async-done(((bf16[1536,18432]{1,0:T(8,128)(2,1)}), bf16[192,18432]{1,0:T(8,128)(2,1)}) %reduce-scatter.21.cloned.1.call-update) | async-done | bytes 7077904
  2542.7 11.4 copy.254
  2554.1 55.2 %reduce-scatter.13.cloned.1.call-done = bf16[192,512]{1,0:T(8,128)(2,1)} async-done(((bf16[1536,512]{1,0:T(8,128)(2,1)}), bf16[192,512]{1,0:T(8,128)(2,1)}) %reduce-scatter.13.cloned.1.call-update) | async-done | bytes 196624 | tf_op jit(solution)/shard_map/reduce_scatter | solution.py:396
  2609.3 67.3 %reduce-scatter.15.cloned.1.call-done = bf16[192,512]{1,0:T(8,128)(2,1)} async-done(((bf16[1536,512]{1,0:T(8,128)(2,1)}), bf16[192,512]{1,0:T(8,128)(2,1)}) %reduce-scatter.15.cloned.1.call-update) | async-done | bytes 196624 | tf_op jit(solution)/shard_map/reduce_scatter | solution.py:399
  2676.5 99.6 %reduce-scatter.17.cloned.1.call-done = bf16[192,1536]{1,0:T(8,128)(2,1)} async-done(((bf16[1536,1536]{1,0:T(8,128)(2,1)}), bf16[192,1536]{1,0:T(8,128)(2,1)}) %reduce-scatter.17.cloned.1.call-update) | async-done | bytes 589840 | tf_op jit(solution)/shard_map/reduce_scatter | solution.py:402
  2776.1 99.1 %reduce-scatter.11.cloned.1.call-done = bf16[192,1536]{1,0:T(8,128)(2,1)} async-done(((bf16[1536,1536]{1,0:T(8,128)(2,1)}), bf16[192,1536]{1,0:T(8,128)(2,1)}) %reduce-scatter.11.cloned.1.call-update) | async-done | bytes 589840 | tf_op jit(solution)/shard_map/reduce_scatter | solution.py:393
  2894.8 59.3 %reduce-scatter.19.cloned.1.call-done = bf16[192,12]{1,0:T(8,128)(2,1)} async-done(((bf16[1536,12]{1,0:T(8,128)(2,1)}), bf16[192,12]{1,0:T(8,128)(2,1)}) %reduce-scatter.19.cloned.1.call-update) | async-done | bytes 4624
  2955.0 16.2 all-reduce.5
  2971.5 11.7 all-reduce.7
  2990.8 7.1 scatter_fusion.1
  3002.4 7.0 scatter_fusion.3
  3009.4 146.1 %all-reduce.11.cloned.1.call-done = (bf16[192,12,1536]{0,2,1:T(8,128)(2,1)}, bf16[192,1536]{1,0:T(8,128)(2,1)}, bf16[192,512]{1,0:T(8,128)(2,1)}, bf16[192,512]{1,0:T(8,128)(2,1)}, bf16[192,1536]{1,0:T(8,128)(2,1)}) async-done(((bf16[192,12,1536]{0,2,1:T(8,128)(2,1)}, bf16[192,1536]{1,0:T(8,128)(2,1)}, bf16[192,512]{1,0:T(8,128)(2,1)}, bf16[192,512]{1,0:T(8,128)(2,1)}, bf16[192,1536]{1,0:T(8,128)(2,1)}), ...) | async-done | bytes 8650768 | tf_op jit(solution)/shard_map/psum | solution.py:417
  3162.4 13.1 copy.243
  (513 shorter events, 287.8 us)
Async XLA Ops:
  7.2 31.2 copy-start
  7.2 143.6 %all-gather.11.cloned.1.call-start = ((), (), s32[]{:S(2)}) async-start(), calls=%async_computation.19 | async-start | bytes 1769472 | tf_op jit(solution)/shard_map/all_gather | solution.py:104
  9.1 144.0 %all-gather.9.cloned.1.call-start = ((), (), s32[]{:S(2)}) async-start(), calls=%async_computation.18 | async-start | bytes 1769472 | tf_op jit(solution)/shard_map/all_gather | solution.py:103
  10.9 186.4 %all-gather.7.cloned.1.call-start = ((), (), s32[]{:S(2)}) async-start(), calls=%async_computation.17 | async-start | bytes 5308416 | tf_op jit(solution)/shard_map/all_gather | solution.py:102
  13.1 322.3 %all-gather.13.cloned.1.call-start = ((), (), s32[]{:S(2)}) async-start(), calls=%async_computation.20 | async-start | bytes 5308416 | tf_op jit(solution)/shard_map/all_gather | solution.py:105
  14.1 1358.4 %all-gather.15.cloned.1.call-start = ((), (), s32[]{:S(2)}) async-start(), calls=%async_computation.21 | async-start | bytes 63700992 | tf_op jit(solution)/shard_map/all_gather | solution.py:215
  30.5 13.4 copy-start.70
  31.9 11.9 all-to-all-start.4
  43.8 104.3 %all-to-all-start = ((bf16[16,32,1536]{2,1,0:T(8,128)(2,1)}), bf16[16,32,1536]{2,1,0:T(8,128)(2,1)S(1)}, u32[]{:S(2)}, u32[]{:S(2)}) async-start(bf16[16,32,1536]{2,1,0:T(8,128)(2,1)} %gather_fusion.1), calls=%async_computation | async-start | bytes 3145728 | tf_op jit(solution)/shard_map/all_to_all | solution.py:79
  47.5 42.8 %copy-start.68 = (f32[192,12]{0,1:T(8,128)S(1)}, f32[192,12]{0,1:T(8,128)}, u32[]{:S(2)}) copy-start(f32[192,12]{0,1:T(8,128)} %param.28) | copy-start | bytes 27652
  47.6 82.9 %copy-start.76 = (s32[2]{0:T(128)S(1)}, s32[2]{0:T(128)}, u32[]{:S(2)}) copy-start(s32[2]{0:T(128)} %constant.322) | copy-start | bytes 28
  47.6 83.0 %copy-start.75 = (s32[2]{0:T(128)S(1)}, s32[2]{0:T(128)}, u32[]{:S(2)}) copy-start(s32[2]{0:T(128)} %constant.325) | copy-start | bytes 28
  90.2 107.1 %copy-start.56 = (f32[1536]{0:T(1024)}, f32[1536]{0:T(1024)S(1)}, u32[]{:S(2)}) copy-start(f32[1536]{0:T(1024)S(1)} %convert_element_type.299) | copy-start | bytes 18436
  90.2 249.6 %copy-start.52 = (f32[1536]{0:T(1024)}, f32[1536]{0:T(1024)S(1)}, u32[]{:S(2)}) copy-start(f32[1536]{0:T(1024)S(1)} %convert_element_type.312) | copy-start | bytes 18436
  126.8 75.1 %copy-start.26 = (f32[288,32]{0,1:T(8,128)}, f32[288,32]{0,1:T(8,128)S(1)}, u32[]{:S(2)}) copy-start(f32[288,32]{0,1:T(8,128)S(1)} %get-tuple-element.630) | copy-start | bytes 110596
  150.4 46.8 %copy-start.10 = (bf16[288,1536]{1,0:T(8,128)(2,1)}, bf16[288,1536]{1,0:T(8,128)(2,1)S(1)}, u32[]{:S(2)}) copy-start(bf16[288,1536]{1,0:T(8,128)(2,1)S(1)} %gather_fusion.2) | copy-start | bytes 2654212
  150.7 46.5 %copy-start.65 = (f32[288]{0:T(512)}, f32[288]{0:T(512)S(1)}, u32[]{:S(2)}) copy-start(f32[288]{0:T(512)S(1)} %add_rsqrt_fusion.1) | copy-start | bytes 3460
  157.0 46.9 %all-to-all-start.2 = ((bf16[288,4,256]{2,0,1:T(8,128)(2,1)}), bf16[288,4,256]{2,0,1:T(8,128)(2,1)S(1)}, u32[]{:S(2)}, u32[]{:S(2)}) async-start(bf16[288,4,256]{2,0,1:T(8,128)(2,1)} %copy.210), calls=%async_computation.2 | async-start | bytes 1179648 | tf_op jit(solution)/shard_map/all_to_all | solution.py:137
  203.9 17.1 all-to-all-start.1
  221.9 75.6 %all-to-all-start.6 = ((bf16[16,32,1536]{2,1,0:T(8,128)(2,1)}), bf16[16,32,1536]{2,1,0:T(8,128)(2,1)S(1)}, u32[]{:S(2)}, u32[]{:S(2)}) async-start(bf16[16,32,1536]{2,1,0:T(8,128)(2,1)} %gather_fusion.7), calls=%async_computation.6 | async-start | bytes 3145728 | tf_op jit(solution)/shard_map/all_to_all | solution.py:80
  297.5 22.7 copy-start.14
  297.5 36.6 %all-to-all-start.3 = ((bf16[4,288,384]{2,1,0:T(8,128)(2,1)}), bf16[4,288,384]{2,1,0:T(8,128)(2,1)}, u32[]{:S(2)}, u32[]{:S(2)}) async-start(bf16[4,288,384]{2,1,0:T(8,128)(2,1)} %copy.214), calls=%async_computation.3 | async-start | bytes 1769472 | tf_op jit(solution)/shard_map/all_to_all | solution.py:205
  302.4 2240.3 %reduce-scatter.21.cloned.1.call-start = ((), (), s32[]{:S(2)}) async-start(), calls=%async_computation.27 | async-start | bytes 63700992
  302.9 18.8 copy-start.44
  323.9 10.2 copy-start.6
  323.9 11.5 copy-start.11
  339.8 11.5 copy-start.62
  341.2 10.1 copy-start.4
  341.3 10.1 copy-start.38
  1398.1 18.4 copy-start.9
  1457.2 12.7 copy-start.50
  1624.9 24.1 copy-start.54
  1625.3 23.7 copy-start.45
  1649.0 32.2 %copy-start.3 = (f32[288,1536]{1,0:T(8,128)S(1)}, f32[288,1536]{1,0:T(8,128)}, u32[]{:S(2)}) copy-start(f32[288,1536]{1,0:T(8,128)} %copy-done.2) | copy-start | bytes 5308420
  1649.0 32.2 %copy-start.63 = (f32[288]{0:T(512)S(1)}, f32[288]{0:T(512)}, u32[]{:S(2)}) copy-start(f32[288]{0:T(512)} %copy-done.62) | copy-start | bytes 3460
  1689.3 16.8 all-to-all-start.7
  1694.1 915.2 %reduce-scatter.13.cloned.1.call-start = ((), (), s32[]{:S(2)}) async-start(), calls=%async_computation.23 | async-start | bytes 1769472 | tf_op jit(solution)/shard_map/reduce_scatter | solution.py:396
  1783.9 16.3 copy-start.27
  1784.0 16.3 copy-start.36
  1803.5 873.0 %reduce-scatter.15.cloned.1.call-start = ((), (), s32[]{:S(2)}) async-start(), calls=%async_computation.24 | async-start | bytes 1769472 | tf_op jit(solution)/shard_map/reduce_scatter | solution.py:399
  1806.0 970.1 %reduce-scatter.17.cloned.1.call-start = ((), (), s32[]{:S(2)}) async-start(), calls=%async_computation.25 | async-start | bytes 5308416 | tf_op jit(solution)/shard_map/reduce_scatter | solution.py:402
  1812.6 1062.6 %reduce-scatter.11.cloned.1.call-start = ((), (), s32[]{:S(2)}) async-start(), calls=%async_computation.22 | async-start | bytes 5308416 | tf_op jit(solution)/shard_map/reduce_scatter | solution.py:393
  1900.7 989.1 %all-to-all-start.5 = ((bf16[2,256,1536]{2,0,1:T(2,128)(2,1)}), bf16[2,256,1536]{2,0,1:T(2,128)(2,1)}, u32[]{:S(2)}, u32[]{:S(2)}) async-start(bf16[2,256,1536]{2,0,1:T(2,128)(2,1)} %copy.224), calls=%async_computation.5 | async-start | bytes 3145728 | tf_op jit(solution)/shard_map/all_to_all | solution.py:425
  1905.3 1048.8 %reduce-scatter.19.cloned.1.call-start = ((), (), s32[]{:S(2)}) async-start(), calls=%async_computation.26 | async-start | bytes 442368
  1906.6 1248.9 %all-reduce.11.cloned.1.call-start = ((), (), s32[]{:S(2)}) async-start(), calls=%async_computation.28 | async-start | bytes 22020096 | tf_op jit(solution)/shard_map/psum | solution.py:417
  2887.0 68.0 %copy-start.67 = (bf16[1536]{0:T(1024)(128)(2,1)S(1)}, bf16[1536]{0:T(1024)(128)(2,1)}, u32[]{:S(2)}) copy-start(bf16[1536]{0:T(1024)(128)(2,1)} %get-tuple-element.532) | copy-start | bytes 9220
  2889.8 108.1 %all-to-all-start.10 = ((bf16[2,256,1536]{2,0,1:T(2,128)(2,1)}), bf16[2,256,1536]{2,0,1:T(2,128)(2,1)S(1)}, u32[]{:S(2)}, u32[]{:S(2)}) async-start(bf16[2,256,1536]{2,0,1:T(2,128)(2,1)} %copy.239), calls=%async_computation.10 | async-start | bytes 3145728 | tf_op jit(solution)/shard_map/all_to_all | solution.py:428
  3162.4 13.1 copy-start.1
  (68 other events, 250.5 us)
Sparse Core Ops, SparseCore 0:
  10.8 49.3 all-gather.10
  62.9 53.0 all-gather.8
  118.8 78.3 all-gather.6
  199.3 102.9 all-gather.12
  303.6 1068.7 all-gather.14
  1624.2 918.4 reduce-scatter.20
  2546.5 62.7 reduce-scatter.12
  2612.7 63.7 reduce-scatter.14
  2680.6 95.4 reduce-scatter.16
  2780.1 95.1 reduce-scatter.10
  2879.5 74.6 reduce-scatter.18
  2957.7 197.7 all-reduce.10
where the time goes:
time: 3200 us; the launch traced here: 3180 us
  waiting for transfers between devices  2230 us (70%)
  local copies, waits for them, and re-layouts  296 us (9%)
  other arithmetic  214 us (7%)
  matrix products  213 us (7%)
  blocking collectives  129 us (4%)
  starting transfers between devices  52.9 us (2%)
  loops' own time  32.1 us (1%)
    all_gather x1, waiting for transfers between devices, body(): lax.all_gather(expert_local, 'dp', axis=2, tiled=True)  1020 us
    unnamed x14, waiting for transfers between devices  690 us
    psum x1, waiting for transfers between devices, body(): lax.psum(expert_share, 'seq').astype(jnp.float32)  146 us
    unnamed x174, local copies, waits for them, and re-layouts  144 us
    reduce_scatter x1, waiting for transfers between devices, body(): lax.psum_scatter(grad_out_term.astype(jnp.bfloat16), 'dp', scatter_dimens...  99.6 us
    reduce_scatter x1, waiting for transfers between devices, body(): lax.psum_scatter(grad_query_term.astype(jnp.bfloat16), 'dp', scatter_dime...  99.1 us
    reduce_scatter x1, waiting for transfers between devices, body(): lax.psum_scatter(grad_value_term.astype(jnp.bfloat16), 'dp', scatter_dime...  67.3 us
  transfers between devices with their start and end apart: 21, of which 12 were waited for; matrix products, arithmetic and copies ran while one was open for 14% of the time, Pallas kernels for 0%

commit v1 on v0

v1 whole, which is shorter than its diff:
```python
import jax
import jax.numpy as jnp
from jax import lax
from jax.experimental import pallas as pl
from jax.experimental.pallas import tpu as pltpu
from jax.sharding import PartitionSpec as P

QUERY_HEADS = 24
KEY_VALUE_HEADS = 8
HEAD = 64
PAIR_TOK = 1152
MEMBERS = 4
LANE = 128
TILE = 384
KEYROWS = 128
UNIT = PAIR_TOK // KEYROWS // 1
eps_norm = 1e-06
rope_base = 10000.0
NEG = -1e30
BF = jnp.bfloat16
F32 = jnp.float32

Q_LOC = QUERY_HEADS // MEMBERS * HEAD
KV_LOC = KEY_VALUE_HEADS // MEMBERS * HEAD
KVH = KEY_VALUE_HEADS // MEMBERS
GROUP = QUERY_HEADS // KEY_VALUE_HEADS
QKV = Q_LOC + 2 * KV_LOC
OUT_F = LANE
OUT_B = Q_LOC - OUT_F

ANY = pl.BlockSpec(memory_space=pl.ANY)
SMEM = pl.BlockSpec(memory_space=pltpu.SMEM)
VM = pl.BlockSpec(memory_space=pltpu.VMEM)


def params(megabytes):
    return pltpu.CompilerParams(vmem_limit_bytes=megabytes << 20)


def cost(flops, moved, trans=0):
    return pl.CostEstimate(flops=flops, bytes_accessed=moved, transcendentals=trans)


def dot(a, b):
    return lax.dot_general(a, b, (((1,), (0,)), ((), ())), preferred_element_type=F32)


def dot_nt(a, b):
    return lax.dot_general(a, b, (((1,), (1,)), ((), ())), preferred_element_type=F32)


def dot_tn(a, b):
    return lax.dot_general(a, b, (((0,), (0,)), ((), ())), preferred_element_type=F32)


def pick_rows(values, order):
    count, block, width = values.shape

    def kernel(order_ref, in_ref, out_ref):
        out_ref[...] = in_ref[...]

    return pl.pallas_call(
        kernel,
        out_shape=jax.ShapeDtypeStruct(values.shape, values.dtype),
        grid_spec=pltpu.PrefetchScalarGridSpec(
            num_scalar_prefetch=1,
            grid=(count,),
            in_specs=[pl.BlockSpec((1, block, width), lambda i, o: (o[i], 0, 0))],
            out_specs=pl.BlockSpec((1, block, width), lambda i, o: (i, 0, 0)),
        ),
        cost_estimate=cost(0, 4 * values.size),
        name="pick",
    )(order, values)


def pick_marked(values, routes, order):
    count, block, width = values.shape
    topk = routes.shape[2]

    def kernel(order_ref, in_ref, route_ref, out_ref):
        out_ref[0, :, :width] = in_ref[0]
        lanes = lax.broadcasted_iota(jnp.int32, (block, LANE), 1)
        mark = jnp.zeros((block, LANE), F32)
        for k in range(topk):
            mark = mark + jnp.where(route_ref[0, :, k : k + 1] == lanes, 1.0, 0.0)
        out_ref[0, :, width:] = mark.astype(BF)

    return pl.pallas_call(
        kernel,
        out_shape=jax.ShapeDtypeStruct((count, block, width + LANE), values.dtype),
        grid_spec=pltpu.PrefetchScalarGridSpec(
            num_scalar_prefetch=1,
            grid=(count,),
            in_specs=[
                pl.BlockSpec((1, block, width), lambda i, o: (o[i], 0, 0)),
                pl.BlockSpec((1, block, topk), lambda i, o: (o[i], 0, 0)),
            ],
            out_specs=pl.BlockSpec((1, block, width + LANE), lambda i, o: (i, 0, 0)),
        ),
        cost_estimate=cost(0, 4 * values.size),
        name="pick_marked",
    )(order, values, routes)


def dealt_index(t, first):
    return jnp.where(t < first, 2 * t, 2 * (t - first) + 1)


def norm_rows(dealt, gain, first, units):
    _, block, width = dealt.shape

    def kernel(first_ref, in_ref, gain_ref, x_ref, a_ref):
        x = in_ref[0].astype(F32)
        scale = lax.rsqrt(jnp.mean(x * x, axis=-1, keepdims=True) + eps_norm)
        x_ref[0] = in_ref[0]
        a_ref[0] = (x * scale * gain_ref[...].astype(F32)).astype(BF)

    shape = jax.ShapeDtypeStruct((units, block, width), BF)
    spec = pl.BlockSpec((1, block, width), lambda t, f: (t, 0, 0))
    return pl.pallas_call(
        kernel,
        out_shape=(shape, shape),
        grid_spec=pltpu.PrefetchScalarGridSpec(
            num_scalar_prefetch=1,
            grid=(units,),
            in_specs=[
                pl.BlockSpec((1, block, width), lambda t, f: (dealt_index(t, f[0]), 0, 0)),
                pl.BlockSpec((1, width), lambda t, f: (0, 0)),
            ],
            out_specs=(spec, spec),
        ),
        cost_estimate=cost(0, 6 * units * block * width),
        name="norm_rows",
    )(first, dealt, gain)


def take_rows(dealt, first, units):
    _, block, width = dealt.shape

    def kernel(first_ref, in_ref, out_ref):
        out_ref[...] = in_ref[...]

    return pl.pallas_call(
        kernel,
        out_shape=jax.ShapeDtypeStruct((units, block, width), BF),
        grid_spec=pltpu.PrefetchScalarGridSpec(
            num_scalar_prefetch=1,
            grid=(units,),
            in_specs=[pl.BlockSpec((1, block, width), lambda t, f: (dealt_index(t, f[0]), 0, 0))],
            out_specs=pl.BlockSpec((1, block, width), lambda t, f: (t, 0, 0)),
        ),
        cost_estimate=cost(0, 4 * units * block * width),
        name="take_rows",
    )(first, dealt)


def spread_rows(rows, first, slots):
    units, block, width = rows.shape

    def source(i, f):
        u = jnp.where(i % 2 == 0, i // 2, f[0] + i // 2)
        return jnp.minimum(u, units - 1)

    def kernel(first_ref, in_ref, out_ref):
        i = pl.program_id(0)
        limit = jnp.where(i % 2 == 0, first_ref[0], units - first_ref[0])
        keep = i // 2 < limit
        out_ref[...] = jnp.where(keep, in_ref[...].astype(F32), 0.0).astype(BF)

    return pl.pallas_call(
        kernel,
        out_shape=jax.ShapeDtypeStruct((slots, block, width), BF),
        grid_spec=pltpu.PrefetchScalarGridSpec(
            num_scalar_prefetch=1,
            grid=(slots,),
            in_specs=[pl.BlockSpec((1, block, width), lambda i, f: (source(i, f), 0, 0))],
            out_specs=pl.BlockSpec((1, block, width), lambda i, f: (i, 0, 0)),
        ),
        cost_estimate=cost(0, 4 * slots * block * width),
        name="spread_rows",
    )(first, rows)


def place_rows(values, order):
    count, block, width = values.shape

    def kernel(order_ref, in_ref, out_ref):
        out_ref[...] = in_ref[...].astype(F32)

    return pl.pallas_call(
        kernel,
        out_shape=jax.ShapeDtypeStruct(values.shape, F32),
        grid_spec=pltpu.PrefetchScalarGridSpec(
            num_scalar_prefetch=1,
            grid=(count,),
            in_specs=[pl.BlockSpec((1, block, width), lambda i, o: (i, 0, 0))],
            out_specs=pl.BlockSpec((1, block, width), lambda i, o: (o[i], 0, 0)),
        ),
        cost_estimate=cost(0, 6 * values.size),
        name="place_rows",
    )(order, values)


def cut_experts(weight, base, per):
    rows, count, width = weight.shape
    step = 16
    half = width // 2

    def kernel(base_ref, in_ref, *out_refs):
        for e in range(per):
            for j in range(MEMBERS):

                @pl.when(base_ref[0] == j * per)
                def _():
                    value = in_ref[:, j * per + e, :].astype(BF)
                    out_refs[2 * e][...] = value[:, :half]
                    out_refs[2 * e + 1][...] = value[:, half:]

    return pl.pallas_call(
        kernel,
        out_shape=tuple(jax.ShapeDtypeStruct((rows, half), BF) for _ in range(2 * per)),
        grid_spec=pltpu.PrefetchScalarGridSpec(
            num_scalar_prefetch=1,
            grid=(rows // step,),
            in_specs=[pl.BlockSpec((step, count, width), lambda i, b: (i, 0, 0))],
            out_specs=tuple(pl.BlockSpec((step, half), lambda i, b: (i, 0)) for _ in range(2 * per)),
        ),
        cost_estimate=cost(0, 6 * weight.size),
        name="cut_experts",
    )(base, weight)


def start_rows(refs, scratch, table, at, sems):
    copies = []
    for k in range(MEMBERS):
        place = pl.multiple_of(table[at + k] * 32, 32)
        copies.append(
            pltpu.make_async_copy(refs[k], scratch.at[:, pl.ds(place, 32), :], sems.at[k])
        )
        copies[-1].start()
    return copies


def start_weights(refs_f, refs_b, wf, wb, scratch, table, sems):
    copies = []
    n = len(refs_f)
    for s in range(n):
        rows = refs_f[s].shape[0]
        row_f = pl.multiple_of(table[s], 16)
        row_b = pl.multiple_of(table[n + s], 16)
        copies.append(
            pltpu.make_async_copy(
                refs_f[s].at[:, pl.ds(0, wf)],
                scratch.at[pl.ds(row_f, rows), pl.ds(0, wf)],
                sems.at[s],
            )
        )
        copies.append(
            pltpu.make_async_copy(
                refs_b[s].at[:, pl.ds(0, wb)],
                scratch.at[pl.ds(row_b, rows), pl.ds(wf, wb)],
                sems.at[n + s],
            )
        )
    for c in copies:
        c.start()
    return copies


def start_out(refs, scratch, table, at, sems):
    copies = []
    for k in range(MEMBERS):
        copies.append(pltpu.make_async_copy(refs[k], scratch.at[table[at + k]], sems.at[k]))
        copies[-1].start()
    return copies


def wait_all(copies):
    for c in copies:
        c.wait()


def turn(values, cosine, sine):
    width = values.shape[1]
    lanes = lax.broadcasted_iota(jnp.int32, values.shape, 1)
    low = pltpu.roll(values, width - HEAD // 2, 1)
    high = pltpu.roll(values, HEAD // 2, 1)
    swapped = jnp.where(lanes % HEAD < HEAD // 2, low, high)
    reps = width // LANE
    return values * jnp.concatenate([cosine] * reps, 1) + swapped * jnp.concatenate([sine] * reps, 1)


def bias_for(t, extent, first_len):
    gi = lax.broadcasted_iota(jnp.int32, (KEYROWS, extent), 0) + t * KEYROWS
    gj = lax.broadcasted_iota(jnp.int32, (KEYROWS, extent), 1)
    allowed = (gj <= gi) & ((gi < first_len) | (gj >= first_len))
    return jnp.concatenate([jnp.where(allowed, 0.0, NEG)] * GROUP, 0)


def attention_forward(table, base, af, ab, rows_a, wout, cosine, sine, width):
    n = len(af)
    tiles = PAIR_TOK // TILE
    per = TILE // KEYROWS

    def kernel(*refs):
        tab = refs[0]
        f_refs = refs[1 : 1 + n]
        b_refs = refs[1 + n : 1 + 2 * n]
        a_refs = refs[1 + 2 * n : 5 + 2 * n]
        o_refs = refs[5 + 2 * n : 9 + 2 * n]
        cos_ref, sin_ref = refs[9 + 2 * n : 11 + 2 * n]
        part, q_out, k_out, v_out, heads = refs[11 + 2 * n : 16 + 2 * n]
        a_v, w_v, o_v, sem_a, sem_w, sem_o = refs[16 + 2 * n :]
        ca = start_rows(a_refs, a_v, tab, base, sem_a)
        cw = start_weights(f_refs, b_refs, Q_LOC, 2 * KV_LOC, w_v, tab, sem_w)
        co = start_out(o_refs, o_v, tab, base + 4, sem_o)
        wait_all(cw)
        wait_all(ca)
        first_len = tab[base + 8]

        def project(i, carry):
            block = a_v[pl.ds(i * per, per)].reshape(TILE, width)
            y = dot(block, w_v[...])
            rows = pl.ds(pl.multiple_of(i * TILE, TILE), TILE)
            turned = turn(y[:, : Q_LOC + KV_LOC], cos_ref[rows, :], sin_ref[rows, :])
            q = (turned[:, :Q_LOC] * 0.125).astype(BF)
            k = turned[:, Q_LOC:].astype(BF)
            v = y[:, Q_LOC + KV_LOC :].astype(BF)
            for j in range(KVH):
                k_out[j, rows, :] = k[:, j * HEAD : (j + 1) * HEAD]
                v_out[j, rows, :] = v[:, j * HEAD : (j + 1) * HEAD]
                for h in range(GROUP):
                    c = (j * GROUP + h) * HEAD
                    for r in range(per):
                        q_out[j, i * per + r, h * KEYROWS : (h + 1) * KEYROWS, :] = q[
                            r * KEYROWS : (r + 1) * KEYROWS, c : c + HEAD
                        ]
            return carry

        lax.fori_loop(0, tiles, project, 0)
        for c in range(tiles):
            extent = (c + 1) * TILE

            def attend(i, carry, c=c, extent=extent):
                t = c * per + i
                bias = bias_for(t, extent, first_len)
                mixed = []
                for j in range(KVH):
                    s = dot_nt(q_out[j, t], k_out[j, :extent, :]) + bias
                    top = jnp.max(s, axis=1, keepdims=True)
                    p = jnp.exp(s - top)
                    total = jnp.sum(p, axis=1, keepdims=True)
                    o = dot(p.astype(BF), v_out[j, :extent, :]) / total
                    mixed += [o[h * KEYROWS : (h + 1) * KEYROWS] for h in range(GROUP)]
                rows = pl.ds(pl.multiple_of(t * KEYROWS, KEYROWS), KEYROWS)
                heads[rows, :] = jnp.concatenate(mixed, 1).astype(BF)
                return carry

            lax.fori_loop(0, per, attend, 0)
        wait_all(co)

        def project_out(i, carry):
            rows = pl.ds(pl.multiple_of(i * TILE, TILE), TILE)
            h = heads[rows, :]
            for j in range(MEMBERS):
                y = dot(h, o_v[j]).astype(BF)
                part[pl.ds(i * per, per), :, j * Q_LOC : (j + 1) * Q_LOC] = y.reshape(
                    per, KEYROWS, Q_LOC
                )
            return carry

        lax.fori_loop(0, tiles, project_out, 0)

    nt = PAIR_TOK // KEYROWS
    return pl.pallas_call(
        kernel,
        out_shape=(
            jax.ShapeDtypeStruct((nt, KEYROWS, width), BF),
            jax.ShapeDtypeStruct((KVH, nt, GROUP * KEYROWS, HEAD), BF),
            jax.ShapeDtypeStruct((KVH, PAIR_TOK, HEAD), BF),
            jax.ShapeDtypeStruct((KVH, PAIR_TOK, HEAD), BF),
            jax.ShapeDtypeStruct((PAIR_TOK, Q_LOC), BF),
        ),
        in_specs=[SMEM] + [ANY] * (2 * n + 8) + [VM, VM],
        out_specs=(VM,) * 5,
        scratch_shapes=[
            pltpu.VMEM((nt, KEYROWS, width), BF),
            pltpu.VMEM((width, QKV), BF),
            pltpu.VMEM((MEMBERS, Q_LOC, Q_LOC), BF),
            pltpu.SemaphoreType.DMA((4,)),
            pltpu.SemaphoreType.DMA((2 * n,)),
            pltpu.SemaphoreType.DMA((4,)),
        ],
        compiler_params=params(48),
        cost_estimate=cost(15 * 10**9, 14 << 20, 5 * 10**6),
        name="attention_forward",
    )(table, *af, *ab, *rows_a, *wout, cosine, sine)


def attention_backward(table, base, af, ab, rows_m, wout, q, k, v, cosine, sine, width):
    n = len(af)
    tiles = PAIR_TOK // TILE
    per = TILE // KEYROWS
    nt = PAIR_TOK // KEYROWS
    wide = rows_m[0].shape[2]

    def kernel(*refs):
        tab = refs[0]
        f_refs = refs[1 : 1 + n]
        b_refs = refs[1 + n : 1 + 2 * n]
        m_refs = refs[1 + 2 * n : 5 + 2 * n]
        o_refs = refs[5 + 2 * n : 9 + 2 * n]
        q_ref, k_ref, v_ref, cos_ref, sin_ref = refs[9 + 2 * n : 14 + 2 * n]
        da, dqkv = refs[14 + 2 * n : 16 + 2 * n]
        m_v, w_v, o_v, dh_s, dq_s, dk_s, dv_s, sem_m, sem_w, sem_o = refs[16 + 2 * n :]
        cm = start_rows(m_refs, m_v, tab, base, sem_m)
        co = start_out(o_refs, o_v, tab, base + 4, sem_o)
        cw = start_weights(f_refs, b_refs, Q_LOC, 2 * KV_LOC, w_v, tab, sem_w)
        dk_s[...] = jnp.zeros_like(dk_s)
        dv_s[...] = jnp.zeros_like(dv_s)
        wait_all(co)
        wait_all(cm)
        first_len = tab[base + 8]

        def heads_back(i, carry):
            total = None
            for j in range(MEMBERS):
                block = m_v[pl.ds(i * per, per), :, j * Q_LOC : (j + 1) * Q_LOC]
                y = dot_nt(block.reshape(TILE, Q_LOC), o_v[j])
                total = y if total is None else total + y
            total = total.astype(BF)
            for j in range(KVH):
                for h in range(GROUP):
                    c = (j * GROUP + h) * HEAD
                    for r in range(per):
                        dh_s[j, i * per + r, h * KEYROWS : (h + 1) * KEYROWS, :] = total[
                            r * KEYROWS : (r + 1) * KEYROWS, c : c + HEAD
                        ]
            return carry

        lax.fori_loop(0, tiles, heads_back, 0)
        for c in range(tiles):
            extent = (c + 1) * TILE

            def attend(i, carry, c=c, extent=extent):
                t = c * per + i
                bias = bias_for(t, extent, first_len)
                for j in range(KVH):
                    qb = q_ref[j, t]
                    db = dh_s[j, t]
                    kb = k_ref[j, :extent, :]
                    s = dot_nt(qb, kb) + bias
                    top = jnp.max(s, axis=1, keepdims=True)
                    p = jnp.exp(s - top)
                    p = p * (1.0 / jnp.sum(p, axis=1, keepdims=True))
                    dp = dot_nt(db, v_ref[j, :extent, :])
                    prod = p * dp
                    delta = jnp.sum(prod, axis=1, keepdims=True)
                    ds = (prod - p * delta).astype(BF)
                    dq_s[j, t] = dot(ds, kb) * 0.125
                    dk_s[j, :extent, :] += dot_tn(ds, qb)
                    dv_s[j, :extent, :] += dot_tn(p.astype(BF), db)
                return carry

            lax.fori_loop(0, per, attend, 0)
        wait_all(cw)

        def inputs_back(i, carry):
            rows = pl.ds(pl.multiple_of(i * TILE, TILE), TILE)
            cols = []
            for j in range(KVH):
                for h in range(GROUP):
                    cols.append(
                        jnp.concatenate(
                            [
                                dq_s[j, i * per + r, h * KEYROWS : (h + 1) * KEYROWS, :]
                                for r in range(per)
                            ],
                            0,
                        )
                    )
            cols += [dk_s[j, rows, :] for j in range(KVH)]
            joined = jnp.concatenate(cols, 1).astype(BF).astype(F32)
            turned = turn(joined, cos_ref[rows, :], -sin_ref[rows, :])
            value = jnp.concatenate([dv_s[j, rows, :] for j in range(KVH)], 1)
            out = jnp.concatenate([turned, value], 1).astype(BF)
            dqkv[rows, :] = out
            y = dot_nt(out, w_v[...]).astype(BF)
            da[pl.ds(i * per, per)] = y.reshape(per, KEYROWS, width)
            return carry

        lax.fori_loop(0, tiles, inputs_back, 0)

    return pl.pallas_call(
        kernel,
        out_shape=(
            jax.ShapeDtypeStruct((nt, KEYROWS, width), BF),
            jax.ShapeDtypeStruct((PAIR_TOK, QKV), BF),
        ),
        in_specs=[SMEM] + [ANY] * (2 * n + 8) + [VM] * 5,
        out_specs=(VM,) * 2,
        scratch_shapes=[
            pltpu.VMEM((nt, KEYROWS, wide), BF),
            pltpu.VMEM((width, QKV), BF),
            pltpu.VMEM((MEMBERS, Q_LOC, Q_LOC), BF),
            pltpu.VMEM((KVH, nt, GROUP * KEYROWS, HEAD), BF),
            pltpu.VMEM((KVH, nt, GROUP * KEYROWS, HEAD), F32),
            pltpu.VMEM((KVH, PAIR_TOK, HEAD), F32),
            pltpu.VMEM((KVH, PAIR_TOK, HEAD), F32),
            pltpu.SemaphoreType.DMA((4,)),
            pltpu.SemaphoreType.DMA((2 * n,)),
            pltpu.SemaphoreType.DMA((4,)),
        ],
        compiler_params=params(56),
        cost_estimate=cost(20 * 10**9, 16 << 20, 5 * 10**6),
        name="attention_backward",
    )(table, *af, *ab, *rows_m, *wout, q, k, v, cosine, sine)


def attention_grads(table, base, rows_a, rows_b, rows_m, heads, dqkv, width):
    nt = PAIR_TOK // KEYROWS
    step = 256
    wide = rows_m[0].shape[2]

    def kernel(*refs):
        tab = refs[0]
        a_refs, b_refs, m_refs = refs[1:5], refs[5:9], refs[9:13]
        heads_ref, d_ref = refs[13:15]
        gq, go, gr = refs[15:18]
        a_v, b_v, m_v, sem_a, sem_b, sem_m = refs[18:]
        j = pl.program_id(0)

        @pl.when(j == 0)
        def _():
            ca = start_rows(a_refs, a_v, tab, base, sem_a)
            cb = start_rows(b_refs, b_v, tab, base, sem_b)
            cm = start_rows(m_refs, m_v, tab, base, sem_m)
            wait_all(ca)
            wait_all(cb)
            wait_all(cm)

        cols = pl.ds(pl.multiple_of(j * step, step), step)
        a = a_v[:, :, cols].reshape(PAIR_TOK, step)
        gq[...] = dot_tn(a, d_ref[...]).astype(BF)
        b = b_v[:, :, cols].reshape(PAIR_TOK, step)
        gr[...] = dot_tn(b, m_v[:, :, width:].reshape(PAIR_TOK, LANE)).astype(BF)
        m = m_v[:, :, cols].reshape(PAIR_TOK, step)
        go[...] = dot_tn(heads_ref[...], m).astype(BF)

    return pl.pallas_call(
        kernel,
        grid=(width // step,),
        out_shape=(
            jax.ShapeDtypeStruct((width, QKV), BF),
            jax.ShapeDtypeStruct((Q_LOC, width), BF),
            jax.ShapeDtypeStruct((width, LANE), BF),
        ),
        in_specs=[SMEM]
        + [ANY] * 12
        + [
            pl.BlockSpec((PAIR_TOK, Q_LOC), lambda j: (0, 0)),
            pl.BlockSpec((PAIR_TOK, QKV), lambda j: (0, 0)),
        ],
        out_specs=(
            pl.BlockSpec((step, QKV), lambda j: (j, 0)),
            pl.BlockSpec((Q_LOC, step), lambda j: (0, j)),
            pl.BlockSpec((step, LANE), lambda j: (j, 0)),
        ),
        scratch_shapes=[
            pltpu.VMEM((nt, KEYROWS, width), BF),
            pltpu.VMEM((nt, KEYROWS, width), BF),
            pltpu.VMEM((nt, KEYROWS, wide), BF),
            pltpu.SemaphoreType.DMA((4,)),
            pltpu.SemaphoreType.DMA((4,)),
            pltpu.SemaphoreType.DMA((4,)),
        ],
        compiler_params=params(40),
        cost_estimate=cost(4 * 10**9, 16 << 20),
        name="attention_grads",
    )(table, *rows_a, *rows_b, *rows_m, heads, dqkv)


def expert_kernel(table, base, slot, wf, wb, rows_b, rows_d, router, width, hidden):
    n = len(wf)
    nt = PAIR_TOK // KEYROWS
    tiles = PAIR_TOK // TILE
    per = TILE // KEYROWS
    step = 256
    cuts = width // step
    wide = width + LANE
    half = wf[0].shape[1]

    def kernel(*refs):
        tab = refs[0]
        f_refs = refs[1 : 1 + n]
        w_refs = refs[1 + n : 1 + 2 * n]
        b_refs = refs[1 + 2 * n : 5 + 2 * n]
        d_refs = refs[5 + 2 * n : 9 + 2 * n]
        r_ref = refs[9 + 2 * n]
        db, out, grad = refs[10 + 2 * n : 13 + 2 * n]
        w_v, b_v, d_v, dgu_v, gh_v, sem_w, sem_b, sem_d = refs[13 + 2 * n :]
        i = pl.program_id(0)

        @pl.when(i == 0)
        def _():
            cw = start_weights(f_refs, w_refs, half, half, w_v, tab, sem_w)
            cb = start_rows(b_refs, b_v, tab, base, sem_b)
            cd = start_rows(d_refs, d_v, tab, base, sem_d)
            wait_all(cw)
            wait_all(cb)
            wait_all(cd)

        @pl.when(i < tiles)
        def _():
            at = pl.ds(i * per, per)
            b = b_v[at].reshape(TILE, width)
            dy = d_v[at, :, :width].reshape(TILE, width)
            mark = d_v[at, :, width:].reshape(TILE, LANE).astype(F32)
            expert = tab[base + 9] + slot
            lanes = lax.broadcasted_iota(jnp.int32, (TILE, LANE), 1)
            logits = jnp.where(mark > 0.0, dot_nt(b, r_ref[...]), NEG)
            top = jnp.max(logits, axis=1, keepdims=True)
            weight = jnp.where(mark > 0.0, jnp.exp(logits - top), 0.0)
            gates = weight / jnp.sum(weight, axis=1, keepdims=True)
            gate = jnp.sum(jnp.where(lanes == expert, gates, 0.0), axis=1, keepdims=True)
            gu = dot(b, w_v[:, : 2 * hidden])
            back = dot(dy, w_v[:, 2 * hidden :])
            g = gu[:, :hidden]
            u = gu[:, hidden:]
            sig = 1.0 / (1.0 + jnp.exp(-g))
            act = g * sig
            hb = (act * u).astype(BF)
            hf = hb.astype(F32)
            dgate = jnp.sum(hf * back, axis=1, keepdims=True)
            gh = (hf * gate).astype(BF)
            dh = back * gate
            dg = dh * u * (sig * (1.0 + g * (1.0 - sig)))
            dgu = jnp.concatenate([dg, dh * act], 1).astype(BF)
            rows = pl.ds(pl.multiple_of(i * TILE, TILE), TILE)
            dgu_v[rows, :] = dgu
            gh_v[rows, :] = gh
            db[:, :, :width] = (
                dot_nt(dgu, w_v[:, : 2 * hidden]).astype(BF).reshape(per, KEYROWS, width)
            )
            high = dgate.astype(BF).astype(F32)
            low = dgate - high
            extra = jnp.where(
                lanes == expert, high, jnp.where(lanes == expert + LANE // 2, low, 0.0)
            )
            db[:, :, width:] = extra.astype(BF).reshape(per, KEYROWS, LANE)
            out[...] = dot_nt(gh, w_v[:, 2 * hidden :]).astype(BF).reshape(per, KEYROWS, width)

        @pl.when(i >= tiles)
        def _():
            cols = pl.ds(pl.multiple_of((i - tiles) * step, step), step)
            b = b_v[:, :, cols].reshape(PAIR_TOK, step)
            grad[:, : 2 * hidden] = dot_tn(b, dgu_v[...]).astype(BF)
            dy = d_v[:, :, cols].reshape(PAIR_TOK, step)
            grad[:, 2 * hidden :] = dot_tn(dy, gh_v[...]).astype(BF)

    return pl.pallas_call(
        kernel,
        grid=(tiles + cuts,),
        out_shape=(
            jax.ShapeDtypeStruct((nt, KEYROWS, wide), BF),
            jax.ShapeDtypeStruct((nt, KEYROWS, width), BF),
            jax.ShapeDtypeStruct((width, 3 * hidden), BF),
        ),
        in_specs=[SMEM] + [ANY] * (2 * n + 8) + [pl.BlockSpec((LANE, width), lambda i: (0, 0))],
        out_specs=(
            pl.BlockSpec((per, KEYROWS, wide), lambda i: (jnp.minimum(i, tiles - 1), 0, 0)),
            pl.BlockSpec((per, KEYROWS, width), lambda i: (jnp.minimum(i, tiles - 1), 0, 0)),
            pl.BlockSpec((step, 3 * hidden), lambda i: (jnp.maximum(i - tiles, 0), 0)),
        ),
        scratch_shapes=[
            pltpu.VMEM((width, 3 * hidden), BF),
            pltpu.VMEM((nt, KEYROWS, width), BF),
            pltpu.VMEM((nt, KEYROWS, wide), BF),
            pltpu.VMEM((PAIR_TOK, 2 * hidden), BF),
            pltpu.VMEM((PAIR_TOK, hidden), BF),
            pltpu.SemaphoreType.DMA((2 * n,)),
            pltpu.SemaphoreType.DMA((4,)),
            pltpu.SemaphoreType.DMA((4,)),
        ],
        compiler_params=params(48),
        cost_estimate=cost(17 * 10**9, 26 << 20, 10**6),
        name="expert",
    )(table, *wf, *wb, *rows_b, *rows_d, router)


def turn_out_weight(places, af, ab):
    n = len(af)
    rows = af[0].shape[0]

    def kernel(*refs):
        tab = refs[0]
        f_refs = refs[1 : 1 + n]
        b_refs = refs[1 + n : 1 + 2 * n]
        out, sems = refs[1 + 2 * n :]
        copies = []
        for s in range(n):
            at = pl.ds(pl.multiple_of(tab[n + s], 16), rows)
            copies.append(
                pltpu.make_async_copy(
                    f_refs[s].at[:, pl.ds(Q_LOC, OUT_F)],
                    out.at[tab[s], at, pl.ds(0, OUT_F)],
                    sems.at[s],
                )
            )
            at = pl.ds(pl.multiple_of(tab[3 * n + s], 16), rows)
            copies.append(
                pltpu.make_async_copy(
                    b_refs[s].at[:, pl.ds(2 * KV_LOC, OUT_B)],
                    out.at[tab[2 * n + s], at, pl.ds(OUT_F, OUT_B)],
                    sems.at[n + s],
                )
            )
        for c in copies:
            c.start()
        wait_all(copies)

    return pl.pallas_call(
        kernel,
        out_shape=jax.ShapeDtypeStruct((MEMBERS, Q_LOC, Q_LOC), BF),
        in_specs=[SMEM] + [ANY] * (2 * n),
        out_specs=ANY,
        scratch_shapes=[pltpu.SemaphoreType.DMA((2 * n,))],
        cost_estimate=cost(0, 3 << 20),
        name="turn_out_weight",
    )(places, *af, *ab)


def join_experts(places, shares, per):
    rows, half = shares[0][0].shape
    width = 2 * half
    count = MEMBERS * per
    step = 16

    def kernel(*refs):
        tab = refs[0]
        ins = refs[1 : 1 + 2 * count]
        out, hold = refs[1 + 2 * count :]
        for k in range(MEMBERS):
            for e in range(per):
                for side in range(2):
                    value = ins[(k * per + e) * 2 + side][...].astype(F32)
                    hold[tab[k] * per + e, :, side * half : (side + 1) * half] = value
        for c in range(count):
            out[:, c, :] = hold[c]

    flat = [part for share in shares for part in share]
    return pl.pallas_call(
        kernel,
        out_shape=jax.ShapeDtypeStruct((rows, count, width), F32),
        grid=(rows // step,),
        in_specs=[SMEM] + [pl.BlockSpec((step, half), lambda i: (i, 0))] * (2 * count),
        out_specs=pl.BlockSpec((step, count, width), lambda i: (i, 0, 0)),
        scratch_shapes=[pltpu.VMEM((count, step, width), F32)],
        compiler_params=params(32),
        cost_estimate=cost(0, 6 * rows * count * width),
        name="join_experts",
    )(places, *flat)


def ring_place(index, n):
    return jnp.where(index % 2 == 0, index // 2, n - 1 - index // 2)


def ring_index(place, n):
    return jnp.where(place < n // 2, 2 * place, 2 * (n - 1 - place) + 1)


def ring_pairs(n):
    ring = list(range(0, n, 2)) + list(range(n - 1, 0, -2))
    ahead = [(ring[i], ring[(i + 1) % n]) for i in range(n)]
    back = [(b, a) for a, b in ahead]
    return ahead, back


def swap(values, bits):
    return lax.ppermute(values, "seq", [(i, i ^ bits) for i in range(MEMBERS)])


def share_rows(values):
    across = swap(values, 2)
    return [values, swap(values, 1), across, swap(across, 1)]


def body(
    tokens,
    cotangent,
    routes,
    lengths,
    deal_order,
    attn_gain,
    query_weight,
    key_matrix,
    value_matrix,
    out_weight,
    moe_gain,
    router_weight,
    expert_weight,
):
    n = lax.axis_size("dp")
    group = lax.axis_index("dp")
    member = lax.axis_index("seq")
    slots, block, width = tokens.shape
    units = PAIR_TOK // (MEMBERS * block)
    local_rows = query_weight.shape[0]
    n_expert = router_weight.shape[1]
    hidden = expert_weight.shape[2] // 3
    per = n_expert // MEMBERS
    ahead, back = ring_pairs(n)
    natural = block == 32

    place = ring_place(group, n)
    steps = jnp.arange(n, dtype=jnp.int32)
    from_f = ring_index((place - steps) % n, n).astype(jnp.int32)
    from_b = ring_index((place + steps) % n, n).astype(jnp.int32)
    xors = jnp.bitwise_xor(jnp.arange(MEMBERS, dtype=jnp.int32), member)
    row_place = xors if natural else jnp.arange(MEMBERS, dtype=jnp.int32)
    first_seq = deal_order[2 * group]
    first_len = lengths[first_seq]
    first = (first_len // (MEMBERS * block)).reshape(1)
    base = 2 * n
    table = jnp.concatenate(
        [
            from_f * local_rows,
            from_b * local_rows,
            row_place,
            xors,
            jnp.stack([first_len, per * member]),
        ]
    ).astype(jnp.int32)
    share = n // MEMBERS
    out_places = jnp.concatenate(
        [
            jnp.bitwise_xor(from_f // share, member),
            from_f % share * local_rows,
            jnp.bitwise_xor(from_b // share, member),
            from_b % share * local_rows,
        ]
    ).astype(jnp.int32)

    small = jnp.concatenate(
        [attn_gain[None], moe_gain[None], router_weight.T, jnp.zeros((2, local_rows), F32)], 0
    ).astype(BF)
    rows_small = small.shape[0]
    everywhere = jnp.zeros((n, rows_small, local_rows), BF)
    everywhere = lax.dynamic_update_slice(everywhere, small[None], (group, 0, 0))
    f, b = small, small
    for s in range(1, n // 2 + 1):
        f = lax.ppermute(f, "dp", ahead)
        everywhere = lax.dynamic_update_slice(everywhere, f[None], (from_f[s], 0, 0))
        if s < n // 2:
            b = lax.ppermute(b, "dp", back)
            everywhere = lax.dynamic_update_slice(everywhere, b[None], (from_b[s], 0, 0))
    everywhere = everywhere.transpose(1, 0, 2).reshape(rows_small, width)
    gain_a = everywhere[0:1]
    gain_m = everywhere[1:2].astype(F32)
    router = jnp.concatenate(
        [everywhere[2 : 2 + n_expert], jnp.zeros((LANE - n_expert, width), BF)], 0
    )

    sent_x = pick_rows(tokens, deal_order)
    sent_d = pick_marked(cotangent, routes, deal_order)
    dealt_x = lax.all_to_all(sent_x, "dp", split_axis=0, concat_axis=0, tiled=True)
    dealt_d = lax.all_to_all(sent_d, "dp", split_axis=0, concat_axis=0, tiled=True)
    x_rows, a_rows = norm_rows(dealt_x, gain_a, first, units)
    d_rows = take_rows(dealt_d, first, units)

    def cut(values, size):
        return lax.dynamic_slice_in_dim(values, member * size, size, axis=1).astype(BF)

    out_cols = cut(out_weight, Q_LOC)
    attn_f = jnp.concatenate([cut(query_weight, Q_LOC), out_cols[:, :OUT_F]], 1)
    attn_b = jnp.concatenate(
        [cut(key_matrix, KV_LOC), cut(value_matrix, KV_LOC), out_cols[:, OUT_F:]], 1
    )
    expert_parts = cut_experts(expert_weight, (per * member).reshape(1), per)

    def ring_gather(f, b):
        fs, bs = [f], [b]
        for _ in range(n - 1):
            fs.append(lax.ppermute(fs[-1], "dp", ahead))
            bs.append(lax.ppermute(bs[-1], "dp", back))
        return fs, bs

    def ring_scatter(part_f, part_b):
        f, b = part_f(1), part_b(1)
        for s in range(2, n + 1):
            f = lax.ppermute(f, "dp", ahead)
            b = lax.ppermute(b, "dp", back)
            f = (f.astype(F32) + part_f(s % n).astype(F32)).astype(BF)
            b = (b.astype(F32) + part_b(s % n).astype(F32)).astype(BF)
        return f, b

    def rows_of(chunks):
        if natural:
            return chunks
        w = chunks[0].shape[2]
        whole = jnp.zeros((units, MEMBERS, block, w), BF)
        for k in range(MEMBERS):
            whole = lax.dynamic_update_slice(whole, chunks[k][:, None], (0, xors[k], 0, 0))
        whole = whole.reshape(PAIR_TOK // KEYROWS, MEMBERS, 32, w)
        return [whole[:, j] for j in range(MEMBERS)]

    def gather_rows(values):
        return rows_of(share_rows(values))

    def scatter_rows(parts):
        shaped = [p.reshape(units, MEMBERS, block, p.shape[2]) for p in parts]

        def part(k):
            total = None
            for p in shaped:
                one = lax.dynamic_index_in_dim(p, xors[k], axis=1, keepdims=False).astype(F32)
                total = one if total is None else total + one
            return total

        far = swap(part(3).astype(BF), 1)
        near = swap(part(1).astype(BF), 1)
        cross = swap((part(2) + far.astype(F32)).astype(BF), 2)
        return part(0) + near.astype(F32) + cross.astype(F32)

    attn_fs, attn_bs = ring_gather(attn_f, attn_b)
    expert_fs, expert_bs = [], []
    for e in range(per):
        fs, bs = ring_gather(expert_parts[2 * e], expert_parts[2 * e + 1])
        expert_fs.append(fs)
        expert_bs.append(bs)

    turned = turn_out_weight(out_places, attn_fs, attn_bs)
    wout = [turned[0]] + [swap(turned[k], k) for k in range(1, MEMBERS)]

    row = jnp.arange(PAIR_TOK, dtype=jnp.int32)
    pos = row - jnp.where(row >= first_len, first_len, 0)
    freq = rope_base ** (-(jnp.arange(HEAD // 2, dtype=F32) * 2.0 / HEAD))
    angle = pos.astype(F32)[:, None] * freq[None, :]
    cosine = jnp.concatenate([jnp.cos(angle)] * 4, 1)
    sine = jnp.sin(angle)
    sine = jnp.concatenate([-sine, sine, -sine, sine], 1)

    rows_a = gather_rows(a_rows)
    rows_d = gather_rows(d_rows)
    part, q, k, v, heads = attention_forward(
        table, base, attn_fs, attn_bs, rows_a, wout, cosine, sine, width
    )
    middle = x_rows.astype(F32) + scatter_rows([part])

    inverse = lax.rsqrt(jnp.mean(middle * middle, axis=-1, keepdims=True) + eps_norm)
    b_rows = (middle * inverse * gain_m).astype(BF)
    rows_b = gather_rows(b_rows)

    dbs, outs, grads = [], [], []
    for e in range(per):
        db, out, grad = expert_kernel(
            table, base, e, expert_fs[e], expert_bs[e], rows_b, rows_d, router, width, hidden
        )
        dbs.append(db)
        outs.append(out)
        grads.append(grad)

    own_b = b_rows.reshape(units * block, width)
    mark = d_rows[:, :, width:].reshape(units * block, LANE).astype(F32)
    logits = dot_nt(own_b, router)
    gates = jax.nn.softmax(jnp.where(mark > 0.0, logits, -jnp.inf), axis=-1)

    back_sum = scatter_rows(dbs).reshape(units * block, width + LANE)
    extra = back_sum[:, width:]
    dgate = extra + jnp.roll(extra, -(LANE // 2), axis=1)
    dgate = jnp.where(mark > 0.0, dgate, 0.0)
    dlogits = (gates * (dgate - jnp.sum(gates * dgate, axis=-1, keepdims=True))).astype(BF)
    db_own = back_sum[:, :width] + dot(dlogits, router)
    mid_own = middle.reshape(units * block, width)
    inv_own = inverse.reshape(units * block, 1)
    d_own = d_rows[:, :, :width].reshape(units * block, width).astype(F32)
    normed = mid_own * inv_own
    scaled = db_own * gain_m
    dmiddle = d_own + inv_own * (
        scaled - normed * jnp.mean(scaled * normed, axis=-1, keepdims=True)
    )
    dmix = jnp.concatenate([dmiddle.astype(BF), dlogits], 1).reshape(units, block, width + LANE)
    rows_m = gather_rows(dmix)

    da, dqkv = attention_backward(
        table, base, attn_fs, attn_bs, rows_m, wout, q, k, v, cosine, sine, width
    )
    gqkv, gout, grouter = attention_grads(table, base, rows_a, rows_b, rows_m, heads, dqkv, width)

    da_own = scatter_rows([da]).reshape(units * block, width)
    x_own = x_rows.reshape(units * block, width).astype(F32)
    inv_x = lax.rsqrt(jnp.mean(x_own * x_own, axis=-1, keepdims=True) + eps_norm)
    normed_x = x_own * inv_x
    scaled_x = da_own * gain_a.astype(F32)
    grad_x = dmiddle + inv_x * (
        scaled_x - normed_x * jnp.mean(scaled_x * normed_x, axis=-1, keepdims=True)
    )
    result = middle + scatter_rows(outs)

    gout_cols = jnp.zeros((width, Q_LOC), BF)
    for kk in range(MEMBERS):
        piece = lax.dynamic_slice_in_dim(gout, xors[kk] * Q_LOC, Q_LOC, axis=1)
        if kk:
            piece = swap(piece, kk)
        gout_cols = lax.dynamic_update_slice(gout_cols, piece, (xors[kk] * Q_LOC, 0))
    full_f = jnp.concatenate([gqkv[:, :Q_LOC], gout_cols[:, :OUT_F]], 1)
    full_b = jnp.concatenate([gqkv[:, Q_LOC:], gout_cols[:, OUT_F:], grouter], 1)

    def piece_f(values, lo, size):
        return lambda s: lax.dynamic_slice(values, (table[s], lo), (local_rows, size))

    def piece_b(values, lo, size):
        return lambda s: lax.dynamic_slice(values, (table[n + s], lo), (local_rows, size))

    half = 3 * hidden // 2
    expert_shares = []
    for e in range(per):
        f, b = ring_scatter(piece_f(grads[e], 0, half), piece_b(grads[e], half, half))
        expert_shares.append((share_rows(f), share_rows(b)))
    share_f, share_b = ring_scatter(
        piece_f(full_f, 0, full_f.shape[1]), piece_b(full_b, 0, full_b.shape[1])
    )
    small_grad = share_b[:, full_b.shape[1] - LANE :]
    shares_f = share_rows(share_f)
    shares_b = share_rows(share_b[:, : full_b.shape[1] - LANE])

    def spread(chunks, lo, size):
        whole = jnp.zeros((local_rows, MEMBERS * size), F32)
        for kk in range(MEMBERS):
            whole = lax.dynamic_update_slice(
                whole, chunks[kk][:, lo : lo + size].astype(F32), (0, xors[kk] * size)
            )
        return whole

    grad_query = spread(shares_f, 0, Q_LOC)
    grad_key = spread(shares_b, 0, KV_LOC)
    grad_value = spread(shares_b, KV_LOC, KV_LOC)
    out_joined = [
        jnp.concatenate([cf[:, Q_LOC:], cb[:, 2 * KV_LOC :]], 1)
        for cf, cb in zip(shares_f, shares_b)
    ]
    grad_out = spread(out_joined, 0, Q_LOC)
    grad_router = small_grad[:, :n_expert].astype(F32)
    shares = [
        [expert_shares[e][side][kk] for e in range(per) for side in range(2)]
        for kk in range(MEMBERS)
    ]
    grad_experts = join_experts(xors, shares, per)

    def low(values):
        return values.astype(BF).astype(F32)

    grad_attn_gain = (
        jnp.sum(low(query_weight) * grad_query, axis=1)
        + jnp.sum(low(key_matrix) * grad_key, axis=1)
        + jnp.sum(low(value_matrix) * grad_value, axis=1)
    ) / low(attn_gain)
    grad_moe_gain = (
        jnp.sum(
            low(expert_weight[:, :, : 2 * hidden]) * grad_experts[:, :, : 2 * hidden], axis=(1, 2)
        )
        + jnp.sum(low(router_weight) * grad_router, axis=1)
    ) / low(moe_gain)

    back_out = lax.all_to_all(
        spread_rows(result.astype(BF), first, slots),
        "dp",
        split_axis=0,
        concat_axis=0,
        tiled=True,
    )
    back_grad = lax.all_to_all(
        spread_rows(grad_x.reshape(units, block, width).astype(BF), first, slots),
        "dp",
        split_axis=0,
        concat_axis=0,
        tiled=True,
    )
    output = place_rows(back_out, deal_order)
    grad_tokens = place_rows(back_grad, deal_order)
    return (
        output,
        grad_tokens,
        grad_attn_gain,
        grad_query,
        grad_key,
        grad_value,
        grad_out,
        grad_moe_gain,
        grad_router,
        grad_experts,
    )


def solution(mesh):
    rows = P(None, ("dp", "seq"), None)
    placed = (
        rows,
        rows,
        rows,
        P(),
        P(),
        P("dp"),
        P("dp", None),
        P("dp", None),
        P("dp", None),
        P("dp", None),
        P("dp"),
        P("dp", None),
        P("dp", None, None),
    )
    return jax.shard_map(
        body,
        mesh=mesh,
        in_specs=placed,
        out_specs=(
            rows,
            rows,
            P("dp"),
            P("dp", None),
            P("dp", None),
            P("dp", None),
            P("dp", None),
            P("dp"),
            P("dp", None),
            P("dp", None, None),
        ),
        check_vma=False,
    )
```

time: 3200 us -> 1000 us (0.31)
  waiting for transfers between devices: 2230 us -> 218 us
  Pallas kernels: 0 us -> 294 us
  matrix products: 213 us -> 0.82 us
  local copies, waits for them, and re-layouts: 296 us -> 91.3 us
  starting transfers between devices: 52.9 us -> 232 us
  blocking collectives: 129 us -> 0 us
  other arithmetic: 214 us -> 85.1 us
  between operations: 17.2 us -> 63.7 us
  loops' own time: 32.1 us -> 0 us
    all_gather x5 -> x0, waiting for transfers between devices: 1050 us -> none  [the longest x1 1020 us: body(): lax.all_gather(expert_local, 'dp', axis=2, tiled=True)]
    unnamed x14 -> x0, waiting for transfers between devices: 690 us -> none
    reduce_scatter x4 -> x0, waiting for transfers between devices: 321 us -> none  [the longest x1 99.6 us: body(): lax.psum_scatter(grad_out_term.astype(jnp.bfloat16), 'dp', scatter_dimens...]
    pallas_call x0 -> x17, Pallas kernels: none -> 294 us  [the longest x3 83.1 us: expert_kernel(): pl.pallas_call(kernel, grid=(tiles + cuts,), out_shape=(jax.ShapeDtypeStr...]
    ppermute x0 -> x173, starting transfers between devices: none -> 212 us  [the longest x54 76.2 us: swap(): return lax.ppermute(values, 'seq', [(i, i ^ bits) for i in range(MEMBERS)])]
    dot_general x49 -> x2, matrix products: 213 us -> 0.82 us  [the longest x1 0.46 us: dot_nt(): lax.dot_general(a, b, (((1,), (1,)), ((), ())), preferred_element_type=F32)]
    ppermute x0 -> x173, waiting for transfers between devices: none -> 208 us  [the longest x28 59.4 us: ring_scatter(): b = lax.ppermute(b, 'dp', back)]
    psum x1 -> x0, waiting for transfers between devices: 146 us -> none  [body(): lax.psum(expert_share, 'seq').astype(jnp.float32)]
  transfers between devices with their start and end apart: 21 -> 177, of which waited for: 12 -> 51; matrix products, arithmetic and copies ran while one was open for 14% -> 16% of each run, Pallas kernels for 0% -> 25%
where the time goes in v1:
time: 1000 us; the launch traced here: 985 us
  Pallas kernels  294 us (29%)
  starting transfers between devices  232 us (23%)
  waiting for transfers between devices  218 us (22%)
  local copies, waits for them, and re-layouts  91.3 us (9%)
  other arithmetic  85.1 us (9%)
  between operations  63.7 us (6%)
    pallas_call x3, Pallas kernels, expert_kernel(): pl.pallas_call(kernel, grid=(tiles + cuts,), out_shape=(jax.ShapeDtypeStr...  83.1 us
    ppermute x54, starting transfers between devices, swap(): return lax.ppermute(values, 'seq', [(i, i ^ bits) for i in range(MEMBERS)])  76.2 us
    ppermute x28, waiting for transfers between devices, ring_scatter(): b = lax.ppermute(b, 'dp', back)  59.4 us
    unnamed x363, local copies, waits for them, and re-layouts  54.7 us
    ppermute x28, waiting for transfers between devices, ring_gather(): fs.append(lax.ppermute(fs[-1], 'dp', ahead))  54.3 us
    ppermute x28, starting transfers between devices, ring_gather(): fs.append(lax.ppermute(fs[-1], 'dp', ahead))  45 us
    pallas_call x1, Pallas kernels, attention_backward(): pl.pallas_call(kernel, out_shape=(jax.ShapeDtypeStruct((nt, KEYROWS, widt...  38.9 us
    ppermute x54, waiting for transfers between devices, swap(): return lax.ppermute(values, 'seq', [(i, i ^ bits) for i in range(MEMBERS)])  38.6 us
  transfers between devices with their start and end apart: 177, of which 51 were waited for; matrix products, arithmetic and copies ran while one was open for 16% of the time, Pallas kernels for 25%

profile of v1, /device:TPU:1, one launch (start us, length us, event | category | flops | bytes accessed | tf_op | source)
XLA Modules:
  0.0 984.6 jit_solution(6169381121299069582)
XLA Ops:
  0.7 10.1 %pick.1 = bf16[16,32,1536]{2,1,0:T(8,128)(2,1)} custom-call(s32[16]{0:T(128)} %order_ref.7, bf16[16,32,1536]{2,1,0:T(8,128)(2,1)} %in_ref.3), custom_call_target="tpu_custom_call" | custom-call | bytes 3145728 | tf_op jit(solution)/shard_map/pick/pallas_call | solution.py:62
  10.8 6.5 all-to-all-start
  23.2 19.9 %collective-permute-done = bf16[16,192]{1,0:T(8,128)(2,1)S(1)} collective-permute-done((bf16[16,192]{1,0:T(8,128)(2,1)S(1)}, bf16[16,192]{1,0:T(8,128)(2,1)S(1)}, u32[]{:S(2)}, u32[]{:S(2)}) %collective-permute-start) | collective-permute-done | bytes 6176 | tf_op jit(solution)/shard_map/ppermute | solution.py:853
  43.1 10.8 %collective-permute-start.2 = (bf16[16,192]{1,0:T(8,128)(2,1)S(1)}, bf16[16,192]{1,0:T(8,128)(2,1)S(1)}, u32[]{:S(2)}, u32[]{:S(2)}) collective-permute-start(bf16[16,192]{1,0:T(8,128)(2,1)S(1)} %collective-permute-done), channel_id=1, source_target_pairs={{0,8},{8,16},{16,24},{24,28},{28,20},{20,12},{12,4},{4,0},{1,9},{9... | collective-permute-start | bytes 18440 | tf_op jit(solution)/shard_map/ppermute | solution.py:853
  83.2 10.6 %pick_marked.1 = bf16[16,32,1664]{2,1,0:T(8,128)(2,1)} custom-call(s32[16]{0:T(128)} %order_ref.7, bf16[16,32,1536]{2,1,0:T(8,128)(2,1)} %in_ref.4, s32[16,32,8]{2,1,0:T(8,128)} %copy.185.route_ref), custom_call_target="tpu_custom_call" | custom-call | bytes 3145728 | tf_op jit(solution)/shard_map/pick_marked/pallas_call | solution.py:88
  105.5 6.1 norm_rows.1
  118.4 16.7 %collective-permute-done.11.refs_6_ = bf16[192,512]{1,0:T(8,128)(2,1)S(1)} collective-permute-done((bf16[192,512]{1,0:T(8,128)(2,1)S(1)}, bf16[192,512]{1,0:T(8,128)(2,1)S(1)}, u32[]{:S(2)}, u32[]{:S(2)}) %collective-permute-start.11) | collective-permute-done | bytes 196640 | tf_op jit(solution)/shard_map/ppermute | solution.py:885
  135.2 11.0 %collective-permute-start.12 = (bf16[192,512]{1,0:T(8,128)(2,1)S(1)}, bf16[192,512]{1,0:T(8,128)(2,1)S(1)}, u32[]{:S(2)}, u32[]{:S(2)}) collective-permute-start(bf16[192,512]{1,0:T(8,128)(2,1)S(1)} %collective-permute-done.11.refs_6_), channel_id=1, source_target_pairs={{0,8},{8,16},{16,24},{24,28},{28,20},{20,12},{12,4},{4,0},{1,9},{9... | collective-permute-start | bytes 589832 | tf_op jit(solution)/shard_map/ppermute | solution.py:885
  157.6 37.7 %turn_out_weight.1 = bf16[4,384,384]{2,1,0:T(8,128)(2,1)} custom-call(s32[32]{0:T(128)} %pad_add_fusion.refs_0_, bf16[192,512]{1,0:T(8,128)(2,1)} %copy-done.4, bf16[192,512]{1,0:T(8,128)(2,1)} %copy-done.20, bf16[192,512]{1,0:T(8,128)(2,1)} %copy-done.24, bf16[192,512]{1,0:T(8,128)(2,1)} %copy-done.28, bf16[192,512]{1,0:T(8,128)(2,1)} %copy-done.32, ...), custom_call_target="tpu_custom_call" | custom-call | bytes 3145728 | tf_op jit(solution)/shard_map/turn_out_weight/pallas_call | solution.py:722
  197.4 4.8 collective-permute-start.24
  206.3 19.7 %copy.184.in_ref = f32[192,12,1536]{2,1,0:T(8,128)} copy(f32[192,12,1536]{2,0,1:T(8,128)} %param.25) | data formatting | bytes 28311552 | tf_op args[12]
  226.0 13.3 %cut_experts.1 = (bf16[192,768]{1,0:T(8,128)(2,1)}, bf16[192,768]{1,0:T(8,128)(2,1)}, bf16[192,768]{1,0:T(8,128)(2,1)}, bf16[192,768]{1,0:T(8,128)(2,1)}, bf16[1...) custom-call(s32[1]{0:T(128)} %bitcast.20.base_ref, f32[192,12,1536]{2,1,0:T(8,128)} %copy.184.in_ref), custom_call_target="tpu_custom_call" | custom-call | bytes 21233664 | tf_op jit(solution)/shard_map/cut_experts/pallas_call | solution.py:219
  249.3 25.7 %attention_forward.1 = (bf16[9,128,1536]{2,1,0:T(8,128)(2,1)}, bf16[2,9,384,64]{3,2,1,0:T(8,128)(2,1)}, bf16[2,1152,64]{2,1,0:T(8,128)(2,1)S(1)}, bf16[2,1152,64]{2,1,0:T(8,128)(2,1)S(1)}, bf16[1152,384]{1,0:T(8,128)(2,1)}) custom-call(s32[26]{0:T(128)S(1)} %concatenate.71.refs_0_, bf16[192,512]{1,0:T(8,128)(2,1)S(1)} %copy-done.5, ...), custom_call_target="tpu_custom_call" | custom-call | flops 15000000512 | bytes 14680064 | tf_op jit(solution)/shard_map/attention_forward/pallas_call | solution.py:375
  282.2 5.3 collective-permute-done.50.refs_2_
  337.5 5.7 take_rows.1.refs_21_
  357.3 5.0 collective-permute-done.75.refs_14_
  370.1 4.8 collective-permute-done.41.refs_14_
  404.1 6.6 slice.476
  421.5 9.2 collective-permute-start.47
  445.5 4.9 collective-permute-done.77.refs_16_
  454.8 27.8 %expert.5 = (bf16[9,128,1664]{2,1,0:T(8,128)(2,1)}, bf16[9,128,1536]{2,1,0:T(8,128)(2,1)}, bf16[1536,1536]{1,0:T(8,128)(2,1)}) custom-call(s32[26]{0:T(128)S(1)} %concatenate.71.refs_0_, bf16[192,768]{1,0:T(8,128)(2,1)S(1)} %copy-done.71, bf16[192,768]{1,0:T(8,128)(2,1)} %collective-permute-done.64.refs_2_, bf16[192,768]{1,0:T(8,128)(2,1)S(1)} %copy-done.90, ...), custom_call_target="tpu_custom_call" | custom-call | flops 16999999488 | bytes 27262976 | tf_op jit(solution)/shard_map/expert/pallas_call | solution.py:661
  482.9 27.7 %expert.4 = (bf16[9,128,1664]{2,1,0:T(8,128)(2,1)}, bf16[9,128,1536]{2,1,0:T(8,128)(2,1)}, bf16[1536,1536]{1,0:T(8,128)(2,1)}) custom-call(s32[26]{0:T(128)S(1)} %concatenate.71.refs_0_, bf16[192,768]{1,0:T(8,128)(2,1)S(1)} %copy-done.68, bf16[192,768]{1,0:T(8,128)(2,1)S(1)} %copy-done.78, bf16[192,768]{1,0:T(8,128)(2,1)S(1)} %copy-done.86, ...), custom_call_target="tpu_custom_call" | custom-call | flops 16999999488 | bytes 27262976 | tf_op jit(solution)/shard_map/expert/pallas_call | solution.py:661
  510.7 27.6 %expert.3 = (bf16[9,128,1664]{2,1,0:T(8,128)(2,1)}, bf16[9,128,1536]{2,1,0:T(8,128)(2,1)}, bf16[1536,1536]{1,0:T(8,128)(2,1)}) custom-call(s32[26]{0:T(128)S(1)} %concatenate.71.refs_0_, bf16[192,768]{1,0:T(8,128)(2,1)S(1)} %copy-done.64, bf16[192,768]{1,0:T(8,128)(2,1)S(1)} %copy-done.74, bf16[192,768]{1,0:T(8,128)(2,1)S(1)} %copy-done.82, ...), custom_call_target="tpu_custom_call" | custom-call | flops 16999999488 | bytes 27262976 | tf_op jit(solution)/shard_map/expert/pallas_call | solution.py:661
  561.7 4.6 collective-permute-done.148
  568.1 4.6 collective-permute-done.121
  574.4 4.6 collective-permute-done.135
  580.7 4.6 collective-permute-done.149
  587.0 4.6 collective-permute-done.122
  593.3 4.6 collective-permute-done.136
  599.7 4.6 collective-permute-done.150
  632.4 6.0 collective-permute-done.83
  657.0 6.3 collective-permute-start.84
  672.4 5.4 collective-permute-done.126
  681.9 38.9 %attention_backward.1 = (bf16[9,128,1536]{2,1,0:T(8,128)(2,1)}, bf16[1152,640]{1,0:T(8,128)(2,1)}) custom-call(s32[26]{0:T(128)} %copy-done.48, bf16[192,512]{1,0:T(8,128)(2,1)} %copy-done.4, bf16[192,512]{1,0:T(8,128)(2,1)} %copy-done.20, bf16[192,512]{1,0:T(8,128)(2,1)} %copy-done.24, bf16[192,512]{1,0:T(8,128)(2,1)} %copy-done.28, ...), custom_call_target="tpu_custom_call" | custom-call | flops 20000000000 | bytes 16777216 | tf_op jit(solution)/shard_map/attention_backward/pallas_call | solution.py:494
  727.6 11.1 %attention_grads.1 = (bf16[1536,640]{1,0:T(8,128)(2,1)}, bf16[384,1536]{1,0:T(8,128)(2,1)S(1)}, bf16[1536,128]{1,0:T(8,128)(2,1)S(1)}) custom-call(s32[26]{0:T(128)S(1)} %copy-done.49, bf16[9,32,1536]{2,1,0:T(8,128)(2,1)} %get-tuple-element.38.refs_17_.refs_1_, bf16[9,32,1536]{2,1,0:T(8,128)(2,1)} %collective-permute-done.21.refs_18_.refs_2_, ...), custom_call_target="tpu_custom_call" | custom-call | flops 4000000000 | bytes 16777216 | tf_op jit(solution)/shard_map/attention_grads/pallas_call | solution.py:550
  750.9 5.2 collective-permute-done.92
  765.8 5.5 collective-permute-done.162.refs_14_
  778.7 5.3 collective-permute-done.164.refs_16_
  788.8 9.1 spread_rows.2
  817.8 12.6 %join_experts.1 = f32[192,12,1536]{2,1,0:T(8,128)} custom-call(s32[4]{0:T(128)S(1)} %iota_xor_fusion.refs_0_, bf16[192,768]{1,0:T(8,128)(2,1)S(1)} %get-tuple-element.155.refs_1_, bf16[192,768]{1,0:T(8,128)(2,1)S(1)} %get-tuple-element.154.refs_2_, bf16[192,768]{1,0:T(8,128)(2,1)S(1)} %get-tuple-element.139.refs_3_, ...), custom_call_target="tpu_custom_call" | custom-call | bytes 21233664 | tf_op jit(solution)/shard_map/join_experts/pallas_call | solution.py:752
  831.6 11.1 %collective-permute-start.95 = (bf16[192,512]{1,0:T(8,128)(2,1)S(1)}, bf16[192,512]{1,0:T(8,128)(2,1)S(1)}, u32[]{:S(2)}, u32[]{:S(2)}) collective-permute-start(bf16[192,512]{1,0:T(8,128)(2,1)S(1)} %add_convert_fusion.58), channel_id=1, source_target_pairs={{0,8},{8,16},{16,24},{24,28},{28,20},{20,12},{12,4},{4,0},{1,9},{9... | collective-permute-start | bytes 589832 | tf_op jit(solution)/shard_map/ppermute | solution.py:892
  851.9 9.4 fusion
  861.2 13.5 %copy.211 = f32[192,12,1536]{2,0,1:T(8,128)} copy(f32[192,12,1536]{2,1,0:T(8,128)S(1)} %copy-done.114) | data formatting | bytes 28311552
  877.0 10.2 %place_rows.2 = f32[16,32,1536]{2,1,0:T(8,128)} custom-call(s32[16]{0:T(128)} %order_ref.7, bf16[16,32,1536]{2,1,0:T(8,128)(2,1)} %all-to-all-done.2.in_ref), custom_call_target="tpu_custom_call" | custom-call | bytes 4718592 | tf_op jit(solution)/shard_map/place_rows/pallas_call | solution.py:190
  913.3 5.0 collective-permute-done.89
  924.8 9.1 spread_rows.3
  962.2 10.6 %all-to-all-done.3.in_ref = bf16[16,32,1536]{2,1,0:T(8,128)(2,1)S(1)} async-done(((bf16[16,32,1536]{2,1,0:T(8,128)(2,1)}), bf16[16,32,1536]{2,1,0:T(8,128)(2,1)S(1)}, u32[]{:S(2)}, u32[]{:S(2)}) %all-to-all-start.3) | async-done | bytes 1572896 | tf_op jit(solution)/shard_map/all_to_all | solution.py:1073
  973.9 10.2 %place_rows.3 = f32[16,32,1536]{2,1,0:T(8,128)} custom-call(s32[16]{0:T(128)} %order_ref.7, bf16[16,32,1536]{2,1,0:T(8,128)(2,1)} %copy-done.127), custom_call_target="tpu_custom_call" | custom-call | bytes 4718592 | tf_op jit(solution)/shard_map/place_rows/pallas_call | solution.py:190
  (869 shorter events, 386.8 us)
Async XLA Ops:
  10.8 90.4 %all-to-all-start = ((bf16[16,32,1536]{2,1,0:T(8,128)(2,1)}), bf16[16,32,1536]{2,1,0:T(8,128)(2,1)}, u32[]{:S(2)}, u32[]{:S(2)}) async-start(bf16[16,32,1536]{2,1,0:T(8,128)(2,1)} %pick.1), calls=%async_computation | async-start | bytes 3145728 | tf_op jit(solution)/shard_map/all_to_all | solution.py:867
  19.2 34.6 %collective-permute-start.1 = (bf16[16,192]{1,0:T(8,128)(2,1)S(1)}, bf16[16,192]{1,0:T(8,128)(2,1)S(1)}, u32[]{:S(2)}, u32[]{:S(2)}) collective-permute-start(bf16[16,192]{1,0:T(8,128)(2,1)S(1)} %maximum_maximum_fusion.1), channel_id=1, source_target_pairs={{8,0},{16,8},{24,16},{28,24},{20,28},{12,20},{4,12},{0,4},{9,1},{1... | collective-permute-start | bytes 18440 | tf_op jit(solution)/shard_map/ppermute | solution.py:856
  20.3 37.9 %collective-permute-start.7 = (bf16[192,512]{1,0:T(8,128)(2,1)S(1)}, bf16[192,512]{1,0:T(8,128)(2,1)S(1)}, u32[]{:S(2)}, u32[]{:S(2)}) collective-permute-start(bf16[192,512]{1,0:T(8,128)(2,1)S(1)} %pad_maximum_fusion.4.refs_1_), channel_id=1, source_target_pairs={{0,8},{8,16},{16,24},{24,28},{28,20},{20,12},{12,4},{4,0},{1,9},{9... | collective-permute-start | bytes 589832 | tf_op jit(solution)/shard_map/ppermute | solution.py:885
  22.8 37.6 %collective-permute-start.14 = (bf16[192,512]{1,0:T(8,128)(2,1)S(1)}, bf16[192,512]{1,0:T(8,128)(2,1)S(1)}, u32[]{:S(2)}, u32[]{:S(2)}) collective-permute-start(bf16[192,512]{1,0:T(8,128)(2,1)S(1)} %pad_maximum_fusion.5.refs_9_), channel_id=1, source_target_pairs={{8,0},{16,8},{24,16},{28,24},{20,28},{12,20},{4,12},{0,4},{9,1},{1... | collective-permute-start | bytes 589832 | tf_op jit(solution)/shard_map/ppermute | solution.py:886
  58.2 36.5 %collective-permute-start.8 = (bf16[192,512]{1,0:T(8,128)(2,1)S(1)}, bf16[192,512]{1,0:T(8,128)(2,1)S(1)}, u32[]{:S(2)}, u32[]{:S(2)}) collective-permute-start(bf16[192,512]{1,0:T(8,128)(2,1)S(1)} %collective-permute-done.7.refs_2_), channel_id=1, source_target_pairs={{0,8},{8,16},{16,24},{24,28},{28,20},{20,12},{12,4},{4,0},{1,9},{9... | collective-permute-start | bytes 589832 | tf_op jit(solution)/shard_map/ppermute | solution.py:885
  60.5 35.8 %collective-permute-start.15 = (bf16[192,512]{1,0:T(8,128)(2,1)S(1)}, bf16[192,512]{1,0:T(8,128)(2,1)S(1)}, u32[]{:S(2)}, u32[]{:S(2)}) collective-permute-start(bf16[192,512]{1,0:T(8,128)(2,1)S(1)} %collective-permute-done.14.refs_10_), channel_id=1, source_target_pairs={{8,0},{16,8},{24,16},{28,24},{20,28},{12,20},{4,12},{0,4},{9,1},{1... | collective-permute-start | bytes 589832 | tf_op jit(solution)/shard_map/ppermute | solution.py:886
  61.1 33.4 %collective-permute-start.5 = (bf16[16,192]{1,0:T(8,128)(2,1)S(1)}, bf16[16,192]{1,0:T(8,128)(2,1)S(1)}, u32[]{:S(2)}, u32[]{:S(2)}) collective-permute-start(bf16[16,192]{1,0:T(8,128)(2,1)S(1)} %collective-permute-done.3), channel_id=1, source_target_pairs={{8,0},{16,8},{24,16},{28,24},{20,28},{12,20},{4,12},{0,4},{9,1},{1... | collective-permute-start | bytes 18440 | tf_op jit(solution)/shard_map/ppermute | solution.py:856
  61.1 33.6 %collective-permute-start.6 = (bf16[16,192]{1,0:T(8,128)(2,1)S(1)}, bf16[16,192]{1,0:T(8,128)(2,1)S(1)}, u32[]{:S(2)}, u32[]{:S(2)}) collective-permute-start(bf16[16,192]{1,0:T(8,128)(2,1)S(1)} %collective-permute-done.4), channel_id=1, source_target_pairs={{0,8},{8,16},{16,24},{24,28},{28,20},{20,12},{12,4},{4,0},{1,9},{9... | collective-permute-start | bytes 18440 | tf_op jit(solution)/shard_map/ppermute | solution.py:853
  101.1 236.3 %all-to-all-start.1 = ((bf16[16,32,1664]{2,1,0:T(8,128)(2,1)}), bf16[16,32,1664]{2,1,0:T(8,128)(2,1)}, u32[]{:S(2)}, u32[]{:S(2)}) async-start(bf16[16,32,1664]{2,1,0:T(8,128)(2,1)} %pick_marked.1), calls=%async_computation.1 | async-start | bytes 3407872 | tf_op jit(solution)/shard_map/all_to_all | solution.py:868
  111.6 37.8 %collective-permute-start.22 = (bf16[9,32,1536]{2,1,0:T(8,128)(2,1)}, bf16[9,32,1536]{2,1,0:T(8,128)(2,1)}, u32[]{:S(2)}, u32[]{:S(2)}) collective-permute-start(bf16[9,32,1536]{2,1,0:T(8,128)(2,1)} %get-tuple-element.38.refs_17_.refs_1_), channel_id=1, source_target_pairs={{0,2},{1,3},{2,0},{3,1},{4,6},{5,7},{6,4},{7,5},{8,10},{9,11},{10,... | collective-permute-start | bytes 2654216 | tf_op jit(solution)/shard_map/ppermute | solution.py:781
  115.0 31.2 %collective-permute-start.18 = (bf16[192,512]{1,0:T(8,128)(2,1)S(1)}, bf16[192,512]{1,0:T(8,128)(2,1)S(1)}, u32[]{:S(2)}, u32[]{:S(2)}) collective-permute-start(bf16[192,512]{1,0:T(8,128)(2,1)S(1)} %collective-permute-done.17.refs_13_), channel_id=1, source_target_pairs={{8,0},{16,8},{24,16},{28,24},{20,28},{12,20},{4,12},{0,4},{9,1},{1... | collective-permute-start | bytes 589832 | tf_op jit(solution)/shard_map/ppermute | solution.py:886
  146.2 102.0 %collective-permute-start.21 = (bf16[9,32,1536]{2,1,0:T(8,128)(2,1)}, bf16[9,32,1536]{2,1,0:T(8,128)(2,1)}, u32[]{:S(2)}, u32[]{:S(2)}) collective-permute-start(bf16[9,32,1536]{2,1,0:T(8,128)(2,1)} %get-tuple-element.38.refs_17_.refs_1_), channel_id=1, source_target_pairs={{0,1},{1,0},{2,3},{3,2},{4,5},{5,4},{6,7},{7,6},{8,9},{9,8},{10,11... | collective-permute-start | bytes 2654216 | tf_op jit(solution)/shard_map/ppermute | solution.py:781
  149.4 98.8 %collective-permute-start.23 = (bf16[9,32,1536]{2,1,0:T(8,128)(2,1)}, bf16[9,32,1536]{2,1,0:T(8,128)(2,1)}, u32[]{:S(2)}, u32[]{:S(2)}) collective-permute-start(bf16[9,32,1536]{2,1,0:T(8,128)(2,1)} %collective-permute-done.22.refs_19_.refs_3_), channel_id=1, source_target_pairs={{0,1},{1,0},{2,3},{3,2},{4,5},{5,4},{6,7},{7,6},{8,9},{9,8},{10,11... | collective-permute-start | bytes 2654216 | tf_op jit(solution)/shard_map/ppermute | solution.py:781
  197.4 48.6 %collective-permute-start.24 = (bf16[384,384]{1,0:T(8,128)(2,1)}, bf16[384,384]{1,0:T(8,128)(2,1)S(1)}, u32[]{:S(2)}, u32[]{:S(2)}) collective-permute-start(bf16[384,384]{1,0:T(8,128)(2,1)} %get-tuple-element.182), channel_id=1, source_target_pairs={{0,1},{1,0},{2,3},{3,2},{4,5},{5,4},{6,7},{7,6},{8,9},{9,8},{10,11... | collective-permute-start | bytes 884744 | tf_op jit(solution)/shard_map/ppermute | solution.py:781
  202.2 45.6 %collective-permute-start.25 = (bf16[384,384]{1,0:T(8,128)(2,1)}, bf16[384,384]{1,0:T(8,128)(2,1)}, u32[]{:S(2)}, u32[]{:S(2)}) collective-permute-start(bf16[384,384]{1,0:T(8,128)(2,1)} %get-tuple-element.181), channel_id=1, source_target_pairs={{0,2},{1,3},{2,0},{3,1},{4,6},{5,7},{6,4},{7,5},{8,10},{9,11},{10,... | collective-permute-start | bytes 884744 | tf_op jit(solution)/shard_map/ppermute | solution.py:781
  203.4 44.8 %collective-permute-start.26 = (bf16[384,384]{1,0:T(8,128)(2,1)}, bf16[384,384]{1,0:T(8,128)(2,1)}, u32[]{:S(2)}, u32[]{:S(2)}) collective-permute-start(bf16[384,384]{1,0:T(8,128)(2,1)} %get-tuple-element.180), channel_id=1, source_target_pairs={{0,3},{1,2},{2,1},{3,0},{4,7},{5,6},{6,5},{7,4},{8,11},{9,10},{10,... | collective-permute-start | bytes 884744 | tf_op jit(solution)/shard_map/ppermute | solution.py:781
  246.0 34.6 %collective-permute-start.64 = (bf16[192,768]{1,0:T(8,128)(2,1)}, bf16[192,768]{1,0:T(8,128)(2,1)}, u32[]{:S(2)}, u32[]{:S(2)}) collective-permute-start(bf16[192,768]{1,0:T(8,128)(2,1)} %get-tuple-element.46.refs_1_), channel_id=1, source_target_pairs={{0,8},{8,16},{16,24},{24,28},{28,20},{20,12},{12,4},{4,0},{1,9},{9... | collective-permute-start | bytes 884744 | tf_op jit(solution)/shard_map/ppermute | solution.py:885
  247.8 34.3 %collective-permute-start.71 = (bf16[192,768]{1,0:T(8,128)(2,1)}, bf16[192,768]{1,0:T(8,128)(2,1)}, u32[]{:S(2)}, u32[]{:S(2)}) collective-permute-start(bf16[192,768]{1,0:T(8,128)(2,1)} %get-tuple-element.47.refs_9_), channel_id=1, source_target_pairs={{8,0},{16,8},{24,16},{28,24},{20,28},{12,20},{4,12},{0,4},{9,1},{1... | collective-permute-start | bytes 884744 | tf_op jit(solution)/shard_map/ppermute | solution.py:886
  312.8 33.3 %collective-permute-start.27 = (bf16[9,32,1536]{2,1,0:T(8,128)(2,1)}, bf16[9,32,1536]{2,1,0:T(8,128)(2,1)}, u32[]{:S(2)}, u32[]{:S(2)}) collective-permute-start(bf16[9,32,1536]{2,1,0:T(8,128)(2,1)} %get-tuple-element.172), channel_id=1, source_target_pairs={{0,1},{1,0},{2,3},{3,2},{4,5},{5,4},{6,7},{7,6},{8,9},{9,8},{10,11... | collective-permute-start | bytes 2654216 | tf_op jit(solution)/shard_map/ppermute | solution.py:781
  314.4 31.8 %collective-permute-start.29 = (bf16[9,32,1536]{2,1,0:T(8,128)(2,1)}, bf16[9,32,1536]{2,1,0:T(8,128)(2,1)}, u32[]{:S(2)}, u32[]{:S(2)}) collective-permute-start(bf16[9,32,1536]{2,1,0:T(8,128)(2,1)} %fusion.6), channel_id=1, source_target_pairs={{0,2},{1,3},{2,0},{3,1},{4,6},{5,7},{6,4},{7,5},{8,10},{9,11},{10,... | collective-permute-start | bytes 2654216 | tf_op jit(solution)/shard_map/ppermute | solution.py:781
  362.3 68.3 %collective-permute-start.48 = (bf16[9,32,1664]{2,1,0:T(8,128)(2,1)}, bf16[9,32,1664]{2,1,0:T(8,128)(2,1)}, u32[]{:S(2)}, u32[]{:S(2)}) collective-permute-start(bf16[9,32,1664]{2,1,0:T(8,128)(2,1)} %take_rows.1.refs_21_), channel_id=1, source_target_pairs={{0,2},{1,3},{2,0},{3,1},{4,6},{5,7},{6,4},{7,5},{8,10},{9,11},{10,... | collective-permute-start | bytes 2875400 | tf_op jit(solution)/shard_map/ppermute | solution.py:781
  363.7 72.8 %collective-permute-start.45 = (bf16[9,32,1536]{2,1,0:T(8,128)(2,1)S(1)}, bf16[9,32,1536]{2,1,0:T(8,128)(2,1)S(1)}, u32[]{:S(2)}, u32[]{:S(2)}) collective-permute-start(bf16[9,32,1536]{2,1,0:T(8,128)(2,1)S(1)} %multiply_convert_fusion.refs_17_.refs_5_), channel_id=1, source_target_pairs={{0,2},{1,3},{2,0},{3,1},{4,6},{5,7},{6,4},{7,5},{8,10},{9,11},{10,... | collective-permute-start | bytes 2654216 | tf_op jit(solution)/shard_map/ppermute | solution.py:781
  375.7 45.8 %collective-permute-start.62 = (bf16[192,768]{1,0:T(8,128)(2,1)}, bf16[192,768]{1,0:T(8,128)(2,1)}, u32[]{:S(2)}, u32[]{:S(2)}) collective-permute-start(bf16[192,768]{1,0:T(8,128)(2,1)} %collective-permute-done.61.refs_14_), channel_id=1, source_target_pairs={{8,0},{16,8},{24,16},{28,24},{20,28},{12,20},{4,12},{0,4},{9,1},{1... | collective-permute-start | bytes 884744 | tf_op jit(solution)/shard_map/ppermute | solution.py:886
  391.9 42.6 %collective-permute-start.35 = (bf16[192,768]{1,0:T(8,128)(2,1)S(1)}, bf16[192,768]{1,0:T(8,128)(2,1)}, u32[]{:S(2)}, u32[]{:S(2)}) collective-permute-start(bf16[192,768]{1,0:T(8,128)(2,1)S(1)} %collective-permute-done.34.refs_6_), channel_id=1, source_target_pairs={{0,8},{8,16},{16,24},{24,28},{28,20},{20,12},{12,4},{4,0},{1,9},{9... | collective-permute-start | bytes 884744 | tf_op jit(solution)/shard_map/ppermute | solution.py:885
  392.9 42.8 %collective-permute-start.42 = (bf16[192,768]{1,0:T(8,128)(2,1)S(1)}, bf16[192,768]{1,0:T(8,128)(2,1)}, u32[]{:S(2)}, u32[]{:S(2)}) collective-permute-start(bf16[192,768]{1,0:T(8,128)(2,1)S(1)} %collective-permute-done.41.refs_14_), channel_id=1, source_target_pairs={{8,0},{16,8},{24,16},{28,24},{20,28},{12,20},{4,12},{0,4},{9,1},{1... | collective-permute-start | bytes 884744 | tf_op jit(solution)/shard_map/ppermute | solution.py:886
  421.5 30.0 %collective-permute-start.47 = (bf16[9,32,1664]{2,1,0:T(8,128)(2,1)}, bf16[9,32,1664]{2,1,0:T(8,128)(2,1)}, u32[]{:S(2)}, u32[]{:S(2)}) collective-permute-start(bf16[9,32,1664]{2,1,0:T(8,128)(2,1)} %take_rows.1.refs_21_), channel_id=1, source_target_pairs={{0,1},{1,0},{2,3},{3,2},{4,5},{5,4},{6,7},{7,6},{8,9},{9,8},{10,11... | collective-permute-start | bytes 2875400 | tf_op jit(solution)/shard_map/ppermute | solution.py:781
  450.3 32.4 %collective-permute-start.56 = (bf16[192,768]{1,0:T(8,128)(2,1)}, bf16[192,768]{1,0:T(8,128)(2,1)S(1)}, u32[]{:S(2)}, u32[]{:S(2)}) collective-permute-start(bf16[192,768]{1,0:T(8,128)(2,1)} %collective-permute-done.55.refs_7_), channel_id=1, source_target_pairs={{0,8},{8,16},{16,24},{24,28},{28,20},{20,12},{12,4},{4,0},{1,9},{9... | collective-permute-start | bytes 884744 | tf_op jit(solution)/shard_map/ppermute | solution.py:885
  451.5 31.3 %collective-permute-start.63 = (bf16[192,768]{1,0:T(8,128)(2,1)}, bf16[192,768]{1,0:T(8,128)(2,1)S(1)}, u32[]{:S(2)}, u32[]{:S(2)}) collective-permute-start(bf16[192,768]{1,0:T(8,128)(2,1)} %collective-permute-done.62.refs_15_), channel_id=1, source_target_pairs={{8,0},{16,8},{24,16},{28,24},{20,28},{12,20},{4,12},{0,4},{9,1},{1... | collective-permute-start | bytes 884744 | tf_op jit(solution)/shard_map/ppermute | solution.py:886
  451.8 58.7 %collective-permute-start.36 = (bf16[192,768]{1,0:T(8,128)(2,1)}, bf16[192,768]{1,0:T(8,128)(2,1)S(1)}, u32[]{:S(2)}, u32[]{:S(2)}) collective-permute-start(bf16[192,768]{1,0:T(8,128)(2,1)} %collective-permute-done.35.refs_7_), channel_id=1, source_target_pairs={{0,8},{8,16},{16,24},{24,28},{28,20},{20,12},{12,4},{4,0},{1,9},{9... | collective-permute-start | bytes 884744 | tf_op jit(solution)/shard_map/ppermute | solution.py:885
  453.0 57.6 %collective-permute-start.43 = (bf16[192,768]{1,0:T(8,128)(2,1)}, bf16[192,768]{1,0:T(8,128)(2,1)S(1)}, u32[]{:S(2)}, u32[]{:S(2)}) collective-permute-start(bf16[192,768]{1,0:T(8,128)(2,1)} %collective-permute-done.42.refs_15_), channel_id=1, source_target_pairs={{8,0},{16,8},{24,16},{28,24},{20,28},{12,20},{4,12},{0,4},{9,1},{1... | collective-permute-start | bytes 884744 | tf_op jit(solution)/shard_map/ppermute | solution.py:886
  540.6 65.4 %collective-permute-start.82 = (bf16[9,32,1664]{2,1,0:T(8,128)(2,1)S(1)}, bf16[9,32,1664]{2,1,0:T(8,128)(2,1)S(1)}, u32[]{:S(2)}, u32[]{:S(2)}) collective-permute-start(bf16[9,32,1664]{2,1,0:T(8,128)(2,1)S(1)} %fusion.19), channel_id=1, source_target_pairs={{0,1},{1,0},{2,3},{3,2},{4,5},{5,4},{6,7},{7,6},{8,9},{9,8},{10,11... | collective-permute-start | bytes 2875400 | tf_op jit(solution)/shard_map/ppermute | solution.py:781
  670.8 74.9 %collective-permute-start.78 = (bf16[9,32,1536]{2,1,0:T(8,128)(2,1)}, bf16[9,32,1536]{2,1,0:T(8,128)(2,1)}, u32[]{:S(2)}, u32[]{:S(2)}) collective-permute-start(bf16[9,32,1536]{2,1,0:T(8,128)(2,1)} %get-tuple-element.120), channel_id=1, source_target_pairs={{0,1},{1,0},{2,3},{3,2},{4,5},{5,4},{6,7},{7,6},{8,9},{9,8},{10,11... | collective-permute-start | bytes 2654216 | tf_op jit(solution)/shard_map/ppermute | solution.py:781
  677.7 68.2 %collective-permute-start.80 = (bf16[9,32,1536]{2,1,0:T(8,128)(2,1)}, bf16[9,32,1536]{2,1,0:T(8,128)(2,1)}, u32[]{:S(2)}, u32[]{:S(2)}) collective-permute-start(bf16[9,32,1536]{2,1,0:T(8,128)(2,1)} %fusion.14), channel_id=1, source_target_pairs={{0,2},{1,3},{2,0},{3,1},{4,6},{5,7},{6,4},{7,5},{8,10},{9,11},{10,... | collective-permute-start | bytes 2654216 | tf_op jit(solution)/shard_map/ppermute | solution.py:781
  678.9 41.9 %collective-permute-start.140 = (bf16[192,768]{1,0:T(8,128)(2,1)S(1)}, bf16[192,768]{1,0:T(8,128)(2,1)S(1)}, u32[]{:S(2)}, u32[]{:S(2)}) collective-permute-start(bf16[192,768]{1,0:T(8,128)(2,1)S(1)} %get-tuple-element.140), channel_id=1, source_target_pairs={{8,0},{16,8},{24,16},{28,24},{20,28},{12,20},{4,12},{0,4},{9,1},{1... | collective-permute-start | bytes 884744 | tf_op jit(solution)/shard_map/ppermute | solution.py:893
  680.2 58.8 %collective-permute-start.133 = (bf16[192,768]{1,0:T(8,128)(2,1)S(1)}, bf16[192,768]{1,0:T(8,128)(2,1)}, u32[]{:S(2)}, u32[]{:S(2)}) collective-permute-start(bf16[192,768]{1,0:T(8,128)(2,1)S(1)} %get-tuple-element.141), channel_id=1, source_target_pairs={{0,8},{8,16},{16,24},{24,28},{28,20},{20,12},{12,4},{4,0},{1,9},{9... | collective-permute-start | bytes 884744 | tf_op jit(solution)/shard_map/ppermute | solution.py:892
  680.6 60.4 %collective-permute-start.154 = (bf16[192,768]{1,0:T(8,128)(2,1)}, bf16[192,768]{1,0:T(8,128)(2,1)}, u32[]{:S(2)}, u32[]{:S(2)}) collective-permute-start(bf16[192,768]{1,0:T(8,128)(2,1)} %get-tuple-element.124), channel_id=1, source_target_pairs={{8,0},{16,8},{24,16},{28,24},{20,28},{12,20},{4,12},{0,4},{9,1},{1... | collective-permute-start | bytes 884744 | tf_op jit(solution)/shard_map/ppermute | solution.py:893
  763.5 39.1 %collective-permute-start.165 = (bf16[192,768]{1,0:T(8,128)(2,1)S(1)}, bf16[192,768]{1,0:T(8,128)(2,1)}, u32[]{:S(2)}, u32[]{:S(2)}) collective-permute-start(bf16[192,768]{1,0:T(8,128)(2,1)S(1)} %get-tuple-element.123.refs_5_), channel_id=1, source_target_pairs={{0,2},{1,3},{2,0},{3,1},{4,6},{5,7},{6,4},{7,5},{8,10},{9,11},{10,... | collective-permute-start | bytes 884744 | tf_op jit(solution)/shard_map/ppermute | solution.py:781
  764.9 42.0 %collective-permute-start.166 = (bf16[192,768]{1,0:T(8,128)(2,1)S(1)}, bf16[192,768]{1,0:T(8,128)(2,1)}, u32[]{:S(2)}, u32[]{:S(2)}) collective-permute-start(bf16[192,768]{1,0:T(8,128)(2,1)S(1)} %get-tuple-element.122.refs_6_), channel_id=1, source_target_pairs={{0,2},{1,3},{2,0},{3,1},{4,6},{5,7},{6,4},{7,5},{8,10},{9,11},{10,... | collective-permute-start | bytes 884744 | tf_op jit(solution)/shard_map/ppermute | solution.py:781
  771.2 36.1 %collective-permute-start.167 = (bf16[192,768]{1,0:T(8,128)(2,1)S(1)}, bf16[192,768]{1,0:T(8,128)(2,1)}, u32[]{:S(2)}, u32[]{:S(2)}) collective-permute-start(bf16[192,768]{1,0:T(8,128)(2,1)S(1)} %collective-permute-done.161.refs_13_), channel_id=1, source_target_pairs={{0,1},{1,0},{2,3},{3,2},{4,5},{5,4},{6,7},{7,6},{8,9},{9,8},{10,11... | collective-permute-start | bytes 884744 | tf_op jit(solution)/shard_map/ppermute | solution.py:781
  798.0 79.0 %all-to-all-start.2 = ((bf16[16,32,1536]{2,1,0:T(8,128)(2,1)}), bf16[16,32,1536]{2,1,0:T(8,128)(2,1)}, u32[]{:S(2)}, u32[]{:S(2)}) async-start(bf16[16,32,1536]{2,1,0:T(8,128)(2,1)} %spread_rows.2), calls=%async_computation.2 | async-start | bytes 3145728 | tf_op jit(solution)/shard_map/all_to_all | solution.py:1066
  845.2 51.3 %collective-permute-start.88 = (bf16[9,32,1536]{2,1,0:T(8,128)(2,1)}, bf16[9,32,1536]{2,1,0:T(8,128)(2,1)}, u32[]{:S(2)}, u32[]{:S(2)}) collective-permute-start(bf16[9,32,1536]{2,1,0:T(8,128)(2,1)} %get-tuple-element.171), channel_id=1, source_target_pairs={{0,1},{1,0},{2,3},{3,2},{4,5},{5,4},{6,7},{7,6},{8,9},{9,8},{10,11... | collective-permute-start | bytes 2654216 | tf_op jit(solution)/shard_map/ppermute | solution.py:781
  847.5 39.8 %collective-permute-start.96 = (bf16[192,512]{1,0:T(8,128)(2,1)}, bf16[192,512]{1,0:T(8,128)(2,1)}, u32[]{:S(2)}, u32[]{:S(2)}) collective-permute-start(bf16[192,512]{1,0:T(8,128)(2,1)} %add_convert_fusion.57), channel_id=1, source_target_pairs={{0,8},{8,16},{16,24},{24,28},{28,20},{20,12},{12,4},{4,0},{1,9},{9... | collective-permute-start | bytes 589832 | tf_op jit(solution)/shard_map/ppermute | solution.py:892
  851.6 38.1 %collective-permute-start.106 = (bf16[192,640]{1,0:T(8,128)(2,1)}, bf16[192,640]{1,0:T(8,128)(2,1)}, u32[]{:S(2)}, u32[]{:S(2)}) collective-permute-start(bf16[192,640]{1,0:T(8,128)(2,1)} %add_convert_fusion.50), channel_id=1, source_target_pairs={{8,0},{16,8},{24,16},{28,24},{20,28},{12,20},{4,12},{0,4},{9,1},{1... | collective-permute-start | bytes 737288 | tf_op jit(solution)/shard_map/ppermute | solution.py:893
  874.7 38.6 %collective-permute-start.87 = (bf16[9,32,1536]{2,1,0:T(8,128)(2,1)}, bf16[9,32,1536]{2,1,0:T(8,128)(2,1)}, u32[]{:S(2)}, u32[]{:S(2)}) collective-permute-start(bf16[9,32,1536]{2,1,0:T(8,128)(2,1)} %get-tuple-element.170), channel_id=1, source_target_pairs={{0,1},{1,0},{2,3},{3,2},{4,5},{5,4},{6,7},{7,6},{8,9},{9,8},{10,11... | collective-permute-start | bytes 2654216 | tf_op jit(solution)/shard_map/ppermute | solution.py:781
  907.3 31.1 %collective-permute-start.100 = (bf16[192,512]{1,0:T(8,128)(2,1)S(1)}, bf16[192,512]{1,0:T(8,128)(2,1)}, u32[]{:S(2)}, u32[]{:S(2)}) collective-permute-start(bf16[192,512]{1,0:T(8,128)(2,1)S(1)} %add_convert_fusion.53), channel_id=1, source_target_pairs={{0,1},{1,0},{2,3},{3,2},{4,5},{5,4},{6,7},{7,6},{8,9},{9,8},{10,11... | collective-permute-start | bytes 589832 | tf_op jit(solution)/shard_map/ppermute | solution.py:781
  909.8 30.9 %collective-permute-start.101 = (bf16[192,512]{1,0:T(8,128)(2,1)S(1)}, bf16[192,512]{1,0:T(8,128)(2,1)}, u32[]{:S(2)}, u32[]{:S(2)}) collective-permute-start(bf16[192,512]{1,0:T(8,128)(2,1)S(1)} %add_convert_fusion.53), channel_id=1, source_target_pairs={{0,2},{1,3},{2,0},{3,1},{4,6},{5,7},{6,4},{7,5},{8,10},{9,11},{10,... | collective-permute-start | bytes 589832 | tf_op jit(solution)/shard_map/ppermute | solution.py:781
  912.1 35.3 %collective-permute-start.109 = (bf16[192,640]{1,0:T(8,128)(2,1)S(1)}, bf16[192,640]{1,0:T(8,128)(2,1)S(1)}, u32[]{:S(2)}, u32[]{:S(2)}) collective-permute-start(bf16[192,640]{1,0:T(8,128)(2,1)S(1)} %add_convert_fusion.47), channel_id=1, source_target_pairs={{8,0},{16,8},{24,16},{28,24},{20,28},{12,20},{4,12},{0,4},{9,1},{1... | collective-permute-start | bytes 737288 | tf_op jit(solution)/shard_map/ppermute | solution.py:893
  934.0 38.8 %all-to-all-start.3 = ((bf16[16,32,1536]{2,1,0:T(8,128)(2,1)}), bf16[16,32,1536]{2,1,0:T(8,128)(2,1)S(1)}, u32[]{:S(2)}, u32[]{:S(2)}) async-start(bf16[16,32,1536]{2,1,0:T(8,128)(2,1)} %spread_rows.3), calls=%async_computation.3 | async-start | bytes 3145728 | tf_op jit(solution)/shard_map/all_to_all | solution.py:1073
  (308 other events, 5374.2 us)

commit v2 on v1

v2 whole, which is shorter than its diff:
```python
import jax
import jax.numpy as jnp
from jax import lax
from jax.experimental import pallas as pl
from jax.experimental.pallas import tpu as pltpu
from jax.sharding import PartitionSpec as P

QUERY_HEADS = 24
KEY_VALUE_HEADS = 8
HEAD = 64
PAIR_TOK = 1152
MEMBERS = 4
LANE = 128
TILE = 384
KEYROWS = 128
UNIT = PAIR_TOK // KEYROWS // 1
eps_norm = 1e-06
rope_base = 10000.0
NEG = -1e30
BF = jnp.bfloat16
F32 = jnp.float32

Q_LOC = QUERY_HEADS // MEMBERS * HEAD
KV_LOC = KEY_VALUE_HEADS // MEMBERS * HEAD
KVH = KEY_VALUE_HEADS // MEMBERS
GROUP = QUERY_HEADS // KEY_VALUE_HEADS
QKV = Q_LOC + 2 * KV_LOC
OUT_F = LANE
OUT_B = Q_LOC - OUT_F
GAINS_AT = 64

ANY = pl.BlockSpec(memory_space=pl.ANY)
SMEM = pl.BlockSpec(memory_space=pltpu.SMEM)
VM = pl.BlockSpec(memory_space=pltpu.VMEM)


def params(megabytes):
    return pltpu.CompilerParams(vmem_limit_bytes=megabytes << 20)


def cost(flops, moved, trans=0):
    return pl.CostEstimate(flops=flops // 100, bytes_accessed=moved // 100, transcendentals=trans // 100)


def dot(a, b):
    return lax.dot_general(a, b, (((1,), (0,)), ((), ())), preferred_element_type=F32)


def dot_nt(a, b):
    return lax.dot_general(a, b, (((1,), (1,)), ((), ())), preferred_element_type=F32)


def dot_tn(a, b):
    return lax.dot_general(a, b, (((0,), (0,)), ((), ())), preferred_element_type=F32)


def pick_rows(values, order):
    count = values.shape[0]

    def kernel(order_ref, in_ref, out_ref, sems):
        copies = [
            pltpu.make_async_copy(in_ref.at[order_ref[i]], out_ref.at[i], sems.at[i])
            for i in range(count)
        ]
        for c in copies:
            c.start()
        wait_all(copies)

    return pl.pallas_call(
        kernel,
        out_shape=jax.ShapeDtypeStruct(values.shape, values.dtype),
        in_specs=[SMEM, ANY],
        out_specs=VM,
        scratch_shapes=[pltpu.SemaphoreType.DMA((count,))],
        cost_estimate=cost(0, 4 * values.size),
        name="pick",
    )(order, values)


def pick_marked(values, routes, order):
    count, block, width = values.shape
    topk = routes.shape[2]

    def kernel(order_ref, in_ref, route_ref, out_ref, sems):
        copies = [
            pltpu.make_async_copy(
                in_ref.at[order_ref[i]], out_ref.at[i, :, pl.ds(0, width)], sems.at[i]
            )
            for i in range(count)
        ]
        for c in copies:
            c.start()
        lanes = lax.broadcasted_iota(jnp.int32, (block, LANE), 1)

        def mark_one(i, carry):
            routed = route_ref[order_ref[i]]
            mark = jnp.zeros((block, LANE), F32)
            for k in range(topk):
                mark = mark + jnp.where(routed[:, k : k + 1] == lanes, 1.0, 0.0)
            out_ref[i, :, width:] = mark.astype(BF)
            return carry

        lax.fori_loop(0, count, mark_one, 0)
        wait_all(copies)

    return pl.pallas_call(
        kernel,
        out_shape=jax.ShapeDtypeStruct((count, block, width + LANE), values.dtype),
        in_specs=[SMEM, ANY, VM],
        out_specs=VM,
        scratch_shapes=[pltpu.SemaphoreType.DMA((count,))],
        cost_estimate=cost(0, 4 * values.size),
        name="pick_marked",
    )(order, values, routes)


def take_rows(dealt, first, units):
    _, block, width = dealt.shape

    def kernel(first_ref, in_ref, out_ref, sems):
        copies = []
        for t in range(units):
            source = jnp.where(t < first_ref[0], 2 * t, 2 * (t - first_ref[0]) + 1)
            copies.append(pltpu.make_async_copy(in_ref.at[source], out_ref.at[t], sems.at[t]))
            copies[-1].start()
        wait_all(copies)

    return pl.pallas_call(
        kernel,
        out_shape=jax.ShapeDtypeStruct((units, block, width), BF),
        in_specs=[SMEM, ANY],
        out_specs=VM,
        scratch_shapes=[pltpu.SemaphoreType.DMA((units,))],
        cost_estimate=cost(0, 4 * units * block * width),
        name="take_rows",
    )(first, dealt)


def spread_rows(rows, first, slots):
    units, block, width = rows.shape

    def kernel(first_ref, in_ref, out_ref):
        for i in range(slots):
            u = i // 2 if i % 2 == 0 else first_ref[0] + i // 2
            limit = first_ref[0] if i % 2 == 0 else units - first_ref[0]
            keep = i // 2 < limit

            @pl.when(keep)
            def _():
                out_ref[i] = in_ref[jnp.minimum(u, units - 1)]

            @pl.when(jnp.logical_not(keep))
            def _():
                out_ref[i] = jnp.zeros((block, width), BF)

    return pl.pallas_call(
        kernel,
        out_shape=jax.ShapeDtypeStruct((slots, block, width), BF),
        in_specs=[SMEM, VM],
        out_specs=VM,
        cost_estimate=cost(0, 4 * slots * block * width),
        name="spread_rows",
    )(first, rows)


def place_rows(values, order):
    count, block, width = values.shape

    def kernel(order_ref, in_ref, out_ref, hold, sems):
        copies = []
        for j in range(count):
            hold[j] = in_ref[j].astype(F32)
            copies.append(
                pltpu.make_async_copy(hold.at[j], out_ref.at[order_ref[j]], sems.at[j])
            )
            copies[-1].start()
        wait_all(copies)

    return pl.pallas_call(
        kernel,
        out_shape=jax.ShapeDtypeStruct(values.shape, F32),
        in_specs=[SMEM, VM],
        out_specs=ANY,
        scratch_shapes=[
            pltpu.VMEM(values.shape, F32),
            pltpu.SemaphoreType.DMA((count,)),
        ],
        cost_estimate=cost(0, 6 * values.size),
        name="place_rows",
    )(order, values)


def place_experts(places, shares, weight, lo, count, split, per, total):
    rows = shares[0].shape[0]
    width = shares[0].shape[1] // count
    half = width // 2
    used = 2 * width // 3

    def kernel(*refs):
        tab = refs[0]
        ins = refs[1 : 1 + MEMBERS]
        weight_ref = refs[1 + MEMBERS]
        out, gain, hold, w_v, sems, sem_w = refs[-6:]
        loads = []
        for k in range(MEMBERS):
            for e in range(count):
                at = k * count + e
                loads.append(
                    pltpu.make_async_copy(
                        weight_ref.at[tab[k] * per + lo + e, :, pl.ds(0, used)],
                        w_v.at[tab[k] * count + e],
                        sem_w.at[at],
                    )
                )
                loads[-1].start()
        copies = []
        for k in range(MEMBERS):
            for e in range(count):
                at = tab[k] * count + e
                for side in range(2):
                    col = (side * count + e) * half if split else e * width + side * half
                    hold[at, :, side * half : (side + 1) * half] = ins[k][
                        :, col : col + half
                    ].astype(F32)
                copies.append(
                    pltpu.make_async_copy(
                        hold.at[at], out.at[tab[k] * per + lo + e], sems.at[k * count + e]
                    )
                )
                copies[-1].start()
        wait_all(loads)
        gain[...] = jnp.zeros_like(gain)

        def add(at, carry):
            total = jnp.zeros((rows, LANE), F32)
            for c in range(used // LANE):
                cols = slice(c * LANE, (c + 1) * LANE)
                total = total + w_v[at, :, cols].astype(BF).astype(F32) * hold[at, :, cols]
            gain[...] += total
            return carry

        lax.fori_loop(0, MEMBERS * count, add, 0)
        wait_all(copies)

    before = [] if total is None else [total]
    return pl.pallas_call(
        kernel,
        out_shape=(
            jax.ShapeDtypeStruct((MEMBERS * per, rows, width), F32),
            jax.ShapeDtypeStruct((rows, LANE), F32),
        ),
        in_specs=[SMEM] + [VM] * MEMBERS + [ANY] * (1 + len(before)),
        out_specs=(ANY, VM),
        input_output_aliases={2 + MEMBERS: 0} if before else {},
        scratch_shapes=[
            pltpu.VMEM((MEMBERS * count, rows, width), F32),
            pltpu.VMEM((MEMBERS * count, rows, used), F32),
            pltpu.SemaphoreType.DMA((MEMBERS * count,)),
            pltpu.SemaphoreType.DMA((MEMBERS * count,)),
        ],
        compiler_params=params(40),
        cost_estimate=cost(0, 6 * MEMBERS * count * rows * width),
        name="place_experts",
    )(places, *shares, weight, *before)


def start_rows(refs, scratch, table, at, sems):
    copies = []
    for k in range(MEMBERS):
        place = pl.multiple_of(table[at + k] * 32, 32)
        copies.append(
            pltpu.make_async_copy(refs[k], scratch.at[:, pl.ds(place, 32), :], sems.at[k])
        )
        copies[-1].start()
    return copies


def start_weights(refs_f, refs_b, wf, wb, scratch, table, sems):
    copies = []
    n = len(refs_f)
    for s in range(n):
        rows = refs_f[s].shape[0]
        row_f = pl.multiple_of(table[s], 16)
        row_b = pl.multiple_of(table[n + s], 16)
        copies.append(
            pltpu.make_async_copy(
                refs_f[s].at[:, pl.ds(0, wf)],
                scratch.at[pl.ds(row_f, rows), pl.ds(0, wf)],
                sems.at[s],
            )
        )
        copies.append(
            pltpu.make_async_copy(
                refs_b[s].at[:, pl.ds(0, wb)],
                scratch.at[pl.ds(row_b, rows), pl.ds(wf, wb)],
                sems.at[n + s],
            )
        )
    for c in copies:
        c.start()
    return copies


def start_out(refs, scratch, table, at, sems):
    copies = []
    for k in range(MEMBERS):
        copies.append(pltpu.make_async_copy(refs[k], scratch.at[table[at + k]], sems.at[k]))
        copies[-1].start()
    return copies


def store_members(out, table, at, tiles, values, cols=None):
    per = values.shape[0] // KEYROWS
    shaped = values.reshape(per, KEYROWS, values.shape[1])
    for j in range(MEMBERS):
        piece = shaped[:, j * 32 : (j + 1) * 32]
        if cols is None:
            out[table[at + j], tiles] = piece
        else:
            out[table[at + j], tiles, :, cols] = piece


def wait_all(copies):
    for c in copies:
        c.wait()


def turn(values, cosine, sine):
    width = values.shape[1]
    lanes = lax.broadcasted_iota(jnp.int32, values.shape, 1)
    low = pltpu.roll(values, width - HEAD // 2, 1)
    high = pltpu.roll(values, HEAD // 2, 1)
    swapped = jnp.where(lanes % HEAD < HEAD // 2, low, high)
    reps = width // LANE
    return values * jnp.concatenate([cosine] * reps, 1) + swapped * jnp.concatenate([sine] * reps, 1)


def bias_for(t, extent, first_len):
    gi = lax.broadcasted_iota(jnp.int32, (KEYROWS, extent), 0) + t * KEYROWS
    gj = lax.broadcasted_iota(jnp.int32, (KEYROWS, extent), 1)
    allowed = (gj <= gi) & ((gi < first_len) | (gj >= first_len))
    return jnp.concatenate([jnp.where(allowed, 0.0, NEG)] * GROUP, 0)


def attention_forward(table, base, af, ab, rows_x, cosine, sine, width):
    n = len(af)
    tiles = PAIR_TOK // TILE
    per = TILE // KEYROWS
    nt = PAIR_TOK // KEYROWS
    chunk = af[0].shape[0]

    def kernel(*refs):
        tab = refs[0]
        f_refs = refs[1 : 1 + n]
        b_refs = refs[1 + n : 1 + 2 * n]
        x_refs = refs[1 + 2 * n : 5 + 2 * n]
        cos_ref, sin_ref = refs[5 + 2 * n : 7 + 2 * n]
        a_out, q_out, k_out, v_out, heads, small, gains = refs[7 + 2 * n : 14 + 2 * n]
        w_v, sem_x, sem_w, sem_s = refs[14 + 2 * n :]
        cs = []
        for s in range(n):
            row = pl.ds(pl.multiple_of(tab[s], 16), chunk)
            cs.append(
                pltpu.make_async_copy(
                    f_refs[s].at[:, pl.ds(Q_LOC + OUT_F, LANE)], small.at[row, :], sem_s.at[s]
                )
            )
            cs[-1].start()
        cw = start_weights(f_refs, b_refs, Q_LOC, 2 * KV_LOC, w_v, tab, sem_w)
        cx = start_rows(x_refs, a_out, tab, base, sem_x)
        wait_all(cs)
        pick = lax.broadcasted_iota(jnp.int32, (8, LANE), 1)
        pick = pick == lax.broadcasted_iota(jnp.int32, (8, LANE), 0) + GAINS_AT
        gains[...] = dot_nt(pick.astype(F32).astype(BF), small[...])
        wait_all(cw)
        wait_all(cx)
        first_len = tab[base + 8]

        def project(i, carry):
            at = pl.ds(i * per, per)
            x = a_out[at].reshape(TILE, width).astype(F32)
            scale = lax.rsqrt(jnp.mean(x * x, axis=-1, keepdims=True) + eps_norm)
            block = (x * scale * gains[0:1, :]).astype(BF)
            a_out[at] = block.reshape(per, KEYROWS, width)
            y = dot(block, w_v[...])
            rows = pl.ds(pl.multiple_of(i * TILE, TILE), TILE)
            turned = turn(y[:, : Q_LOC + KV_LOC], cos_ref[rows, :], sin_ref[rows, :])
            q = (turned[:, :Q_LOC] * 0.125).astype(BF)
            k = turned[:, Q_LOC:].astype(BF)
            v = y[:, Q_LOC + KV_LOC :].astype(BF)
            for j in range(KVH):
                k_out[j, rows, :] = k[:, j * HEAD : (j + 1) * HEAD]
                v_out[j, rows, :] = v[:, j * HEAD : (j + 1) * HEAD]
                for h in range(GROUP):
                    c = (j * GROUP + h) * HEAD
                    for r in range(per):
                        q_out[j, i * per + r, h * KEYROWS : (h + 1) * KEYROWS, :] = q[
                            r * KEYROWS : (r + 1) * KEYROWS, c : c + HEAD
                        ]
            return carry

        lax.fori_loop(0, tiles, project, 0)
        for c in range(tiles):
            extent = (c + 1) * TILE

            def attend(i, carry, c=c, extent=extent):
                t = c * per + i
                bias = bias_for(t, extent, first_len)
                mixed = []
                for j in range(KVH):
                    s = dot_nt(q_out[j, t], k_out[j, :extent, :]) + bias
                    top = jnp.max(s, axis=1, keepdims=True)
                    p = jnp.exp(s - top)
                    total = jnp.sum(p, axis=1, keepdims=True)
                    o = dot(p.astype(BF), v_out[j, :extent, :]) / total
                    mixed += [o[h * KEYROWS : (h + 1) * KEYROWS] for h in range(GROUP)]
                rows = pl.ds(pl.multiple_of(t * KEYROWS, KEYROWS), KEYROWS)
                heads[rows, :] = jnp.concatenate(mixed, 1).astype(BF)
                return carry

            lax.fori_loop(0, per, attend, 0)

    return pl.pallas_call(
        kernel,
        out_shape=(
            jax.ShapeDtypeStruct((nt, KEYROWS, width), BF),
            jax.ShapeDtypeStruct((KVH, nt, GROUP * KEYROWS, HEAD), BF),
            jax.ShapeDtypeStruct((KVH, PAIR_TOK, HEAD), BF),
            jax.ShapeDtypeStruct((KVH, PAIR_TOK, HEAD), BF),
            jax.ShapeDtypeStruct((PAIR_TOK, Q_LOC), BF),
            jax.ShapeDtypeStruct((width, LANE), BF),
            jax.ShapeDtypeStruct((8, width), F32),
        ),
        in_specs=[SMEM] + [ANY] * (2 * n + 4) + [VM, VM],
        out_specs=(VM,) * 7,
        scratch_shapes=[
            pltpu.VMEM((width, QKV), BF),
            pltpu.SemaphoreType.DMA((4,)),
            pltpu.SemaphoreType.DMA((2 * n,)),
            pltpu.SemaphoreType.DMA((n,)),
        ],
        compiler_params=params(48),
        cost_estimate=cost(12 * 10**9, 14 << 20, 5 * 10**6),
        name="attention_forward",
    )(table, *af, *ab, *rows_x, cosine, sine)


def project_out(table, base, heads, wout, width):
    tiles = PAIR_TOK // TILE
    per = TILE // KEYROWS
    nt = PAIR_TOK // KEYROWS

    def kernel(tab, heads, *refs):
        o_refs, (part, o_v, sem_o) = refs[:MEMBERS], refs[MEMBERS:]
        wait_all(start_out(o_refs, o_v, tab, base + 4, sem_o))
        for i in range(tiles):
            h = heads[i * TILE : (i + 1) * TILE, :]
            for j in range(MEMBERS):
                y = dot(h, o_v[j]).astype(BF)
                store_members(
                    part, tab, base, pl.ds(i * per, per), y, pl.ds(j * Q_LOC, Q_LOC)
                )

    return pl.pallas_call(
        kernel,
        out_shape=jax.ShapeDtypeStruct((MEMBERS, nt, 32, width), BF),
        in_specs=[SMEM, VM] + [ANY] * MEMBERS,
        out_specs=VM,
        scratch_shapes=[
            pltpu.VMEM((MEMBERS, Q_LOC, Q_LOC), BF),
            pltpu.SemaphoreType.DMA((4,)),
        ],
        compiler_params=params(24),
        cost_estimate=cost(2 * 10**9, 6 << 20),
        name="project_out",
    )(table, heads, *wout)


def attention_backward(table, base, af, ab, rows_m, wout, q, k, v, cosine, sine, width):
    n = len(af)
    tiles = PAIR_TOK // TILE
    per = TILE // KEYROWS
    nt = PAIR_TOK // KEYROWS
    wide = rows_m[0].shape[2]

    def kernel(*refs):
        tab = refs[0]
        f_refs = refs[1 : 1 + n]
        b_refs = refs[1 + n : 1 + 2 * n]
        m_refs = refs[1 + 2 * n : 5 + 2 * n]
        o_refs = refs[5 + 2 * n : 9 + 2 * n]
        q_ref, k_ref, v_ref, cos_ref, sin_ref = refs[9 + 2 * n : 14 + 2 * n]
        da, dqkv = refs[14 + 2 * n : 16 + 2 * n]
        m_v, w_v, o_v, dh_s, dq_s, dk_s, dv_s, sem_m, sem_w, sem_o = refs[16 + 2 * n :]
        cm = start_rows(m_refs, m_v, tab, base, sem_m)
        co = start_out(o_refs, o_v, tab, base + 4, sem_o)
        cw = start_weights(f_refs, b_refs, Q_LOC, 2 * KV_LOC, w_v, tab, sem_w)
        dk_s[...] = jnp.zeros_like(dk_s)
        dv_s[...] = jnp.zeros_like(dv_s)
        wait_all(co)
        wait_all(cm)
        first_len = tab[base + 8]

        def heads_back(i, carry):
            total = None
            for j in range(MEMBERS):
                block = m_v[pl.ds(i * per, per), :, j * Q_LOC : (j + 1) * Q_LOC]
                y = dot_nt(block.reshape(TILE, Q_LOC), o_v[j])
                total = y if total is None else total + y
            total = total.astype(BF)
            for j in range(KVH):
                for h in range(GROUP):
                    c = (j * GROUP + h) * HEAD
                    for r in range(per):
                        dh_s[j, i * per + r, h * KEYROWS : (h + 1) * KEYROWS, :] = total[
                            r * KEYROWS : (r + 1) * KEYROWS, c : c + HEAD
                        ]
            return carry

        lax.fori_loop(0, tiles, heads_back, 0)
        for c in range(tiles):
            extent = (c + 1) * TILE

            def attend(i, carry, c=c, extent=extent):
                t = c * per + i
                bias = bias_for(t, extent, first_len)
                for j in range(KVH):
                    qb = q_ref[j, t]
                    db = dh_s[j, t]
                    kb = k_ref[j, :extent, :]
                    s = dot_nt(qb, kb) + bias
                    top = jnp.max(s, axis=1, keepdims=True)
                    p = jnp.exp(s - top)
                    p = p * (1.0 / jnp.sum(p, axis=1, keepdims=True))
                    dp = dot_nt(db, v_ref[j, :extent, :])
                    prod = p * dp
                    delta = jnp.sum(prod, axis=1, keepdims=True)
                    ds = (prod - p * delta).astype(BF)
                    dq_s[j, t] = dot(ds, kb) * 0.125
                    dk_s[j, :extent, :] += dot_tn(ds, qb)
                    dv_s[j, :extent, :] += dot_tn(p.astype(BF), db)
                return carry

            lax.fori_loop(0, per, attend, 0)
        wait_all(cw)

        def inputs_back(i, carry):
            rows = pl.ds(pl.multiple_of(i * TILE, TILE), TILE)
            cols = []
            for j in range(KVH):
                for h in range(GROUP):
                    cols.append(
                        jnp.concatenate(
                            [
                                dq_s[j, i * per + r, h * KEYROWS : (h + 1) * KEYROWS, :]
                                for r in range(per)
                            ],
                            0,
                        )
                    )
            cols += [dk_s[j, rows, :] for j in range(KVH)]
            joined = jnp.concatenate(cols, 1).astype(BF).astype(F32)
            turned = turn(joined, cos_ref[rows, :], -sin_ref[rows, :])
            value = jnp.concatenate([dv_s[j, rows, :] for j in range(KVH)], 1)
            out = jnp.concatenate([turned, value], 1).astype(BF)
            dqkv[rows, :] = out
            y = dot_nt(out, w_v[...]).astype(BF)
            store_members(da, tab, base, pl.ds(i * per, per), y)
            return carry

        lax.fori_loop(0, tiles, inputs_back, 0)

    return pl.pallas_call(
        kernel,
        out_shape=(
            jax.ShapeDtypeStruct((MEMBERS, nt, 32, width), BF),
            jax.ShapeDtypeStruct((PAIR_TOK, QKV), BF),
        ),
        in_specs=[SMEM] + [ANY] * (2 * n + 8) + [VM] * 5,
        out_specs=(VM,) * 2,
        scratch_shapes=[
            pltpu.VMEM((nt, KEYROWS, wide), BF),
            pltpu.VMEM((width, QKV), BF),
            pltpu.VMEM((MEMBERS, Q_LOC, Q_LOC), BF),
            pltpu.VMEM((KVH, nt, GROUP * KEYROWS, HEAD), BF),
            pltpu.VMEM((KVH, nt, GROUP * KEYROWS, HEAD), F32),
            pltpu.VMEM((KVH, PAIR_TOK, HEAD), F32),
            pltpu.VMEM((KVH, PAIR_TOK, HEAD), F32),
            pltpu.SemaphoreType.DMA((4,)),
            pltpu.SemaphoreType.DMA((2 * n,)),
            pltpu.SemaphoreType.DMA((4,)),
        ],
        compiler_params=params(56),
        cost_estimate=cost(20 * 10**9, 16 << 20, 5 * 10**6),
        name="attention_backward",
    )(table, *af, *ab, *rows_m, *wout, q, k, v, cosine, sine)


def attention_grads(table, base, a_all, rows_b, rows_m, heads, dqkv, width, n):
    nt = PAIR_TOK // KEYROWS
    step = Q_LOC
    chunk = width // n
    owners = step // chunk
    wide = rows_m[0].shape[2]
    wide_f = Q_LOC + OUT_F
    wide_b = 2 * KV_LOC + OUT_B + LANE

    def kernel(*refs):
        tab = refs[0]
        b_refs, m_refs = refs[1:5], refs[5:9]
        a_ref, heads_ref, d_ref = refs[9:12]
        gf, gb, go = refs[12:15]
        b_v, m_v, sem_b, sem_m = refs[15:]
        j = pl.program_id(0)

        @pl.when(j == 0)
        def _():
            cb = start_rows(b_refs, b_v, tab, base, sem_b)
            cm = start_rows(m_refs, m_v, tab, base, sem_m)
            wait_all(cb)
            wait_all(cm)

        cols = pl.ds(pl.multiple_of(j * step, step), step)
        a = a_ref[...].reshape(PAIR_TOK, step)
        gq = dot_tn(a, d_ref[...]).astype(BF)
        b = b_v[:, :, cols].reshape(PAIR_TOK, step)
        gr = dot_tn(b, m_v[:, :, width:].reshape(PAIR_TOK, LANE)).astype(BF)
        for h in range(owners):
            rows = slice(h * chunk, (h + 1) * chunk)
            to_f = tab[base + 10 + j * owners + h]
            to_b = tab[base + 10 + n + j * owners + h]
            gf[to_f, :, :Q_LOC] = gq[rows, :Q_LOC]
            gb[to_b, :, : 2 * KV_LOC] = gq[rows, Q_LOC:]
            gb[to_b, :, 2 * KV_LOC + OUT_B :] = gr[rows, :]
        m = m_v[:, :, cols].reshape(PAIR_TOK, step)
        go[tab[base + 4 + j]] = dot_tn(heads_ref[...], m).astype(BF)

    return pl.pallas_call(
        kernel,
        grid=(width // step,),
        out_shape=(
            jax.ShapeDtypeStruct((n, chunk, wide_f), BF),
            jax.ShapeDtypeStruct((n, chunk, wide_b), BF),
            jax.ShapeDtypeStruct((MEMBERS, Q_LOC, Q_LOC), BF),
        ),
        in_specs=[SMEM]
        + [ANY] * 8
        + [
            pl.BlockSpec((nt, KEYROWS, step), lambda j: (0, 0, j)),
            pl.BlockSpec((PAIR_TOK, Q_LOC), lambda j: (0, 0)),
            pl.BlockSpec((PAIR_TOK, QKV), lambda j: (0, 0)),
        ],
        out_specs=(
            pl.BlockSpec((n, chunk, wide_f), lambda j: (0, 0, 0)),
            pl.BlockSpec((n, chunk, wide_b), lambda j: (0, 0, 0)),
            pl.BlockSpec((MEMBERS, Q_LOC, Q_LOC), lambda j: (0, 0, 0)),
        ),
        scratch_shapes=[
            pltpu.VMEM((nt, KEYROWS, width), BF),
            pltpu.VMEM((nt, KEYROWS, wide), BF),
            pltpu.SemaphoreType.DMA((4,)),
            pltpu.SemaphoreType.DMA((4,)),
        ],
        compiler_params=params(48),
        cost_estimate=cost(4 * 10**9, 16 << 20),
        name="attention_grads",
    )(table, *rows_b, *rows_m, a_all, heads, dqkv)


def pack_out_grads(table, base, pieces, part_f, part_b):
    n, chunk, wide_f = part_f.shape
    wide_b = part_b.shape[2]
    owners = n // MEMBERS

    def kernel(*refs):
        tab = refs[0]
        ins = refs[1 : 1 + MEMBERS]
        out_f, out_b, sems = refs[3 + MEMBERS :]
        copies = []
        for k in range(MEMBERS):
            for h in range(owners):
                owner = tab[base + 4 + k] * owners + h
                rows = pl.ds(h * chunk, chunk)
                copies.append(
                    pltpu.make_async_copy(
                        ins[k].at[rows, pl.ds(0, OUT_F)],
                        out_f.at[tab[base + 10 + owner], :, pl.ds(Q_LOC, OUT_F)],
                        sems.at[2 * (k * owners + h)],
                    )
                )
                copies.append(
                    pltpu.make_async_copy(
                        ins[k].at[rows, pl.ds(OUT_F, OUT_B)],
                        out_b.at[tab[base + 10 + n + owner], :, pl.ds(2 * KV_LOC, OUT_B)],
                        sems.at[2 * (k * owners + h) + 1],
                    )
                )
        for c in copies:
            c.start()
        wait_all(copies)

    return pl.pallas_call(
        kernel,
        out_shape=(
            jax.ShapeDtypeStruct(part_f.shape, BF),
            jax.ShapeDtypeStruct(part_b.shape, BF),
        ),
        in_specs=[SMEM] + [VM] * MEMBERS + [ANY, ANY],
        out_specs=(ANY, ANY),
        input_output_aliases={1 + MEMBERS: 0, 2 + MEMBERS: 1},
        scratch_shapes=[pltpu.SemaphoreType.DMA((2 * n,))],
        cost_estimate=cost(0, 3 << 20),
        name="pack_out_grads",
    )(table, *pieces, part_f, part_b)


def place_attention(places, shares):
    rows, width = shares[0].shape

    def kernel(*refs):
        tab = refs[0]
        ins = refs[1 : 1 + MEMBERS]
        gq, gk, gv, go, hold = refs[1 + MEMBERS :]
        for k in range(MEMBERS):
            hold[tab[k]] = ins[k][...].astype(F32)
        at = Q_LOC + OUT_F
        for j in range(MEMBERS):
            gq[:, j * Q_LOC : (j + 1) * Q_LOC] = hold[j, :, :Q_LOC]
            gk[:, j * KV_LOC : (j + 1) * KV_LOC] = hold[j, :, at : at + KV_LOC]
            gv[:, j * KV_LOC : (j + 1) * KV_LOC] = hold[j, :, at + KV_LOC : at + 2 * KV_LOC]
            go[:, j * Q_LOC : j * Q_LOC + OUT_F] = hold[j, :, Q_LOC:at]
            go[:, j * Q_LOC + OUT_F : (j + 1) * Q_LOC] = hold[j, :, at + 2 * KV_LOC :]

    return pl.pallas_call(
        kernel,
        out_shape=tuple(
            jax.ShapeDtypeStruct((rows, MEMBERS * size), F32)
            for size in (Q_LOC, KV_LOC, KV_LOC, Q_LOC)
        ),
        in_specs=[SMEM] + [VM] * MEMBERS,
        out_specs=(VM,) * 4,
        scratch_shapes=[pltpu.VMEM((MEMBERS, rows, width), F32)],
        cost_estimate=cost(0, 6 * MEMBERS * rows * width),
        name="place_attention",
    )(places, *shares)


def expert_kernel(table, base, slot, count, pieces, rows_b, rows_d, router, width, hidden, groups, ringed, offsets):
    many = len(pieces)
    n = many // 2
    half = 3 * hidden // 2
    nt = PAIR_TOK // KEYROWS
    tiles = PAIR_TOK // TILE
    per = TILE // KEYROWS
    step = TILE
    chunk = width // groups
    owners = step // chunk
    cuts = width // step
    wide = width + LANE

    def kernel(*refs):
        tab = refs[0]
        w_refs = refs[1 : 1 + many]
        b_refs = refs[1 + many : 5 + many]
        d_refs = refs[5 + many : 9 + many]
        r_ref = refs[9 + many]
        db, out = refs[10 + many : 12 + many]
        grads = refs[12 + many : 14 + many] if ringed else refs[12 + many : 13 + many]
        scratch = refs[14 + many :] if ringed else refs[13 + many :]
        w_v, b_v, d_v, dgu_v, gh_v, db_v, out_v, sem_w, sem_b, sem_d = scratch[:10]
        i = pl.program_id(0)

        def fetch(e):
            if many == 1:
                cols = pl.ds(e * 3 * hidden, 3 * hidden)
                return [pltpu.make_async_copy(w_refs[0].at[:, cols], w_v.at[e], sem_w.at[e])]
            copies = []
            for at in range(many):
                side = at // n
                rows = w_refs[at].shape[0]
                copies.append(
                    pltpu.make_async_copy(
                        w_refs[at].at[:, pl.ds(offsets[side] + e * half, half)],
                        w_v.at[
                            e,
                            pl.ds(pl.multiple_of(tab[at], 16), rows),
                            pl.ds(side * half, half),
                        ],
                        sem_w.at[e * many + at],
                    )
                )
            return copies

        @pl.when(i == 0)
        def _():
            cb = start_rows(b_refs, b_v, tab, base, sem_b)
            for e in range(count):
                for c in fetch(e):
                    c.start()
            cd = start_rows(d_refs, d_v, tab, base, sem_d)
            wait_all(cb)
            wait_all(cd)

        @pl.when(i < tiles)
        def _():
            at = pl.ds(i * per, per)
            b = b_v[at].reshape(TILE, width)
            mark = d_v[at, :, width:].reshape(TILE, LANE).astype(F32)
            lanes = lax.broadcasted_iota(jnp.int32, (TILE, LANE), 1)
            logits = jnp.where(mark > 0.0, dot(b, r_ref[...]), NEG)
            top = jnp.max(logits, axis=1, keepdims=True)
            weight = jnp.where(mark > 0.0, jnp.exp(logits - top), 0.0)
            gates = weight / jnp.sum(weight, axis=1, keepdims=True)
            rows = pl.ds(pl.multiple_of(i * TILE, TILE), TILE)

            def one(e, extra):
                for c in range(count):

                    @pl.when((i == 0) & (e == c))
                    def _(c=c):
                        wait_all(fetch(c))

                expert = tab[base + 9] + slot + e
                b = b_v[at].reshape(TILE, width)
                dy = d_v[at, :, :width].reshape(TILE, width)
                gate = jnp.sum(jnp.where(lanes == expert, gates, 0.0), axis=1, keepdims=True)
                gu = dot(b, w_v[e, :, : 2 * hidden])
                back = dot(dy, w_v[e, :, 2 * hidden :])
                g = gu[:, :hidden]
                u = gu[:, hidden:]
                sig = 1.0 / (1.0 + jnp.exp(-g))
                act = g * sig
                hb = (act * u).astype(BF)
                hf = hb.astype(F32)
                dgate = jnp.sum(hf * back, axis=1, keepdims=True)
                gh = (hf * gate).astype(BF)
                dh = back * gate
                dg = dh * u * (sig * (1.0 + g * (1.0 - sig)))
                dgu = jnp.concatenate([dg, dh * act], 1).astype(BF)
                dgu_v[e, rows, :] = dgu
                gh_v[e, rows, :] = gh
                y = dot_nt(dgu, w_v[e, :, : 2 * hidden])
                z = dot_nt(gh, w_v[e, :, 2 * hidden :])

                @pl.when(e == 0)
                def _():
                    db_v[...] = y
                    out_v[...] = z

                @pl.when(e > 0)
                def _():
                    db_v[...] += y
                    out_v[...] += z

                high = dgate.astype(BF).astype(F32)
                low = dgate - high
                return extra + jnp.where(
                    lanes == expert, high, jnp.where(lanes == expert + LANE // 2, low, 0.0)
                )

            extra = lax.fori_loop(0, count, one, jnp.zeros((TILE, LANE), F32))
            whole = slice(None)
            store_members(db, tab, base, whole, db_v[...].astype(BF), pl.ds(0, width))
            store_members(db, tab, base, whole, extra.astype(BF), pl.ds(width, LANE))
            store_members(out, tab, base, whole, out_v[...].astype(BF))

        @pl.when(i >= tiles)
        def _():
            cols = pl.ds(pl.multiple_of((i - tiles) * step, step), step)
            b = b_v[:, :, cols].reshape(PAIR_TOK, step)
            dy = d_v[:, :, cols].reshape(PAIR_TOK, step)
            if not ringed:
                grads[0][:, : 2 * hidden] = dot_tn(b, dgu_v[0]).astype(BF)
                grads[0][:, 2 * hidden :] = dot_tn(dy, gh_v[0]).astype(BF)
            else:
                g_v, sem_g = scratch[10:]
                j = i - tiles
                for e in range(count):
                    one = dot_tn(b, dgu_v[e]).astype(BF)
                    g_v[0, j, :, e * half : (e + 1) * half] = one[:, :half]
                    g_v[1, j, :, e * half : e * half + 2 * hidden - half] = one[:, half:]
                    two = dot_tn(dy, gh_v[e]).astype(BF)
                    g_v[1, j, :, e * half + 2 * hidden - half : (e + 1) * half] = two

                def send(j, h, side):
                    owner = j * owners + h
                    return pltpu.make_async_copy(
                        g_v.at[side, j, pl.ds(h * chunk, chunk)],
                        grads[side].at[tab[base + 10 + side * groups + owner]],
                        sem_g.at[side * groups + owner],
                    )

                for h in range(owners):
                    for side in range(2):
                        send(j, h, side).start()

                @pl.when(j == cuts - 1)
                def _():
                    for t in range(cuts):
                        for h in range(owners):
                            for side in range(2):
                                send(t, h, side).wait()

    if ringed:
        grad_specs = (ANY, ANY)
        grad_shapes = (jax.ShapeDtypeStruct((groups, chunk, count * half), BF),) * 2
        more = [
            pltpu.VMEM((2, cuts, step, count * half), BF),
            pltpu.SemaphoreType.DMA((2 * groups,)),
        ]
    else:
        grad_specs = (
            pl.BlockSpec((step, 3 * hidden), lambda i: (jnp.maximum(i - tiles, 0), 0)),
        )
        grad_shapes = (jax.ShapeDtypeStruct((width, 3 * hidden), BF),)
        more = []
    return pl.pallas_call(
        kernel,
        grid=(tiles + cuts,),
        out_shape=(
            jax.ShapeDtypeStruct((MEMBERS, nt, 32, wide), BF),
            jax.ShapeDtypeStruct((MEMBERS, nt, 32, width), BF),
        )
        + grad_shapes,
        in_specs=[SMEM] + [ANY] * (many + 8) + [pl.BlockSpec((width, LANE), lambda i: (0, 0))],
        out_specs=(
            pl.BlockSpec(
                (MEMBERS, per, 32, wide), lambda i: (0, jnp.minimum(i, tiles - 1), 0, 0)
            ),
            pl.BlockSpec(
                (MEMBERS, per, 32, width), lambda i: (0, jnp.minimum(i, tiles - 1), 0, 0)
            ),
        )
        + grad_specs,
        scratch_shapes=[
            pltpu.VMEM((count, width, 3 * hidden), BF),
            pltpu.VMEM((nt, KEYROWS, width), BF),
            pltpu.VMEM((nt, KEYROWS, wide), BF),
            pltpu.VMEM((count, PAIR_TOK, 2 * hidden), BF),
            pltpu.VMEM((count, PAIR_TOK, hidden), BF),
            pltpu.VMEM((TILE, width), F32),
            pltpu.VMEM((TILE, width), F32),
            pltpu.SemaphoreType.DMA((count * many,)),
            pltpu.SemaphoreType.DMA((4,)),
            pltpu.SemaphoreType.DMA((4,)),
        ]
        + more,
        compiler_params=params(58),
        cost_estimate=cost(17 * 10**9 * count, (12 + 14 * count) << 20, 10**6 * count),
        name="expert",
    )(table, *pieces, *rows_b, *rows_d, router)


def turn_out_weight(places, af, ab):
    n = len(af)
    rows = af[0].shape[0]

    def kernel(*refs):
        tab = refs[0]
        f_refs = refs[1 : 1 + n]
        b_refs = refs[1 + n : 1 + 2 * n]
        out, sems = refs[1 + 2 * n :]
        copies = []
        for s in range(n):
            at = pl.ds(pl.multiple_of(tab[n + s], 16), rows)
            copies.append(
                pltpu.make_async_copy(
                    f_refs[s].at[:, pl.ds(Q_LOC, OUT_F)],
                    out.at[tab[s], at, pl.ds(0, OUT_F)],
                    sems.at[s],
                )
            )
            at = pl.ds(pl.multiple_of(tab[3 * n + s], 16), rows)
            copies.append(
                pltpu.make_async_copy(
                    b_refs[s].at[:, pl.ds(2 * KV_LOC, OUT_B)],
                    out.at[tab[2 * n + s], at, pl.ds(OUT_F, OUT_B)],
                    sems.at[n + s],
                )
            )
        for c in copies:
            c.start()
        wait_all(copies)

    return pl.pallas_call(
        kernel,
        out_shape=jax.ShapeDtypeStruct((MEMBERS, Q_LOC, Q_LOC), BF),
        in_specs=[SMEM] + [ANY] * (2 * n),
        out_specs=VM,
        scratch_shapes=[pltpu.SemaphoreType.DMA((2 * n,))],
        cost_estimate=cost(0, 3 << 20),
        name="turn_out_weight",
    )(places, *af, *ab)


def ring_place(index, n):
    return jnp.where(index % 2 == 0, index // 2, n - 1 - index // 2)


def ring_index(place, n):
    return jnp.where(place < n // 2, 2 * place, 2 * (n - 1 - place) + 1)


def ring_pairs(n):
    ring = list(range(0, n, 2)) + list(range(n - 1, 0, -2))
    ahead = [(ring[i], ring[(i + 1) % n]) for i in range(n)]
    back = [(b, a) for a, b in ahead]
    return ahead, back


def after(value, *deps):
    return lax.optimization_barrier((value,) + deps)[0]


def swap(values, bits):
    return lax.ppermute(values, "seq", [(i, i ^ bits) for i in range(MEMBERS)])


def share_rows(values):
    across = swap(values, 2)
    return [values, swap(values, 1), across, swap(across, 1)]


def body(
    tokens,
    cotangent,
    routes,
    lengths,
    deal_order,
    attn_gain,
    query_weight,
    key_matrix,
    value_matrix,
    out_weight,
    moe_gain,
    router_weight,
    expert_weight,
):
    n = lax.axis_size("dp")
    group = lax.axis_index("dp")
    member = lax.axis_index("seq")
    slots, block, width = tokens.shape
    units = PAIR_TOK // (MEMBERS * block)
    local_rows = query_weight.shape[0]
    n_expert = router_weight.shape[1]
    hidden = expert_weight.shape[2] // 3
    per = n_expert // MEMBERS
    ahead, back = ring_pairs(n)
    natural = block == 32

    place = ring_place(group, n)
    steps = jnp.arange(n, dtype=jnp.int32)
    from_f = ring_index((place - steps) % n, n).astype(jnp.int32)
    from_b = ring_index((place + steps) % n, n).astype(jnp.int32)
    xors = jnp.bitwise_xor(jnp.arange(MEMBERS, dtype=jnp.int32), member)
    row_place = xors if natural else jnp.arange(MEMBERS, dtype=jnp.int32)
    first_seq = deal_order[2 * group]
    first_len = lengths[first_seq]
    first = (first_len // (MEMBERS * block)).reshape(1)
    base = 2 * n
    table = jnp.concatenate(
        [
            from_f * local_rows,
            from_b * local_rows,
            row_place,
            xors,
            jnp.stack([first_len, per * member]),
            (place - ring_place(steps, n)) % n,
            (ring_place(steps, n) - place) % n,
        ]
    ).astype(jnp.int32)
    share = n // MEMBERS
    out_places = jnp.concatenate(
        [
            jnp.bitwise_xor(from_f // share, member),
            from_f % share * local_rows,
            jnp.bitwise_xor(from_b // share, member),
            from_b % share * local_rows,
        ]
    ).astype(jnp.int32)

    sent_x = pick_rows(tokens, deal_order)
    dealt_x = lax.all_to_all(sent_x, "dp", split_axis=0, concat_axis=0, tiled=True)
    x_rows = take_rows(dealt_x, first, units)

    def cut(values, size):
        return lax.dynamic_slice_in_dim(values, member * size, size, axis=1).astype(BF)

    small = jnp.concatenate(
        [
            router_weight,
            jnp.zeros((local_rows, GAINS_AT - n_expert), F32),
            attn_gain[:, None],
            moe_gain[:, None],
            jnp.zeros((local_rows, LANE - GAINS_AT - 2), F32),
        ],
        1,
    ).astype(BF)
    out_cols = cut(out_weight, Q_LOC)
    attn_f = jnp.concatenate([cut(query_weight, Q_LOC), out_cols[:, :OUT_F], small], 1)
    attn_b = jnp.concatenate(
        [cut(key_matrix, KV_LOC), cut(value_matrix, KV_LOC), out_cols[:, OUT_F:]], 1
    )
    expert_first = expert_weight.transpose(1, 0, 2)
    expert_own = lax.dynamic_slice_in_dim(expert_first, per * member, per, axis=0).astype(BF)

    def rows_of(chunks):
        if natural:
            return chunks
        w = chunks[0].shape[2]
        whole = jnp.zeros((units, MEMBERS, block, w), BF)
        for k in range(MEMBERS):
            whole = lax.dynamic_update_slice(whole, chunks[k][:, None], (0, xors[k], 0, 0))
        whole = whole.reshape(PAIR_TOK // KEYROWS, MEMBERS, 32, w)
        return [whole[:, j] for j in range(MEMBERS)]

    def scatter_parts(parts):
        if natural:
            shaped = parts
        else:
            shaped = []
            for p in parts:
                rows = p.transpose(1, 0, 2, 3).reshape(units, MEMBERS, block, p.shape[3])
                shaped.append(
                    [
                        lax.dynamic_index_in_dim(rows, xors[k], axis=1, keepdims=False)
                        for k in range(MEMBERS)
                    ]
                )

        def part(k):
            total = None
            for p in shaped:
                one = p[k].astype(F32)
                total = one if total is None else total + one
            return total

        return part

    def scatter_near(part, *deps):
        far = swap(after(part(3).astype(BF), *deps), 1)
        near = swap(after(part(1).astype(BF), *deps), 1)
        hop = (part(2) + far.astype(F32)).astype(BF)
        return near, hop

    def scatter_end(part, near, cross):
        return part(0) + near.astype(F32) + cross.astype(F32)

    class Gather:
        def __init__(self, f, b):
            self.fs, self.bs = [f], [b]

        def step(self, *deps):
            if len(self.fs) < n:
                self.fs.append(lax.ppermute(after(self.fs[-1], *deps), "dp", ahead))
                self.bs.append(lax.ppermute(after(self.bs[-1], *deps), "dp", back))

        def last(self, ago=1):
            return self.fs[-ago], self.bs[-ago]

        def finish(self):
            while len(self.fs) < n:
                self.step()

    class Scatter:
        def __init__(self, part_f, part_b):
            self.parts = part_f, part_b
            self.sums = part_f(1), part_b(1)
            self.at = 1

        def step(self, *deps):
            if self.at < n:
                f = lax.ppermute(after(self.sums[0], *deps), "dp", ahead)
                b = lax.ppermute(after(self.sums[1], *deps), "dp", back)
                self.at += 1
                own = [part(self.at % n) for part in self.parts]
                self.sums = tuple(
                    (got.astype(F32) + mine.astype(F32)).astype(BF)
                    for got, mine in zip((f, b), own)
                )

        def finish(self):
            while self.at < n:
                self.step()
            return self.sums

    half = 3 * hidden // 2
    ring = Gather(
        after(jnp.concatenate([attn_f, expert_own[0, :, :half]], 1), sent_x),
        after(jnp.concatenate([attn_b, expert_own[0, :, half:]], 1), sent_x),
    )
    offsets = (attn_f.shape[1], attn_b.shape[1])
    sent_d = pick_marked(after(cotangent, sent_x), routes, deal_order)
    ring.step()
    ring.step(sent_d)
    x_across, x_near = swap(x_rows, 2), swap(x_rows, 1)
    ring.step(x_rows)
    dealt_d = lax.all_to_all(
        after(sent_d, *ring.last(2)), "dp", split_axis=0, concat_axis=0, tiled=True
    )
    ring.finish()
    ring_fs, ring_bs = ring.fs, ring.bs
    others = per - 1
    second = Gather(
        after(jnp.concatenate([expert_own[e, :, :half] for e in range(1, per)], 1), *ring.last()),
        after(jnp.concatenate([expert_own[e, :, half:] for e in range(1, per)], 1), *ring.last()),
    )
    second.step()
    turned = turn_out_weight(out_places, ring_fs, ring_bs)
    wout = [turned[0]] + [swap(turned[k], k) for k in range(1, MEMBERS)]

    row = jnp.arange(PAIR_TOK, dtype=jnp.int32)
    pos = row - jnp.where(row >= first_len, first_len, 0)
    freq = rope_base ** (-(jnp.arange(HEAD // 2, dtype=F32) * 2.0 / HEAD))
    angle = pos.astype(F32)[:, None] * freq[None, :]
    cosine = jnp.concatenate([jnp.cos(angle)] * 4, 1)
    sine = jnp.sin(angle)
    sine = jnp.concatenate([-sine, sine, -sine, sine], 1)

    rows_x = [after(x_rows, turned), x_near, x_across, swap(x_across, 1)]
    a_all, q, k, v, heads, router, gains = attention_forward(
        table, base, ring_fs, ring_bs, rows_of(rows_x), cosine, sine, width
    )
    second.step(heads)
    d_rows = take_rows(dealt_d, first, units)
    part = project_out(table, base, after(heads, d_rows, *second.last(2)), wout, width)
    gain_a = gains[0:1]
    gain_m = gains[1:2]
    mix = scatter_parts([part])
    mix_near, mix_hop = scatter_near(mix)
    mix_cross = swap(mix_hop, 2)
    second.step(mix_hop)
    middle = after(x_rows, *second.last(2)).astype(F32) + scatter_end(mix, mix_near, mix_cross)

    inverse = lax.rsqrt(jnp.mean(middle * middle, axis=-1, keepdims=True) + eps_norm)
    b_rows = (middle * inverse * gain_m).astype(BF)
    b_across, b_near = swap(b_rows, 2), swap(b_rows, 1)
    second.step(b_rows)
    d_own_rows = after(d_rows, b_rows, *second.last(2))
    d_across, d_near = swap(d_own_rows, 2), swap(d_own_rows, 1)
    second.step(b_across)
    second.finish()
    rows_b = rows_of([b_rows, b_near, b_across, swap(b_across, 1)])
    rows_d = rows_of([d_rows, d_near, d_across, swap(d_across, 1)])

    db, out, grad = expert_kernel(
        table,
        base,
        0,
        1,
        ring_fs + ring_bs,
        rows_b,
        rows_d,
        router,
        width,
        hidden,
        n,
        False,
        offsets,
    )
    dbs, outs = [db], [out]
    first_share = lax.psum_scatter(grad, "dp", scatter_dimension=0, tiled=True)
    db, out, grad_f, grad_b = expert_kernel(
        after(table, dbs[0]),
        base,
        1,
        others,
        second.fs + second.bs,
        rows_b,
        rows_d,
        router,
        width,
        hidden,
        n,
        True,
        (0, 0),
    )
    dbs.append(db)
    outs.append(out)
    shed = Scatter(lambda s: grad_f[s], lambda s: grad_b[s])
    shed.step()

    own_b = b_rows.reshape(units * block, width)
    mark = d_rows[:, :, width:].reshape(units * block, LANE).astype(F32)
    logits = dot(own_b, router)
    gates = jax.nn.softmax(jnp.where(mark > 0.0, logits, -jnp.inf), axis=-1)

    back_part = scatter_parts(dbs)
    back_near, back_hop = scatter_near(back_part)
    back_cross = swap(back_hop, 2)
    shed.step(back_hop)
    back_sum = scatter_end(back_part, back_near, back_cross).reshape(units * block, width + LANE)
    extra = back_sum[:, width:]
    dgate = extra + jnp.roll(extra, -(LANE // 2), axis=1)
    dgate = jnp.where(mark > 0.0, dgate, 0.0)
    dlogits = (gates * (dgate - jnp.sum(gates * dgate, axis=-1, keepdims=True))).astype(BF)
    db_own = back_sum[:, :width] + dot_nt(dlogits, router)
    mid_own = middle.reshape(units * block, width)
    inv_own = inverse.reshape(units * block, 1)
    d_own = d_rows[:, :, :width].reshape(units * block, width).astype(F32)
    normed = mid_own * inv_own
    scaled = db_own * gain_m
    dmiddle = d_own + inv_own * (
        scaled - normed * jnp.mean(scaled * normed, axis=-1, keepdims=True)
    )
    dmix = jnp.concatenate([dmiddle.astype(BF), dlogits], 1).reshape(units, block, width + LANE)
    m_across, m_near = swap(dmix, 2), swap(dmix, 1)
    shed.step(dmix)
    out_part = scatter_parts(outs)
    out_near, out_hop = scatter_near(out_part, dmix)
    m_far = swap(m_across, 1)
    out_cross = swap(after(out_hop, m_across), 2)
    shed.step(m_across)
    result = middle + scatter_end(out_part, out_near, out_cross)
    sent_out = spread_rows(result.astype(BF), first, slots)
    back_out = lax.all_to_all(sent_out, "dp", split_axis=0, concat_axis=0, tiled=True)
    rows_m = rows_of([after(dmix, sent_out, first_share, *shed.sums), m_near, m_across, m_far])
    first_shares = share_rows(first_share)

    da, dqkv = attention_backward(
        table, base, ring_fs, ring_bs, rows_m, wout, q, k, v, cosine, sine, width
    )
    shed.step(da)
    da_part = scatter_parts([da])
    da_near, da_hop = scatter_near(da_part, back_out)
    da_cross = swap(da_hop, 2)
    half_f, half_b, gout = attention_grads(
        table, base, a_all, rows_b, rows_m, after(heads, da_hop), dqkv, width, n
    )
    gout = after(gout, da_cross)
    pieces = [gout[0]] + [swap(gout[kk], kk) for kk in range(1, MEMBERS)]
    full_f, full_b = pack_out_grads(table, base, pieces, half_f, half_b)
    da_own = scatter_end(da_part, da_near, da_cross).reshape(units * block, width)
    x_own = x_rows.reshape(units * block, width).astype(F32)
    inv_x = lax.rsqrt(jnp.mean(x_own * x_own, axis=-1, keepdims=True) + eps_norm)
    normed_x = x_own * inv_x
    scaled_x = da_own * gain_a
    grad_x = dmiddle + inv_x * (
        scaled_x - normed_x * jnp.mean(scaled_x * normed_x, axis=-1, keepdims=True)
    )

    sent_grad = spread_rows(grad_x.reshape(units, block, width).astype(BF), first, slots)
    back_grad = lax.all_to_all(sent_grad, "dp", split_axis=0, concat_axis=0, tiled=True)
    output = place_rows(after(back_out, sent_grad), deal_order)
    grad_tokens = place_rows(back_grad, deal_order)

    pair_f, pair_b = shed.finish()
    pair_share = jnp.concatenate([pair_f, pair_b], 1)
    pair_shares = share_rows(pair_share)
    grad_first, gain_first = place_experts(
        xors, first_shares, expert_first, 0, 1, False, per, None
    )
    grad_first, gain_rest = place_experts(
        xors, pair_shares, expert_first, 1, others, True, per, grad_first
    )
    full_f = after(full_f, pair_f, sent_grad)
    full_b = after(full_b, pair_b, sent_grad)
    final = Scatter(lambda s: full_f[s], lambda s: full_b[s])
    final.step()
    final.step(output)
    final.step()
    final.step()
    final.step(gain_rest)
    final.step(grad_tokens)
    share_f, share_b = final.finish()
    small_grad = share_b[:, full_b.shape[2] - LANE :]
    shares = share_rows(jnp.concatenate([share_f, share_b[:, : full_b.shape[2] - LANE]], 1))

    grad_query, grad_key, grad_value, grad_out = place_attention(xors, shares)
    grad_router = small_grad[:, :n_expert].astype(F32)
    grad_experts = grad_first.transpose(1, 0, 2)

    def low(values):
        return values.astype(BF).astype(F32)

    grad_attn_gain = (
        jnp.sum(low(query_weight) * grad_query, axis=1)
        + jnp.sum(low(key_matrix) * grad_key, axis=1)
        + jnp.sum(low(value_matrix) * grad_value, axis=1)
    ) / low(attn_gain)
    grad_moe_gain = (
        jnp.sum(gain_first + gain_rest, axis=1)
        + jnp.sum(low(router_weight) * grad_router, axis=1)
    ) / low(moe_gain)

    return (
        output,
        grad_tokens,
        grad_attn_gain,
        grad_query,
        grad_key,
        grad_value,
        grad_out,
        grad_moe_gain,
        grad_router,
        grad_experts,
    )


def solution(mesh):
    rows = P(None, ("dp", "seq"), None)
    placed = (
        rows,
        rows,
        rows,
        P(),
        P(),
        P("dp"),
        P("dp", None),
        P("dp", None),
        P("dp", None),
        P("dp", None),
        P("dp"),
        P("dp", None),
        P("dp", None, None),
    )
    return jax.shard_map(
        body,
        mesh=mesh,
        in_specs=placed,
        out_specs=(
            rows,
            rows,
            P("dp"),
            P("dp", None),
            P("dp", None),
            P("dp", None),
            P("dp", None),
            P("dp"),
            P("dp", None),
            P("dp", None, None),
        ),
        check_vma=False,
    )
```

time: 1000 us -> 760 us (0.76)
  Pallas kernels: 294 us -> 211 us
  local copies, waits for them, and re-layouts: 91.3 us -> 34.8 us
  between operations: 63.7 us -> 20.4 us
  starting transfers between devices: 232 us -> 194 us
    ppermute x119 -> x56, starting transfers between devices: 136 us -> 83.1 us  [the longest x14 41.4 us: step(): self.fs.append(lax.ppermute(after(self.fs[-1], *deps), 'dp', ahead))]
    unnamed x363 -> x201, local copies, waits for them, and re-layouts: 54.7 us -> 13.3 us
    pallas_call x1, Pallas kernels: 37.7 us -> 3.2 us  [turn_out_weight(): pl.pallas_call(kernel, out_shape=jax.ShapeDtypeStruct((MEMBERS, Q_LOC, Q_...]
    slice x23 -> x3, local copies, waits for them, and re-layouts: 17.6 us -> 0.05 us  [the longest x1 0.03 us: body(): gain_a = gains[0:1]]
    pallas_call x2, Pallas kernels: 20.4 us -> 6.43 us  [place_rows(): pl.pallas_call(kernel, out_shape=jax.ShapeDtypeStruct(values.shape, F32),...]
    pallas_call x2, Pallas kernels: 18.3 us -> 5.2 us  [spread_rows(): pl.pallas_call(kernel, out_shape=jax.ShapeDtypeStruct((slots, block, widt...]
    all_to_all x3, waiting for transfers between devices: 10.6 us -> 0.01 us  [the longest x1 0.01 us: body(): lax.all_to_all(after(sent_d, *ring.last(2)), 'dp', split_axis=0, concat_a...]
    all_to_all x3, starting transfers between devices: 13.4 us -> 23.4 us  [the longest x1 13.7 us: body(): lax.all_to_all(sent_out, 'dp', split_axis=0, concat_axis=0, tiled=True)]
  transfers between devices with their start and end apart: 177 -> 100, of which waited for: 51 -> 39; matrix products, arithmetic and copies ran while one was open for 16% -> 13% of each run, Pallas kernels for 25% -> 27%
where the time goes in v2:
time: 760 us; the launch traced here: 754 us
  waiting for transfers between devices  217 us (29%)
  Pallas kernels  211 us (28%)
  starting transfers between devices  194 us (26%)
  other arithmetic  75.2 us (10%)
  local copies, waits for them, and re-layouts  34.8 us (5%)
  between operations  20.4 us (3%)
    ppermute x14, waiting for transfers between devices, step(): self.fs.append(lax.ppermute(after(self.fs[-1], *deps), 'dp', ahead))  111 us
    pallas_call x2, Pallas kernels, expert_kernel(): pl.pallas_call(kernel, grid=(tiles + cuts,), out_shape=(jax.ShapeDtypeStr...  86.8 us
    ppermute x39, starting transfers between devices, swap(): return lax.ppermute(values, 'seq', [(i, i ^ bits) for i in range(MEMBERS)])  81.1 us
    ppermute x39, waiting for transfers between devices, swap(): return lax.ppermute(values, 'seq', [(i, i ^ bits) for i in range(MEMBERS)])  46 us
    ppermute x14, starting transfers between devices, step(): self.fs.append(lax.ppermute(after(self.fs[-1], *deps), 'dp', ahead))  41.4 us
    pallas_call x1, Pallas kernels, attention_backward(): pl.pallas_call(kernel, out_shape=(jax.ShapeDtypeStruct((MEMBERS, nt, 32,...  39.3 us
    convert_element_type x28, other arithmetic, step(): (got.astype(F32) + mine.astype(F32)).astype(BF)  34.1 us
    ppermute x14, waiting for transfers between devices, step(): f = lax.ppermute(after(self.sums[0], *deps), 'dp', ahead)  27.2 us
  transfers between devices with their start and end apart: 100, of which 39 were waited for; matrix products, arithmetic and copies ran while one was open for 13% of the time, Pallas kernels for 27%

profile of v2, /device:TPU:1, one launch (start us, length us, event | category | flops | bytes accessed | tf_op | source)
XLA Modules:
  0.0 753.6 jit_solution(18078167029287743170)
XLA Ops:
  7.2 3.4 pick.1
  10.6 6.5 all-to-all-start
  25.8 4.2 pick_marked.1
  30.1 24.3 %collective-permute-done.refs_2_ = bf16[192,1408]{1,0:T(8,128)(2,1)S(1)} collective-permute-done((bf16[192,1408]{1,0:T(8,128)(2,1)S(1)}, bf16[192,1408]{1,0:T(8,128)(2,1)S(1)}, u32[]{:S(2)}, u32[]{:S(2)}) %collective-permute-start) | collective-permute-done | bytes 540704 | tf_op jit(solution)/shard_map/ppermute | solution.py:1155
  54.4 10.8 %collective-permute-start.1 = (bf16[192,1408]{1,0:T(8,128)(2,1)S(1)}, bf16[192,1408]{1,0:T(8,128)(2,1)S(1)}, u32[]{:S(2)}, u32[]{:S(2)}) collective-permute-start(bf16[192,1408]{1,0:T(8,128)(2,1)S(1)} %collective-permute-done.refs_2_), channel_id=1, source_target_pairs={{0,8},{8,16},{16,24},{24,28},{28,20},{20,12},{12,4},{4,0},{1,9},{9... | collective-permute-start | bytes 1622024 | tf_op jit(solution)/shard_map/ppermute | solution.py:1155
  78.6 4.7 all-to-all-start.1
  83.3 5.5 collective-permute-done.2.refs_4_
  91.5 36.3 %collective-permute-done.3.refs_5_ = bf16[192,1408]{1,0:T(8,128)(2,1)} collective-permute-done((bf16[192,1408]{1,0:T(8,128)(2,1)S(1)}, bf16[192,1408]{1,0:T(8,128)(2,1)}, u32[]{:S(2)}, u32[]{:S(2)}) %collective-permute-start.3) | collective-permute-done | bytes 540704 | tf_op jit(solution)/shard_map/ppermute | solution.py:1155
  127.8 11.3 %collective-permute-start.4 = (bf16[192,1408]{1,0:T(8,128)(2,1)}, bf16[192,1408]{1,0:T(8,128)(2,1)}, u32[]{:S(2)}, u32[]{:S(2)}) collective-permute-start(bf16[192,1408]{1,0:T(8,128)(2,1)} %collective-permute-done.3.refs_5_), channel_id=1, source_target_pairs={{0,8},{8,16},{16,24},{24,28},{28,20},{20,12},{12,4},{4,0},{1,9},{9... | collective-permute-start | bytes 1622024 | tf_op jit(solution)/shard_map/ppermute | solution.py:1155
  141.0 7.8 %collective-permute-done.4.refs_6_ = bf16[192,1408]{1,0:T(8,128)(2,1)} collective-permute-done((bf16[192,1408]{1,0:T(8,128)(2,1)}, bf16[192,1408]{1,0:T(8,128)(2,1)}, u32[]{:S(2)}, u32[]{:S(2)}) %collective-permute-start.4) | collective-permute-done | bytes 540704 | tf_op jit(solution)/shard_map/ppermute | solution.py:1155
  154.2 3.5 collective-permute-start.15
  158.1 3.5 collective-permute-start.17
  167.9 6.5 collective-permute-done.13.refs_16_
  181.7 4.3 collective-permute-start.21
  198.2 23.8 %attention_forward.1 = (bf16[9,128,1536]{2,1,0:T(8,128)(2,1)}, bf16[2,9,384,64]{3,2,1,0:T(8,128)(2,1)}, bf16[2,1152,64]{2,1,0:T(8,128)(2,1)}, bf16[2,1152,64]{2,...) custom-call(s32[42]{0:T(128)S(1)} %concatenate.43.refs_0_.tab, ...), custom_call_target="tpu_custom_call" | custom-call | flops 120000000 | bytes 146800 | tf_op jit(solution)/shard_map/attention_forward/pallas_call | solution.py:423
  223.3 4.2 project_out.1
  233.1 13.2 %collective-permute-done.18.refs_3_ = bf16[192,1536]{1,0:T(8,128)(2,1)S(1)} collective-permute-done((bf16[192,1536]{1,0:T(8,128)(2,1)}, bf16[192,1536]{1,0:T(8,128)(2,1)S(1)}, u32[]{:S(2)}, u32[]{:S(2)}) %collective-permute-start.18) | collective-permute-done | bytes 589856 | tf_op jit(solution)/shard_map/ppermute | solution.py:1155
  255.9 4.6 collective-permute-done.30.refs_4_
  262.3 10.6 %collective-permute-done.35.refs_5_ = bf16[192,1536]{1,0:T(8,128)(2,1)S(1)} collective-permute-done((bf16[192,1536]{1,0:T(8,128)(2,1)S(1)}, bf16[192,1536]{1,0:T(8,128)(2,1)S(1)}, u32[]{:S(2)}, u32[]{:S(2)}) %collective-permute-start.35) | collective-permute-done | bytes 589856 | tf_op jit(solution)/shard_map/ppermute | solution.py:1155
  276.6 3.9 collective-permute-start.27
  280.6 5.9 collective-permute-done.36.refs_6_
  287.9 6.0 collective-permute-start.32
  299.7 3.8 collective-permute-start.29
  310.6 31.1 %expert.2 = (bf16[4,9,32,1664]{3,2,1,0:T(8,128)(2,1)}, bf16[4,9,32,1536]{3,2,1,0:T(8,128)(2,1)}, bf16[1536,1536]{1,0:T(8,128)(2,1)}) custom-call(s32[42]{0:T(128)} %copy-done.38, bf16[192,1408]{1,0:T(8,128)(2,1)} %copy-done.2, bf16[192,1408]{1,0:T(8,128)(2,1)} %copy-done.6, bf16[192,1408]{1,0:T(8,128)(2,1)} %copy-done.8, bf16[192,1408]{1,0:T(8,128)(2,1)} %copy-done.43, ...), custom_call_target="tpu_custom_call" | custom-call | flops 170000000 | bytes 272629 | tf_op jit(solution)/shard_map/expert/pallas_call | solution.py:917
  341.8 55.7 %expert.3 = (bf16[4,9,32,1664]{3,2,1,0:T(8,128)(2,1)}, bf16[4,9,32,1536]{3,2,1,0:T(8,128)(2,1)}, bf16[8,192,1536]{2,1,0:T(8,128)(2,1)}, bf16[8,192,1536]{2,1,0:T(8,128)(2,1)}) custom-call(s32[42]{0:T(128)} %copy-done.38, bf16[192,1536]{1,0:T(8,128)(2,1)} %get-tuple-element.94.refs_1_, bf16[192,1536]{1,0:T(8,128)(2,1)} %collective-permute-done.14.refs_2_, ...), custom_call_target="tpu_custom_call" | custom-call | flops 340000000 | bytes 419430 | tf_op jit(solution)/shard_map/expert/pallas_call | solution.py:917
  409.1 6.9 collective-permute-done.50
  420.3 9.2 %collective-permute-done.45 = bf16[9,32,1664]{2,1,0:T(8,128)(2,1)S(1)} collective-permute-done((bf16[9,32,1664]{2,1,0:T(8,128)(2,1)S(1)}, bf16[9,32,1664]{2,1,0:T(8,128)(2,1)S(1)}, u32[]{:S(2)}, u32[]{:S(2)}) %collective-permute-start.45) | collective-permute-done | bytes 958496 | tf_op jit(solution)/shard_map/ppermute | solution.py:1016
  437.8 5.9 collective-permute-done.51
  445.2 4.8 collective-permute-start.52
  455.1 7.9 %collective-permute-done.48.refs_19_.refs_7_ = bf16[9,32,1664]{2,1,0:T(8,128)(2,1)S(1)} collective-permute-done((bf16[9,32,1664]{2,1,0:T(8,128)(2,1)S(1)}, bf16[9,32,1664]{2,1,0:T(8,128)(2,1)S(1)}, u32[]{:S(2)}, u32[]{:S(2)}) %collective-permute-start.48) | collective-permute-done | bytes 958496 | tf_op jit(solution)/shard_map/ppermute | solution.py:1016
  465.2 3.4 collective-permute-done.56
  470.6 3.9 collective-permute-start.53
  485.4 13.7 %all-to-all-start.2 = ((bf16[16,32,1536]{2,1,0:T(8,128)(2,1)}), bf16[16,32,1536]{2,1,0:T(8,128)(2,1)S(1)}, u32[]{:S(2)}, u32[]{:S(2)}) async-start(bf16[16,32,1536]{2,1,0:T(8,128)(2,1)} %spread_rows.2), calls=%async_computation.2 | async-start | bytes 3145728 | tf_op jit(solution)/shard_map/all_to_all | solution.py:1316
  503.5 39.3 %attention_backward.1 = (bf16[4,9,32,1536]{3,2,1,0:T(8,128)(2,1)}, bf16[1152,640]{1,0:T(8,128)(2,1)}) custom-call(s32[42]{0:T(128)} %copy-done.38, bf16[192,1408]{1,0:T(8,128)(2,1)} %copy-done.2, bf16[192,1408]{1,0:T(8,128)(2,1)} %copy-done.6, bf16[192,1408]{1,0:T(8,128)(2,1)} %copy-done.8, bf16[192,1408]{1,0:T(8,128)(2,1)} %copy-done.43, ...), custom_call_target="tpu_custom_call" | custom-call | flops 200000000 | bytes 167772 | tf_op jit(solution)/shard_map/attention_backward/pallas_call | solution.py:573
  545.9 9.1 %collective-permute-done.73 = bf16[192,1536]{1,0:T(8,128)(2,1)} collective-permute-done((bf16[192,1536]{1,0:T(8,128)(2,1)S(1)}, bf16[192,1536]{1,0:T(8,128)(2,1)}, u32[]{:S(2)}, u32[]{:S(2)}) %collective-permute-start.73) | collective-permute-done | bytes 589856 | tf_op jit(solution)/shard_map/ppermute | solution.py:1174
  562.5 4.4 collective-permute-start.61
  575.9 12.1 %attention_grads.1 = (bf16[8,192,512]{2,1,0:T(8,128)(2,1)}, bf16[8,192,640]{2,1,0:T(8,128)(2,1)}, bf16[4,384,384]{2,1,0:T(8,128)(2,1)}) custom-call(s32[42]{0:T(128)S(1)} %copy-done.39, bf16[9,32,1536]{2,1,0:T(8,128)(2,1)S(1)} %copy-done.1, bf16[9,32,1536]{2,1,0:T(8,128)(2,1)S(1)} %copy-done.15, bf16[9,32,1536]{2,1,0:T(8,128)(2,1)S(1)} %copy-done.13, ...), custom_call_target="tpu_custom_call" | custom-call | flops 40000000 | bytes 167772 | tf_op jit(solution)/shard_map/attention_grads/pallas_call | solution.py:638
  597.6 9.1 %collective-permute-start.63 = (bf16[384,384]{1,0:T(8,128)(2,1)}, bf16[384,384]{1,0:T(8,128)(2,1)}, u32[]{:S(2)}, u32[]{:S(2)}) collective-permute-start(bf16[384,384]{1,0:T(8,128)(2,1)} %get-tuple-element.220), channel_id=1, source_target_pairs={{0,1},{1,0},{2,3},{3,2},{4,5},{5,4},{6,7},{7,6},{8,9},{9,8},{10,11... | collective-permute-start | bytes 884744 | tf_op jit(solution)/shard_map/ppermute | solution.py:1016
  614.1 5.0 all-to-all-start.3
  620.3 4.9 collective-permute-done.64.refs_3_
  625.1 12.9 %collective-permute-done.65.refs_4_ = bf16[384,384]{1,0:T(8,128)(2,1)} collective-permute-done((bf16[384,384]{1,0:T(8,128)(2,1)}, bf16[384,384]{1,0:T(8,128)(2,1)}, u32[]{:S(2)}, u32[]{:S(2)}) %collective-permute-start.65) | collective-permute-done | bytes 294944 | tf_op jit(solution)/shard_map/ppermute | solution.py:1016
  651.4 9.9 %collective-permute-start.70 = (bf16[192,512]{1,0:T(8,128)(2,1)S(1)}, bf16[192,512]{1,0:T(8,128)(2,1)S(1)}, u32[]{:S(2)}, u32[]{:S(2)}) collective-permute-start(bf16[192,512]{1,0:T(8,128)(2,1)S(1)} %fusion.49), channel_id=1, source_target_pairs={{0,8},{8,16},{16,24},{24,28},{28,20},{20,12},{12,4},{4,0},{1,9},{9... | collective-permute-start | bytes 589832 | tf_op jit(solution)/shard_map/ppermute | solution.py:1173
  676.3 4.1 collective-permute-done.87
  682.9 4.7 place_experts.2
  688.6 7.6 %place_experts.3 = (f32[12,192,1536]{2,1,0:T(8,128)}, f32[192,128]{1,0:T(8,128)S(1)}) custom-call(s32[4]{0:T(128)S(1)} %iota_xor_fusion.refs_0_, bf16[192,3072]{1,0:T(8,128)(2,1)S(1)} %pad_maximum_fusion.refs_1_, bf16[192,3072]{1,0:T(8,128)(2,1)S(1)} %collective-permute-done.76.refs_2_, ...), custom_call_target="tpu_custom_call", output_to_operand_aliasing={{0}: (6, {})} | custom-call | bytes 141557 | tf_op jit(solution)/shard_map/place_experts/pallas_call | solution.py:246
  713.8 3.8 collective-permute-done.84
  723.0 8.3 %collective-permute-start.92 = (bf16[192,1024]{1,0:T(8,128)(2,1)S(1)}, bf16[192,1024]{1,0:T(8,128)(2,1)S(1)}, u32[]{:S(2)}, u32[]{:S(2)}) collective-permute-start(bf16[192,1024]{1,0:T(8,128)(2,1)S(1)} %pad_maximum_fusion.7.refs_1_), channel_id=1, source_target_pairs={{0,1},{1,0},{2,3},{3,2},{4,5},{5,4},{6,7},{7,6},{8,9},{9,8},{10,11... | collective-permute-start | bytes 1179656 | tf_op jit(solution)/shard_map/ppermute | solution.py:1016
  731.3 6.2 collective-permute-start.94
  (482 shorter events, 241.0 us)
Async XLA Ops:
  10.6 60.4 %all-to-all-start = ((bf16[16,32,1536]{2,1,0:T(8,128)(2,1)}), bf16[16,32,1536]{2,1,0:T(8,128)(2,1)}, u32[]{:S(2)}, u32[]{:S(2)}) async-start(bf16[16,32,1536]{2,1,0:T(8,128)(2,1)} %pick.1), calls=%async_computation | async-start | bytes 3145728 | tf_op jit(solution)/shard_map/all_to_all | solution.py:1083
  22.3 32.1 %collective-permute-start = (bf16[192,1408]{1,0:T(8,128)(2,1)S(1)}, bf16[192,1408]{1,0:T(8,128)(2,1)S(1)}, u32[]{:S(2)}, u32[]{:S(2)}) collective-permute-start(bf16[192,1408]{1,0:T(8,128)(2,1)S(1)} %concatenate.41.refs_1_), channel_id=1, source_target_pairs={{0,8},{8,16},{16,24},{24,28},{28,20},{20,12},{12,4},{4,0},{1,9},{9... | collective-permute-start | bytes 1622024 | tf_op jit(solution)/shard_map/ppermute | solution.py:1155
  24.8 40.4 %collective-permute-start.7 = (bf16[192,1280]{1,0:T(8,128)(2,1)S(1)}, bf16[192,1280]{1,0:T(8,128)(2,1)S(1)}, u32[]{:S(2)}, u32[]{:S(2)}) collective-permute-start(bf16[192,1280]{1,0:T(8,128)(2,1)S(1)} %pad_maximum_fusion.6.refs_9_), channel_id=1, source_target_pairs={{8,0},{16,8},{24,16},{28,24},{20,28},{12,20},{4,12},{0,4},{9,1},{1... | collective-permute-start | bytes 1474568 | tf_op jit(solution)/shard_map/ppermute | solution.py:1156
  54.4 21.9 %collective-permute-start.1 = (bf16[192,1408]{1,0:T(8,128)(2,1)S(1)}, bf16[192,1408]{1,0:T(8,128)(2,1)S(1)}, u32[]{:S(2)}, u32[]{:S(2)}) collective-permute-start(bf16[192,1408]{1,0:T(8,128)(2,1)S(1)} %collective-permute-done.refs_2_), channel_id=1, source_target_pairs={{0,8},{8,16},{16,24},{24,28},{28,20},{20,12},{12,4},{4,0},{1,9},{9... | collective-permute-start | bytes 1622024 | tf_op jit(solution)/shard_map/ppermute | solution.py:1155
  78.6 112.0 %all-to-all-start.1 = ((bf16[16,32,1664]{2,1,0:T(8,128)(2,1)}), bf16[16,32,1664]{2,1,0:T(8,128)(2,1)}, u32[]{:S(2)}, u32[]{:S(2)}) async-start(bf16[16,32,1664]{2,1,0:T(8,128)(2,1)} %pick_marked.1), calls=%async_computation.1 | async-start | bytes 3407872 | tf_op jit(solution)/shard_map/all_to_all | solution.py:1198
  83.2 420.3 %reduce-scatter.2.cloned.1.call-start = ((), (), s32[]{:S(2)}) async-start(), calls=%async_computation.5 | async-start | bytes 5308416 | tf_op jit(solution)/shard_map/reduce_scatter | solution.py:1262
  88.8 39.0 %collective-permute-start.3 = (bf16[192,1408]{1,0:T(8,128)(2,1)S(1)}, bf16[192,1408]{1,0:T(8,128)(2,1)}, u32[]{:S(2)}, u32[]{:S(2)}) collective-permute-start(bf16[192,1408]{1,0:T(8,128)(2,1)S(1)} %collective-permute-done.2.refs_4_), channel_id=1, source_target_pairs={{0,8},{8,16},{16,24},{24,28},{28,20},{20,12},{12,4},{4,0},{1,9},{9... | collective-permute-start | bytes 1622024 | tf_op jit(solution)/shard_map/ppermute | solution.py:1155
  91.5 47.6 %collective-permute-start.10 = (bf16[192,1280]{1,0:T(8,128)(2,1)S(1)}, bf16[192,1280]{1,0:T(8,128)(2,1)S(1)}, u32[]{:S(2)}, u32[]{:S(2)}) collective-permute-start(bf16[192,1280]{1,0:T(8,128)(2,1)S(1)} %collective-permute-done.9.refs_12_), channel_id=1, source_target_pairs={{8,0},{16,8},{24,16},{28,24},{20,28},{12,20},{4,12},{0,4},{9,1},{1... | collective-permute-start | bytes 1474568 | tf_op jit(solution)/shard_map/ppermute | solution.py:1156
  127.8 21.0 %collective-permute-start.4 = (bf16[192,1408]{1,0:T(8,128)(2,1)}, bf16[192,1408]{1,0:T(8,128)(2,1)}, u32[]{:S(2)}, u32[]{:S(2)}) collective-permute-start(bf16[192,1408]{1,0:T(8,128)(2,1)} %collective-permute-done.3.refs_5_), channel_id=1, source_target_pairs={{0,8},{8,16},{16,24},{24,28},{28,20},{20,12},{12,4},{4,0},{1,9},{9... | collective-permute-start | bytes 1622024 | tf_op jit(solution)/shard_map/ppermute | solution.py:1155
  139.1 19.0 %collective-permute-start.16 = (bf16[9,32,1536]{2,1,0:T(8,128)(2,1)}, bf16[9,32,1536]{2,1,0:T(8,128)(2,1)}, u32[]{:S(2)}, u32[]{:S(2)}) collective-permute-start(bf16[9,32,1536]{2,1,0:T(8,128)(2,1)} %take_rows.2.refs_17_), channel_id=1, source_target_pairs={{0,2},{1,3},{2,0},{3,1},{4,6},{5,7},{6,4},{7,5},{8,10},{9,11},{10,... | collective-permute-start | bytes 2654216 | tf_op jit(solution)/shard_map/ppermute | solution.py:1016
  154.2 31.8 %collective-permute-start.15 = (bf16[9,32,1536]{2,1,0:T(8,128)(2,1)}, bf16[9,32,1536]{2,1,0:T(8,128)(2,1)}, u32[]{:S(2)}, u32[]{:S(2)}) collective-permute-start(bf16[9,32,1536]{2,1,0:T(8,128)(2,1)} %take_rows.2.refs_17_), channel_id=1, source_target_pairs={{0,1},{1,0},{2,3},{3,2},{4,5},{5,4},{6,7},{7,6},{8,9},{9,8},{10,11... | collective-permute-start | bytes 2654216 | tf_op jit(solution)/shard_map/ppermute | solution.py:1016
  158.1 29.0 %collective-permute-start.17 = (bf16[9,32,1536]{2,1,0:T(8,128)(2,1)}, bf16[9,32,1536]{2,1,0:T(8,128)(2,1)}, u32[]{:S(2)}, u32[]{:S(2)}) collective-permute-start(bf16[9,32,1536]{2,1,0:T(8,128)(2,1)} %collective-permute-done.16.refs_19_), channel_id=1, source_target_pairs={{0,1},{1,0},{2,3},{3,2},{4,5},{5,4},{6,7},{7,6},{8,9},{9,8},{10,11... | collective-permute-start | bytes 2654216 | tf_op jit(solution)/shard_map/ppermute | solution.py:1016
  174.4 47.5 %collective-permute-start.14 = (bf16[192,1536]{1,0:T(8,128)(2,1)}, bf16[192,1536]{1,0:T(8,128)(2,1)}, u32[]{:S(2)}, u32[]{:S(2)}) collective-permute-start(bf16[192,1536]{1,0:T(8,128)(2,1)} %get-tuple-element.94.refs_1_), channel_id=1, source_target_pairs={{0,8},{8,16},{16,24},{24,28},{28,20},{20,12},{12,4},{4,0},{1,9},{9... | collective-permute-start | bytes 1769480 | tf_op jit(solution)/shard_map/ppermute | solution.py:1155
  175.5 46.5 %collective-permute-start.19 = (bf16[192,1536]{1,0:T(8,128)(2,1)}, bf16[192,1536]{1,0:T(8,128)(2,1)}, u32[]{:S(2)}, u32[]{:S(2)}) collective-permute-start(bf16[192,1536]{1,0:T(8,128)(2,1)} %get-tuple-element.98.refs_9_), channel_id=1, source_target_pairs={{8,0},{16,8},{24,16},{28,24},{20,28},{12,20},{4,12},{0,4},{9,1},{1... | collective-permute-start | bytes 1769480 | tf_op jit(solution)/shard_map/ppermute | solution.py:1156
  181.7 40.3 %collective-permute-start.21 = (bf16[384,384]{1,0:T(8,128)(2,1)}, bf16[384,384]{1,0:T(8,128)(2,1)}, u32[]{:S(2)}, u32[]{:S(2)}) collective-permute-start(bf16[384,384]{1,0:T(8,128)(2,1)} %get-tuple-element.224), channel_id=1, source_target_pairs={{0,1},{1,0},{2,3},{3,2},{4,5},{5,4},{6,7},{7,6},{8,9},{9,8},{10,11... | collective-permute-start | bytes 884744 | tf_op jit(solution)/shard_map/ppermute | solution.py:1016
  185.9 36.0 %collective-permute-start.22 = (bf16[384,384]{1,0:T(8,128)(2,1)}, bf16[384,384]{1,0:T(8,128)(2,1)}, u32[]{:S(2)}, u32[]{:S(2)}) collective-permute-start(bf16[384,384]{1,0:T(8,128)(2,1)} %get-tuple-element.223), channel_id=1, source_target_pairs={{0,2},{1,3},{2,0},{3,1},{4,6},{5,7},{6,4},{7,5},{8,10},{9,11},{10,... | collective-permute-start | bytes 884744 | tf_op jit(solution)/shard_map/ppermute | solution.py:1016
  187.2 34.8 %collective-permute-start.23 = (bf16[384,384]{1,0:T(8,128)(2,1)}, bf16[384,384]{1,0:T(8,128)(2,1)}, u32[]{:S(2)}, u32[]{:S(2)}) collective-permute-start(bf16[384,384]{1,0:T(8,128)(2,1)} %get-tuple-element.222), channel_id=1, source_target_pairs={{0,3},{1,2},{2,1},{3,0},{4,7},{5,6},{6,5},{7,4},{8,11},{9,10},{10,... | collective-permute-start | bytes 884744 | tf_op jit(solution)/shard_map/ppermute | solution.py:1016
  227.8 21.0 %collective-permute-start.24 = (bf16[9,32,1536]{2,1,0:T(8,128)(2,1)S(1)}, bf16[9,32,1536]{2,1,0:T(8,128)(2,1)S(1)}, u32[]{:S(2)}, u32[]{:S(2)}) collective-permute-start(bf16[9,32,1536]{2,1,0:T(8,128)(2,1)S(1)} %get-tuple-element.208), channel_id=1, source_target_pairs={{0,1},{1,0},{2,3},{3,2},{4,5},{5,4},{6,7},{7,6},{8,9},{9,8},{10,11... | collective-permute-start | bytes 2654216 | tf_op jit(solution)/shard_map/ppermute | solution.py:1016
  230.3 21.2 %collective-permute-start.26 = (bf16[9,32,1536]{2,1,0:T(8,128)(2,1)S(1)}, bf16[9,32,1536]{2,1,0:T(8,128)(2,1)S(1)}, u32[]{:S(2)}, u32[]{:S(2)}) collective-permute-start(bf16[9,32,1536]{2,1,0:T(8,128)(2,1)S(1)} %fusion.6), channel_id=1, source_target_pairs={{0,2},{1,3},{2,0},{3,1},{4,6},{5,7},{6,4},{7,5},{8,10},{9,11},{10,... | collective-permute-start | bytes 2654216 | tf_op jit(solution)/shard_map/ppermute | solution.py:1016
  254.7 20.2 %collective-permute-start.28 = (bf16[9,32,1536]{2,1,0:T(8,128)(2,1)S(1)}, bf16[9,32,1536]{2,1,0:T(8,128)(2,1)S(1)}, u32[]{:S(2)}, u32[]{:S(2)}) collective-permute-start(bf16[9,32,1536]{2,1,0:T(8,128)(2,1)S(1)} %multiply_convert_fusion.refs_17_.refs_1_), channel_id=1, source_target_pairs={{0,2},{1,3},{2,0},{3,1},{4,6},{5,7},{6,4},{7,5},{8,10},{9,11},{10,... | collective-permute-start | bytes 2654216 | tf_op jit(solution)/shard_map/ppermute | solution.py:1016
  262.0 33.6 %collective-permute-start.33 = (bf16[9,32,1664]{2,1,0:T(8,128)(2,1)}, bf16[9,32,1664]{2,1,0:T(8,128)(2,1)}, u32[]{:S(2)}, u32[]{:S(2)}) collective-permute-start(bf16[9,32,1664]{2,1,0:T(8,128)(2,1)} %take_rows.3.refs_21_), channel_id=1, source_target_pairs={{0,2},{1,3},{2,0},{3,1},{4,6},{5,7},{6,4},{7,5},{8,10},{9,11},{10,... | collective-permute-start | bytes 2875400 | tf_op jit(solution)/shard_map/ppermute | solution.py:1016
  276.6 28.7 %collective-permute-start.27 = (bf16[9,32,1536]{2,1,0:T(8,128)(2,1)S(1)}, bf16[9,32,1536]{2,1,0:T(8,128)(2,1)S(1)}, u32[]{:S(2)}, u32[]{:S(2)}) collective-permute-start(bf16[9,32,1536]{2,1,0:T(8,128)(2,1)S(1)} %multiply_convert_fusion.refs_17_.refs_1_), channel_id=1, source_target_pairs={{0,1},{1,0},{2,3},{3,2},{4,5},{5,4},{6,7},{7,6},{8,9},{9,8},{10,11... | collective-permute-start | bytes 2654216 | tf_op jit(solution)/shard_map/ppermute | solution.py:1016
  287.9 22.7 %collective-permute-start.32 = (bf16[9,32,1664]{2,1,0:T(8,128)(2,1)}, bf16[9,32,1664]{2,1,0:T(8,128)(2,1)}, u32[]{:S(2)}, u32[]{:S(2)}) collective-permute-start(bf16[9,32,1664]{2,1,0:T(8,128)(2,1)} %take_rows.3.refs_21_), channel_id=1, source_target_pairs={{0,1},{1,0},{2,3},{3,2},{4,5},{5,4},{6,7},{7,6},{8,9},{9,8},{10,11... | collective-permute-start | bytes 2875400 | tf_op jit(solution)/shard_map/ppermute | solution.py:1016
  303.9 37.8 %collective-permute-start.38 = (bf16[192,1536]{1,0:T(8,128)(2,1)}, bf16[192,1536]{1,0:T(8,128)(2,1)}, u32[]{:S(2)}, u32[]{:S(2)}) collective-permute-start(bf16[192,1536]{1,0:T(8,128)(2,1)} %collective-permute-done.37.refs_7_), channel_id=1, source_target_pairs={{0,8},{8,16},{16,24},{24,28},{28,20},{20,12},{12,4},{4,0},{1,9},{9... | collective-permute-start | bytes 1769480 | tf_op jit(solution)/shard_map/ppermute | solution.py:1155
  305.4 36.4 %collective-permute-start.42 = (bf16[192,1536]{1,0:T(8,128)(2,1)}, bf16[192,1536]{1,0:T(8,128)(2,1)}, u32[]{:S(2)}, u32[]{:S(2)}) collective-permute-start(bf16[192,1536]{1,0:T(8,128)(2,1)} %collective-permute-done.41.refs_15_), channel_id=1, source_target_pairs={{8,0},{16,8},{24,16},{28,24},{20,28},{12,20},{4,12},{0,4},{9,1},{1... | collective-permute-start | bytes 1769480 | tf_op jit(solution)/shard_map/ppermute | solution.py:1156
  401.5 18.9 %collective-permute-start.43 = (bf16[9,32,1664]{2,1,0:T(8,128)(2,1)S(1)}, bf16[9,32,1664]{2,1,0:T(8,128)(2,1)S(1)}, u32[]{:S(2)}, u32[]{:S(2)}) collective-permute-start(bf16[9,32,1664]{2,1,0:T(8,128)(2,1)S(1)} %get-tuple-element.202), channel_id=1, source_target_pairs={{0,1},{1,0},{2,3},{3,2},{4,5},{5,4},{6,7},{7,6},{8,9},{9,8},{10,11... | collective-permute-start | bytes 2875400 | tf_op jit(solution)/shard_map/ppermute | solution.py:1016
  407.8 21.7 %collective-permute-start.45 = (bf16[9,32,1664]{2,1,0:T(8,128)(2,1)S(1)}, bf16[9,32,1664]{2,1,0:T(8,128)(2,1)S(1)}, u32[]{:S(2)}, u32[]{:S(2)}) collective-permute-start(bf16[9,32,1664]{2,1,0:T(8,128)(2,1)S(1)} %fusion.1), channel_id=1, source_target_pairs={{0,2},{1,3},{2,0},{3,1},{4,6},{5,7},{6,4},{7,5},{8,10},{9,11},{10,... | collective-permute-start | bytes 2875400 | tf_op jit(solution)/shard_map/ppermute | solution.py:1016
  418.8 25.0 %collective-permute-start.51 = (bf16[192,1536]{1,0:T(8,128)(2,1)S(1)}, bf16[192,1536]{1,0:T(8,128)(2,1)S(1)}, u32[]{:S(2)}, u32[]{:S(2)}) collective-permute-start(bf16[192,1536]{1,0:T(8,128)(2,1)S(1)} %fusion.31), channel_id=1, source_target_pairs={{0,8},{8,16},{16,24},{24,28},{28,20},{20,12},{12,4},{4,0},{1,9},{9... | collective-permute-start | bytes 1769480 | tf_op jit(solution)/shard_map/ppermute | solution.py:1173
  419.1 30.9 %collective-permute-start.55 = (bf16[192,1536]{1,0:T(8,128)(2,1)S(1)}, bf16[192,1536]{1,0:T(8,128)(2,1)S(1)}, u32[]{:S(2)}, u32[]{:S(2)}) collective-permute-start(bf16[192,1536]{1,0:T(8,128)(2,1)S(1)} %fusion.27), channel_id=1, source_target_pairs={{8,0},{16,8},{24,16},{28,24},{20,28},{12,20},{4,12},{0,4},{9,1},{1... | collective-permute-start | bytes 1769480 | tf_op jit(solution)/shard_map/ppermute | solution.py:1174
  443.9 19.1 %collective-permute-start.48 = (bf16[9,32,1664]{2,1,0:T(8,128)(2,1)S(1)}, bf16[9,32,1664]{2,1,0:T(8,128)(2,1)S(1)}, u32[]{:S(2)}, u32[]{:S(2)}) collective-permute-start(bf16[9,32,1664]{2,1,0:T(8,128)(2,1)S(1)} %bitcast.218), channel_id=1, source_target_pairs={{0,2},{1,3},{2,0},{3,1},{4,6},{5,7},{6,4},{7,5},{8,10},{9,11},{10,... | collective-permute-start | bytes 2875400 | tf_op jit(solution)/shard_map/ppermute | solution.py:1016
  445.2 19.0 %collective-permute-start.52 = (bf16[192,1536]{1,0:T(8,128)(2,1)S(1)}, bf16[192,1536]{1,0:T(8,128)(2,1)S(1)}, u32[]{:S(2)}, u32[]{:S(2)}) collective-permute-start(bf16[192,1536]{1,0:T(8,128)(2,1)S(1)} %fusion.30), channel_id=1, source_target_pairs={{0,8},{8,16},{16,24},{24,28},{28,20},{20,12},{12,4},{4,0},{1,9},{9... | collective-permute-start | bytes 1769480 | tf_op jit(solution)/shard_map/ppermute | solution.py:1173
  451.2 52.3 %collective-permute-start.58 = (bf16[9,32,1664]{2,1,0:T(8,128)(2,1)S(1)}, bf16[9,32,1664]{2,1,0:T(8,128)(2,1)}, u32[]{:S(2)}, u32[]{:S(2)}) collective-permute-start(bf16[9,32,1664]{2,1,0:T(8,128)(2,1)S(1)} %bitcast.219), channel_id=1, source_target_pairs={{0,1},{1,0},{2,3},{3,2},{4,5},{5,4},{6,7},{7,6},{8,9},{9,8},{10,11... | collective-permute-start | bytes 2875400 | tf_op jit(solution)/shard_map/ppermute | solution.py:1016
  453.1 23.4 %collective-permute-start.46 = (bf16[9,32,1536]{2,1,0:T(8,128)(2,1)S(1)}, bf16[9,32,1536]{2,1,0:T(8,128)(2,1)S(1)}, u32[]{:S(2)}, u32[]{:S(2)}) collective-permute-start(bf16[9,32,1536]{2,1,0:T(8,128)(2,1)S(1)} %get-tuple-element.117), channel_id=1, source_target_pairs={{0,1},{1,0},{2,3},{3,2},{4,5},{5,4},{6,7},{7,6},{8,9},{9,8},{10,11... | collective-permute-start | bytes 2654216 | tf_op jit(solution)/shard_map/ppermute | solution.py:1016
  470.6 28.5 %collective-permute-start.53 = (bf16[192,1536]{1,0:T(8,128)(2,1)}, bf16[192,1536]{1,0:T(8,128)(2,1)}, u32[]{:S(2)}, u32[]{:S(2)}) collective-permute-start(bf16[192,1536]{1,0:T(8,128)(2,1)} %fusion.29), channel_id=1, source_target_pairs={{0,8},{8,16},{16,24},{24,28},{28,20},{20,12},{12,4},{4,0},{1,9},{9... | collective-permute-start | bytes 1769480 | tf_op jit(solution)/shard_map/ppermute | solution.py:1173
  474.5 26.8 %collective-permute-start.57 = (bf16[192,1536]{1,0:T(8,128)(2,1)}, bf16[192,1536]{1,0:T(8,128)(2,1)}, u32[]{:S(2)}, u32[]{:S(2)}) collective-permute-start(bf16[192,1536]{1,0:T(8,128)(2,1)} %fusion.25), channel_id=1, source_target_pairs={{8,0},{16,8},{24,16},{28,24},{20,28},{12,20},{4,12},{0,4},{9,1},{1... | collective-permute-start | bytes 1769480 | tf_op jit(solution)/shard_map/ppermute | solution.py:1174
  476.5 27.1 %collective-permute-start.59 = (bf16[9,32,1664]{2,1,0:T(8,128)(2,1)S(1)}, bf16[9,32,1664]{2,1,0:T(8,128)(2,1)}, u32[]{:S(2)}, u32[]{:S(2)}) collective-permute-start(bf16[9,32,1664]{2,1,0:T(8,128)(2,1)S(1)} %collective-permute-done.48.refs_19_.refs_7_), channel_id=1, source_target_pairs={{0,1},{1,0},{2,3},{3,2},{4,5},{5,4},{6,7},{7,6},{8,9},{9,8},{10,11... | collective-permute-start | bytes 2875400 | tf_op jit(solution)/shard_map/ppermute | solution.py:1016
  485.4 77.1 %all-to-all-start.2 = ((bf16[16,32,1536]{2,1,0:T(8,128)(2,1)}), bf16[16,32,1536]{2,1,0:T(8,128)(2,1)S(1)}, u32[]{:S(2)}, u32[]{:S(2)}) async-start(bf16[16,32,1536]{2,1,0:T(8,128)(2,1)} %spread_rows.2), calls=%async_computation.2 | async-start | bytes 3145728 | tf_op jit(solution)/shard_map/all_to_all | solution.py:1316
  566.8 24.4 %collective-permute-start.60 = (bf16[9,32,1536]{2,1,0:T(8,128)(2,1)S(1)}, bf16[9,32,1536]{2,1,0:T(8,128)(2,1)S(1)}, u32[]{:S(2)}, u32[]{:S(2)}) collective-permute-start(bf16[9,32,1536]{2,1,0:T(8,128)(2,1)S(1)} %get-tuple-element.134), channel_id=1, source_target_pairs={{0,1},{1,0},{2,3},{3,2},{4,5},{5,4},{6,7},{7,6},{8,9},{9,8},{10,11... | collective-permute-start | bytes 2654216 | tf_op jit(solution)/shard_map/ppermute | solution.py:1016
  590.6 75.8 %collective-permute-start.77 = (bf16[192,3072]{1,0:T(8,128)(2,1)S(1)}, bf16[192,3072]{1,0:T(8,128)(2,1)S(1)}, u32[]{:S(2)}, u32[]{:S(2)}) collective-permute-start(bf16[192,3072]{1,0:T(8,128)(2,1)S(1)} %pad_maximum_fusion.refs_1_), channel_id=1, source_target_pairs={{0,2},{1,3},{2,0},{3,1},{4,6},{5,7},{6,4},{7,5},{8,10},{9,11},{10,... | collective-permute-start | bytes 3538952 | tf_op jit(solution)/shard_map/ppermute | solution.py:1016
  597.6 22.6 %collective-permute-start.63 = (bf16[384,384]{1,0:T(8,128)(2,1)}, bf16[384,384]{1,0:T(8,128)(2,1)}, u32[]{:S(2)}, u32[]{:S(2)}) collective-permute-start(bf16[384,384]{1,0:T(8,128)(2,1)} %get-tuple-element.220), channel_id=1, source_target_pairs={{0,1},{1,0},{2,3},{3,2},{4,5},{5,4},{6,7},{7,6},{8,9},{9,8},{10,11... | collective-permute-start | bytes 884744 | tf_op jit(solution)/shard_map/ppermute | solution.py:1016
  606.8 18.4 %collective-permute-start.64 = (bf16[384,384]{1,0:T(8,128)(2,1)}, bf16[384,384]{1,0:T(8,128)(2,1)}, u32[]{:S(2)}, u32[]{:S(2)}) collective-permute-start(bf16[384,384]{1,0:T(8,128)(2,1)} %get-tuple-element.219), channel_id=1, source_target_pairs={{0,2},{1,3},{2,0},{3,1},{4,6},{5,7},{6,4},{7,5},{8,10},{9,11},{10,... | collective-permute-start | bytes 884744 | tf_op jit(solution)/shard_map/ppermute | solution.py:1016
  607.9 30.2 %collective-permute-start.65 = (bf16[384,384]{1,0:T(8,128)(2,1)}, bf16[384,384]{1,0:T(8,128)(2,1)}, u32[]{:S(2)}, u32[]{:S(2)}) collective-permute-start(bf16[384,384]{1,0:T(8,128)(2,1)} %get-tuple-element.218), channel_id=1, source_target_pairs={{0,3},{1,2},{2,1},{3,0},{4,7},{5,6},{6,5},{7,4},{8,11},{9,10},{10,... | collective-permute-start | bytes 884744 | tf_op jit(solution)/shard_map/ppermute | solution.py:1016
  614.1 87.7 %all-to-all-start.3 = ((bf16[16,32,1536]{2,1,0:T(8,128)(2,1)}), bf16[16,32,1536]{2,1,0:T(8,128)(2,1)}, u32[]{:S(2)}, u32[]{:S(2)}) async-start(bf16[16,32,1536]{2,1,0:T(8,128)(2,1)} %spread_rows.3), calls=%async_computation.4 | async-start | bytes 3145728 | tf_op jit(solution)/shard_map/all_to_all | solution.py:1343
  619.1 44.2 %collective-permute-start.80 = (bf16[192,1536]{1,0:T(8,128)(2,1)S(1)}, bf16[192,1536]{1,0:T(8,128)(2,1)S(1)}, u32[]{:S(2)}, u32[]{:S(2)}) collective-permute-start(bf16[192,1536]{1,0:T(8,128)(2,1)S(1)} %copy-done.35), channel_id=1, source_target_pairs={{0,2},{1,3},{2,0},{3,1},{4,6},{5,7},{6,4},{7,5},{8,10},{9,11},{10,... | collective-permute-start | bytes 1769480 | tf_op jit(solution)/shard_map/ppermute | solution.py:1016
  662.5 19.5 %collective-permute-start.79 = (bf16[192,1536]{1,0:T(8,128)(2,1)S(1)}, bf16[192,1536]{1,0:T(8,128)(2,1)S(1)}, u32[]{:S(2)}, u32[]{:S(2)}) collective-permute-start(bf16[192,1536]{1,0:T(8,128)(2,1)S(1)} %copy-done.35), channel_id=1, source_target_pairs={{0,1},{1,0},{2,3},{3,2},{4,5},{5,4},{6,7},{7,6},{8,9},{9,8},{10,11... | collective-permute-start | bytes 1769480 | tf_op jit(solution)/shard_map/ppermute | solution.py:1016
  663.3 19.6 %collective-permute-start.81 = (bf16[192,1536]{1,0:T(8,128)(2,1)S(1)}, bf16[192,1536]{1,0:T(8,128)(2,1)S(1)}, u32[]{:S(2)}, u32[]{:S(2)}) collective-permute-start(bf16[192,1536]{1,0:T(8,128)(2,1)S(1)} %collective-permute-done.80.refs_3_), channel_id=1, source_target_pairs={{0,1},{1,0},{2,3},{3,2},{4,5},{5,4},{6,7},{7,6},{8,9},{9,8},{10,11... | collective-permute-start | bytes 1769480 | tf_op jit(solution)/shard_map/ppermute | solution.py:1016
  665.1 23.6 %collective-permute-start.76 = (bf16[192,3072]{1,0:T(8,128)(2,1)S(1)}, bf16[192,3072]{1,0:T(8,128)(2,1)S(1)}, u32[]{:S(2)}, u32[]{:S(2)}) collective-permute-start(bf16[192,3072]{1,0:T(8,128)(2,1)S(1)} %pad_maximum_fusion.refs_1_), channel_id=1, source_target_pairs={{0,1},{1,0},{2,3},{3,2},{4,5},{5,4},{6,7},{7,6},{8,9},{9,8},{10,11... | collective-permute-start | bytes 3538952 | tf_op jit(solution)/shard_map/ppermute | solution.py:1016
  666.4 22.2 %collective-permute-start.78 = (bf16[192,3072]{1,0:T(8,128)(2,1)S(1)}, bf16[192,3072]{1,0:T(8,128)(2,1)S(1)}, u32[]{:S(2)}, u32[]{:S(2)}) collective-permute-start(bf16[192,3072]{1,0:T(8,128)(2,1)S(1)} %collective-permute-done.77.refs_3_), channel_id=1, source_target_pairs={{0,1},{1,0},{2,3},{3,2},{4,5},{5,4},{6,7},{7,6},{8,9},{9,8},{10,11... | collective-permute-start | bytes 3538952 | tf_op jit(solution)/shard_map/ppermute | solution.py:1016
  (151 other events, 2734.1 us)
Sparse Core Ops, SparseCore 0:
  341.9 107.2 reduce-scatter.1

commit v3 on v2

--- a/solution.py
+++ b/solution.py
@@ -1184,6 +1184,14 @@
                 self.step()
             return self.sums
 
+    row = jnp.arange(PAIR_TOK, dtype=jnp.int32)
+    pos = row - jnp.where(row >= first_len, first_len, 0)
+    freq = rope_base ** (-(jnp.arange(HEAD // 2, dtype=F32) * 2.0 / HEAD))
+    angle = pos.astype(F32)[:, None] * freq[None, :]
+    cosine = jnp.concatenate([jnp.cos(angle)] * 4, 1)
+    sine = jnp.sin(angle)
+    sine = jnp.concatenate([-sine, sine, -sine, sine], 1)
+
     half = 3 * hidden // 2
     ring = Gather(
         after(jnp.concatenate([attn_f, expert_own[0, :, :half]], 1), sent_x),
@@ -1194,30 +1202,24 @@
     ring.step()
     ring.step(sent_d)
     x_across, x_near = swap(x_rows, 2), swap(x_rows, 1)
+    others = per - 1
+    second_f = jnp.concatenate([expert_own[e, :, :half] for e in range(1, per)], 1)
+    second_b = jnp.concatenate([expert_own[e, :, half:] for e in range(1, per)], 1)
     ring.step(x_rows)
+    ring.step(cosine, sine)
+    ring.step(x_across, second_f, second_b)
+    x_far = swap(x_across, 1)
+    ring.finish()
     dealt_d = lax.all_to_all(
-        after(sent_d, *ring.last(2)), "dp", split_axis=0, concat_axis=0, tiled=True
+        after(sent_d, *ring.last()), "dp", split_axis=0, concat_axis=0, tiled=True
     )
-    ring.finish()
     ring_fs, ring_bs = ring.fs, ring.bs
-    others = per - 1
-    second = Gather(
-        after(jnp.concatenate([expert_own[e, :, :half] for e in range(1, per)], 1), *ring.last()),
-        after(jnp.concatenate([expert_own[e, :, half:] for e in range(1, per)], 1), *ring.last()),
-    )
+    second = Gather(after(second_f, *ring.last()), after(second_b, *ring.last()))
     second.step()
     turned = turn_out_weight(out_places, ring_fs, ring_bs)
     wout = [turned[0]] + [swap(turned[k], k) for k in range(1, MEMBERS)]
 
-    row = jnp.arange(PAIR_TOK, dtype=jnp.int32)
-    pos = row - jnp.where(row >= first_len, first_len, 0)
-    freq = rope_base ** (-(jnp.arange(HEAD // 2, dtype=F32) * 2.0 / HEAD))
-    angle = pos.astype(F32)[:, None] * freq[None, :]
-    cosine = jnp.concatenate([jnp.cos(angle)] * 4, 1)
-    sine = jnp.sin(angle)
-    sine = jnp.concatenate([-sine, sine, -sine, sine], 1)
-
-    rows_x = [after(x_rows, turned), x_near, x_across, swap(x_across, 1)]
+    rows_x = [after(x_rows, turned), x_near, x_across, x_far]
     a_all, q, k, v, heads, router, gains = attention_forward(
         table, base, ring_fs, ring_bs, rows_of(rows_x), cosine, sine, width
     )

time: 760 us -> 744 us (0.979)
  waiting for transfers between devices: 217 us -> 196 us
  starting transfers between devices: 194 us -> 204 us
    ppermute x14, waiting for transfers between devices: 111 us -> 88.5 us  [step(): self.fs.append(lax.ppermute(after(self.fs[-1], *deps), 'dp', ahead))]
    ppermute x14, starting transfers between devices: 2.84 us -> 17.4 us  [step(): self.bs.append(lax.ppermute(after(self.bs[-1], *deps), 'dp', back))]
  transfers between devices with their start and end apart: 100 -> 100, of which waited for: 39 -> 37; matrix products, arithmetic and copies ran while one was open for 13% -> 12% of each run, Pallas kernels for 27% -> 27%
where the time goes in v3:
time: 744 us; the launch traced here: 736 us
  Pallas kernels  209 us (28%)
  starting transfers between devices  204 us (27%)
  waiting for transfers between devices  196 us (26%)
  other arithmetic  71.5 us (10%)
  local copies, waits for them, and re-layouts  33.8 us (5%)
  between operations  20.3 us (3%)
    ppermute x14, waiting for transfers between devices, step(): self.fs.append(lax.ppermute(after(self.fs[-1], *deps), 'dp', ahead))  88.5 us
    pallas_call x2, Pallas kernels, expert_kernel(): pl.pallas_call(kernel, grid=(tiles + cuts,), out_shape=(jax.ShapeDtypeStr...  85.1 us
    ppermute x39, starting transfers between devices, swap(): return lax.ppermute(values, 'seq', [(i, i ^ bits) for i in range(MEMBERS)])  77.8 us
    ppermute x39, waiting for transfers between devices, swap(): return lax.ppermute(values, 'seq', [(i, i ^ bits) for i in range(MEMBERS)])  40.9 us
    ppermute x14, starting transfers between devices, step(): self.fs.append(lax.ppermute(after(self.fs[-1], *deps), 'dp', ahead))  39.7 us
    pallas_call x1, Pallas kernels, attention_backward(): pl.pallas_call(kernel, out_shape=(jax.ShapeDtypeStruct((MEMBERS, nt, 32,...  39.1 us
    convert_element_type x28, other arithmetic, step(): (got.astype(F32) + mine.astype(F32)).astype(BF)  32.1 us
    ppermute x14, waiting for transfers between devices, step(): b = lax.ppermute(after(self.sums[1], *deps), 'dp', back)  28.7 us
  transfers between devices with their start and end apart: 100, of which 37 were waited for; matrix products, arithmetic and copies ran while one was open for 12% of the time, Pallas kernels for 27%

profile of v3, /device:TPU:1, one launch (start us, length us, event | category | flops | bytes accessed | tf_op | source)
XLA Modules:
  0.0 735.6 jit_solution(14813491315412164434)
XLA Ops:
  7.2 3.4 pick.1
  10.6 6.5 all-to-all-start
  25.8 4.2 pick_marked.1
  30.1 24.3 %collective-permute-done.refs_2_ = bf16[192,1408]{1,0:T(8,128)(2,1)S(1)} collective-permute-done((bf16[192,1408]{1,0:T(8,128)(2,1)S(1)}, bf16[192,1408]{1,0:T(8,128)(2,1)S(1)}, u32[]{:S(2)}, u32[]{:S(2)}) %collective-permute-start) | collective-permute-done | bytes 540704 | tf_op jit(solution)/shard_map/ppermute | solution.py:1155
  54.4 10.8 %collective-permute-start.1 = (bf16[192,1408]{1,0:T(8,128)(2,1)S(1)}, bf16[192,1408]{1,0:T(8,128)(2,1)S(1)}, u32[]{:S(2)}, u32[]{:S(2)}) collective-permute-start(bf16[192,1408]{1,0:T(8,128)(2,1)S(1)} %collective-permute-done.refs_2_), channel_id=1, source_target_pairs={{0,8},{8,16},{16,24},{24,28},{28,20},{20,12},{12,4},{4,0},{1,9},{9... | collective-permute-start | bytes 1622024 | tf_op jit(solution)/shard_map/ppermute | solution.py:1155
  82.7 6.0 collective-permute-done.2.refs_4_
  94.6 5.7 collective-permute-done.3.refs_5_
  102.5 8.5 %collective-permute-done.5.refs_6_ = bf16[192,1408]{1,0:T(8,128)(2,1)S(1)} collective-permute-done((bf16[192,1408]{1,0:T(8,128)(2,1)S(1)}, bf16[192,1408]{1,0:T(8,128)(2,1)S(1)}, u32[]{:S(2)}, u32[]{:S(2)}) %collective-permute-start.5) | collective-permute-done | bytes 540704 | tf_op jit(solution)/shard_map/ppermute | solution.py:1155
  113.2 8.5 %collective-permute-done.6.refs_7_ = bf16[192,1408]{1,0:T(8,128)(2,1)S(1)} collective-permute-done((bf16[192,1408]{1,0:T(8,128)(2,1)S(1)}, bf16[192,1408]{1,0:T(8,128)(2,1)S(1)}, u32[]{:S(2)}, u32[]{:S(2)}) %collective-permute-start.6) | collective-permute-done | bytes 540704 | tf_op jit(solution)/shard_map/ppermute | solution.py:1155
  125.2 7.6 %collective-permute-done.14.refs_16_ = bf16[192,1280]{1,0:T(8,128)(2,1)S(1)} collective-permute-done((bf16[192,1280]{1,0:T(8,128)(2,1)S(1)}, bf16[192,1280]{1,0:T(8,128)(2,1)S(1)}, u32[]{:S(2)}, u32[]{:S(2)}) %collective-permute-start.14) | collective-permute-done | bytes 491552 | tf_op jit(solution)/shard_map/ppermute | solution.py:1156
  132.8 6.7 all-to-all-start.1
  139.5 5.5 collective-permute-start.16
  162.1 23.6 %attention_forward.1 = (bf16[9,128,1536]{2,1,0:T(8,128)(2,1)}, bf16[2,9,384,64]{3,2,1,0:T(8,128)(2,1)}, bf16[2,1152,64]{2,1,0:T(8,128)(2,1)}, bf16[2,1152,64]{2,...) custom-call(s32[42]{0:T(128)S(1)} %concatenate.46.refs_0_.tab, ...), custom_call_target="tpu_custom_call" | custom-call | flops 120000000 | bytes 146800 | tf_op jit(solution)/shard_map/attention_forward/pallas_call | solution.py:423
  188.3 4.1 project_out.1
  196.6 4.9 collective-permute-start.18
  201.6 12.3 %collective-permute-done.18.refs_3_ = bf16[192,1536]{1,0:T(8,128)(2,1)S(1)} collective-permute-done((bf16[192,1536]{1,0:T(8,128)(2,1)}, bf16[192,1536]{1,0:T(8,128)(2,1)S(1)}, u32[]{:S(2)}, u32[]{:S(2)}) %collective-permute-start.18) | collective-permute-done | bytes 589856 | tf_op jit(solution)/shard_map/ppermute | solution.py:1155
  221.3 7.3 collective-permute-done.30.refs_4_
  230.3 10.3 %collective-permute-done.35.refs_5_ = bf16[192,1536]{1,0:T(8,128)(2,1)S(1)} collective-permute-done((bf16[192,1536]{1,0:T(8,128)(2,1)S(1)}, bf16[192,1536]{1,0:T(8,128)(2,1)S(1)}, u32[]{:S(2)}, u32[]{:S(2)}) %collective-permute-start.35) | collective-permute-done | bytes 589856 | tf_op jit(solution)/shard_map/ppermute | solution.py:1155
  240.6 4.0 collective-permute-start.36
  244.8 4.2 collective-permute-start.27
  249.0 4.5 collective-permute-done.36.refs_6_
  255.8 14.4 %collective-permute-start.41 = (bf16[192,1536]{1,0:T(8,128)(2,1)S(1)}, bf16[192,1536]{1,0:T(8,128)(2,1)}, u32[]{:S(2)}, u32[]{:S(2)}) collective-permute-start(bf16[192,1536]{1,0:T(8,128)(2,1)S(1)} %collective-permute-done.40.refs_14_), channel_id=1, source_target_pairs={{8,0},{16,8},{24,16},{28,24},{20,28},{12,20},{4,12},{0,4},{9,1},{1... | collective-permute-start | bytes 1769480 | tf_op jit(solution)/shard_map/ppermute | solution.py:1156
  270.1 6.3 collective-permute-start.32
  285.6 30.8 %expert.2 = (bf16[4,9,32,1664]{3,2,1,0:T(8,128)(2,1)}, bf16[4,9,32,1536]{3,2,1,0:T(8,128)(2,1)}, bf16[1536,1536]{1,0:T(8,128)(2,1)}) custom-call(s32[42]{0:T(128)} %copy-done.39, bf16[192,1408]{1,0:T(8,128)(2,1)} %copy-done.2, bf16[192,1408]{1,0:T(8,128)(2,1)} %copy-done.6, bf16[192,1408]{1,0:T(8,128)(2,1)} %copy-done.8, bf16[192,1408]{1,0:T(8,128)(2,1)} %copy-done.44, ...), custom_call_target="tpu_custom_call" | custom-call | flops 170000000 | bytes 272629 | tf_op jit(solution)/shard_map/expert/pallas_call | solution.py:917
  316.5 54.2 %expert.3 = (bf16[4,9,32,1664]{3,2,1,0:T(8,128)(2,1)}, bf16[4,9,32,1536]{3,2,1,0:T(8,128)(2,1)}, bf16[8,192,1536]{2,1,0:T(8,128)(2,1)}, bf16[8,192,1536]{2,1,0:T(8,128)(2,1)}) custom-call(s32[42]{0:T(128)} %copy-done.39, bf16[192,1536]{1,0:T(8,128)(2,1)} %get-tuple-element.102.refs_1_, bf16[192,1536]{1,0:T(8,128)(2,1)} %collective-permute-done.15.refs_2_, ...), custom_call_target="tpu_custom_call" | custom-call | flops 340000000 | bytes 419430 | tf_op jit(solution)/shard_map/expert/pallas_call | solution.py:917
  372.8 7.2 collective-permute-start.44
  387.6 8.9 %collective-permute-done.50 = bf16[192,1536]{1,0:T(8,128)(2,1)S(1)} collective-permute-done((bf16[192,1536]{1,0:T(8,128)(2,1)S(1)}, bf16[192,1536]{1,0:T(8,128)(2,1)S(1)}, u32[]{:S(2)}, u32[]{:S(2)}) %collective-permute-start.50) | collective-permute-done | bytes 589856 | tf_op jit(solution)/shard_map/ppermute | solution.py:1173
  399.4 8.5 %collective-permute-done.45 = bf16[9,32,1664]{2,1,0:T(8,128)(2,1)S(1)} collective-permute-done((bf16[9,32,1664]{2,1,0:T(8,128)(2,1)S(1)}, bf16[9,32,1664]{2,1,0:T(8,128)(2,1)S(1)}, u32[]{:S(2)}, u32[]{:S(2)}) %collective-permute-start.45) | collective-permute-done | bytes 958496 | tf_op jit(solution)/shard_map/ppermute | solution.py:1016
  417.6 5.1 collective-permute-done.51
  426.7 4.6 collective-permute-done.55
  436.2 7.3 collective-permute-done.48.refs_19_.refs_7_
  445.2 4.0 collective-permute-done.56
  467.6 14.5 %all-to-all-start.2 = ((bf16[16,32,1536]{2,1,0:T(8,128)(2,1)}), bf16[16,32,1536]{2,1,0:T(8,128)(2,1)}, u32[]{:S(2)}, u32[]{:S(2)}) async-start(bf16[16,32,1536]{2,1,0:T(8,128)(2,1)} %spread_rows.2), calls=%async_computation.2 | async-start | bytes 3145728 | tf_op jit(solution)/shard_map/all_to_all | solution.py:1318
  487.5 39.1 %attention_backward.1 = (bf16[4,9,32,1536]{3,2,1,0:T(8,128)(2,1)}, bf16[1152,640]{1,0:T(8,128)(2,1)}) custom-call(s32[42]{0:T(128)} %copy-done.39, bf16[192,1408]{1,0:T(8,128)(2,1)} %copy-done.2, bf16[192,1408]{1,0:T(8,128)(2,1)} %copy-done.6, bf16[192,1408]{1,0:T(8,128)(2,1)} %copy-done.8, bf16[192,1408]{1,0:T(8,128)(2,1)} %copy-done.44, ...), custom_call_target="tpu_custom_call" | custom-call | flops 200000000 | bytes 167772 | tf_op jit(solution)/shard_map/attention_backward/pallas_call | solution.py:573
  528.5 10.1 %collective-permute-done.73 = bf16[192,1536]{1,0:T(8,128)(2,1)S(1)} collective-permute-done((bf16[192,1536]{1,0:T(8,128)(2,1)S(1)}, bf16[192,1536]{1,0:T(8,128)(2,1)S(1)}, u32[]{:S(2)}, u32[]{:S(2)}) %collective-permute-start.73) | collective-permute-done | bytes 589856 | tf_op jit(solution)/shard_map/ppermute | solution.py:1174
  546.1 4.3 collective-permute-start.61
  559.3 12.1 %attention_grads.1 = (bf16[8,192,512]{2,1,0:T(8,128)(2,1)}, bf16[8,192,640]{2,1,0:T(8,128)(2,1)}, bf16[4,384,384]{2,1,0:T(8,128)(2,1)}) custom-call(s32[42]{0:T(128)S(1)} %copy-done.40, bf16[9,32,1536]{2,1,0:T(8,128)(2,1)S(1)} %copy-done.1, bf16[9,32,1536]{2,1,0:T(8,128)(2,1)S(1)} %copy-done.15, bf16[9,32,1536]{2,1,0:T(8,128)(2,1)S(1)} %copy-done.13, ...), custom_call_target="tpu_custom_call" | custom-call | flops 40000000 | bytes 167772 | tf_op jit(solution)/shard_map/attention_grads/pallas_call | solution.py:638
  579.5 9.1 %collective-permute-start.63 = (bf16[384,384]{1,0:T(8,128)(2,1)}, bf16[384,384]{1,0:T(8,128)(2,1)}, u32[]{:S(2)}, u32[]{:S(2)}) collective-permute-start(bf16[384,384]{1,0:T(8,128)(2,1)} %get-tuple-element.228), channel_id=1, source_target_pairs={{0,1},{1,0},{2,3},{3,2},{4,5},{5,4},{6,7},{7,6},{8,9},{9,8},{10,11... | collective-permute-start | bytes 884744 | tf_op jit(solution)/shard_map/ppermute | solution.py:1016
  596.4 5.0 all-to-all-start.3
  603.1 4.6 collective-permute-done.64.refs_3_
  607.7 13.3 %collective-permute-done.65.refs_4_ = bf16[384,384]{1,0:T(8,128)(2,1)} collective-permute-done((bf16[384,384]{1,0:T(8,128)(2,1)}, bf16[384,384]{1,0:T(8,128)(2,1)}, u32[]{:S(2)}, u32[]{:S(2)}) %collective-permute-start.65) | collective-permute-done | bytes 294944 | tf_op jit(solution)/shard_map/ppermute | solution.py:1016
  633.7 9.8 %collective-permute-start.70 = (bf16[192,512]{1,0:T(8,128)(2,1)S(1)}, bf16[192,512]{1,0:T(8,128)(2,1)S(1)}, u32[]{:S(2)}, u32[]{:S(2)}) collective-permute-start(bf16[192,512]{1,0:T(8,128)(2,1)S(1)} %fusion.49), channel_id=1, source_target_pairs={{0,8},{8,16},{16,24},{24,28},{28,20},{20,12},{12,4},{4,0},{1,9},{9... | collective-permute-start | bytes 589832 | tf_op jit(solution)/shard_map/ppermute | solution.py:1173
  658.5 4.1 collective-permute-done.87
  665.1 4.7 place_experts.2
  670.9 7.6 %place_experts.3 = (f32[12,192,1536]{2,1,0:T(8,128)}, f32[192,128]{1,0:T(8,128)S(1)}) custom-call(s32[4]{0:T(128)S(1)} %iota_xor_fusion.refs_0_, bf16[192,3072]{1,0:T(8,128)(2,1)S(1)} %pad_maximum_fusion.refs_1_, bf16[192,3072]{1,0:T(8,128)(2,1)S(1)} %collective-permute-done.76.refs_2_, ...), custom_call_target="tpu_custom_call", output_to_operand_aliasing={{0}: (6, {})} | custom-call | bytes 141557 | tf_op jit(solution)/shard_map/place_experts/pallas_call | solution.py:246
  696.0 3.9 collective-permute-done.84
  705.8 8.3 %collective-permute-start.92 = (bf16[192,1024]{1,0:T(8,128)(2,1)S(1)}, bf16[192,1024]{1,0:T(8,128)(2,1)S(1)}, u32[]{:S(2)}, u32[]{:S(2)}) collective-permute-start(bf16[192,1024]{1,0:T(8,128)(2,1)S(1)} %pad_maximum_fusion.7.refs_1_), channel_id=1, source_target_pairs={{0,1},{1,0},{2,3},{3,2},{4,5},{5,4},{6,7},{7,6},{8,9},{9,8},{10,11... | collective-permute-start | bytes 1179656 | tf_op jit(solution)/shard_map/ppermute | solution.py:1016
  714.1 5.7 collective-permute-start.94
  (468 shorter events, 235.0 us)
Async XLA Ops:
  10.6 61.0 %all-to-all-start = ((bf16[16,32,1536]{2,1,0:T(8,128)(2,1)}), bf16[16,32,1536]{2,1,0:T(8,128)(2,1)}, u32[]{:S(2)}, u32[]{:S(2)}) async-start(bf16[16,32,1536]{2,1,0:T(8,128)(2,1)} %pick.1), calls=%async_computation | async-start | bytes 3145728 | tf_op jit(solution)/shard_map/all_to_all | solution.py:1083
  22.3 32.1 %collective-permute-start = (bf16[192,1408]{1,0:T(8,128)(2,1)S(1)}, bf16[192,1408]{1,0:T(8,128)(2,1)S(1)}, u32[]{:S(2)}, u32[]{:S(2)}) collective-permute-start(bf16[192,1408]{1,0:T(8,128)(2,1)S(1)} %concatenate.41.refs_1_), channel_id=1, source_target_pairs={{0,8},{8,16},{16,24},{24,28},{28,20},{20,12},{12,4},{4,0},{1,9},{9... | collective-permute-start | bytes 1622024 | tf_op jit(solution)/shard_map/ppermute | solution.py:1155
  24.8 40.4 %collective-permute-start.8 = (bf16[192,1280]{1,0:T(8,128)(2,1)S(1)}, bf16[192,1280]{1,0:T(8,128)(2,1)S(1)}, u32[]{:S(2)}, u32[]{:S(2)}) collective-permute-start(bf16[192,1280]{1,0:T(8,128)(2,1)S(1)} %pad_maximum_fusion.6.refs_9_), channel_id=1, source_target_pairs={{8,0},{16,8},{24,16},{28,24},{20,28},{12,20},{4,12},{0,4},{9,1},{1... | collective-permute-start | bytes 1474568 | tf_op jit(solution)/shard_map/ppermute | solution.py:1156
  54.4 21.9 %collective-permute-start.1 = (bf16[192,1408]{1,0:T(8,128)(2,1)S(1)}, bf16[192,1408]{1,0:T(8,128)(2,1)S(1)}, u32[]{:S(2)}, u32[]{:S(2)}) collective-permute-start(bf16[192,1408]{1,0:T(8,128)(2,1)S(1)} %collective-permute-done.refs_2_), channel_id=1, source_target_pairs={{0,8},{8,16},{16,24},{24,28},{28,20},{20,12},{12,4},{4,0},{1,9},{9... | collective-permute-start | bytes 1622024 | tf_op jit(solution)/shard_map/ppermute | solution.py:1155
  73.9 20.7 %collective-permute-start.4 = (bf16[9,32,1536]{2,1,0:T(8,128)(2,1)}, bf16[9,32,1536]{2,1,0:T(8,128)(2,1)S(1)}, u32[]{:S(2)}, u32[]{:S(2)}) collective-permute-start(bf16[9,32,1536]{2,1,0:T(8,128)(2,1)} %take_rows.2.refs_17_), channel_id=1, source_target_pairs={{0,2},{1,3},{2,0},{3,1},{4,6},{5,7},{6,4},{7,5},{8,10},{9,11},{10,... | collective-permute-start | bytes 2654216 | tf_op jit(solution)/shard_map/ppermute | solution.py:1016
  132.8 53.0 %all-to-all-start.1 = ((bf16[16,32,1664]{2,1,0:T(8,128)(2,1)}), bf16[16,32,1664]{2,1,0:T(8,128)(2,1)}, u32[]{:S(2)}, u32[]{:S(2)}) async-start(bf16[16,32,1664]{2,1,0:T(8,128)(2,1)} %pick_marked.1), calls=%async_computation.1 | async-start | bytes 3407872 | tf_op jit(solution)/shard_map/all_to_all | solution.py:1213
  139.5 347.0 %reduce-scatter.2.cloned.1.call-start = ((), (), s32[]{:S(2)}) async-start(), calls=%async_computation.5 | async-start | bytes 5308416 | tf_op jit(solution)/shard_map/reduce_scatter | solution.py:1264
  145.8 42.5 %collective-permute-start.15 = (bf16[192,1536]{1,0:T(8,128)(2,1)}, bf16[192,1536]{1,0:T(8,128)(2,1)}, u32[]{:S(2)}, u32[]{:S(2)}) collective-permute-start(bf16[192,1536]{1,0:T(8,128)(2,1)} %get-tuple-element.102.refs_1_), channel_id=1, source_target_pairs={{0,8},{8,16},{16,24},{24,28},{28,20},{20,12},{12,4},{4,0},{1,9},{9... | collective-permute-start | bytes 1769480 | tf_op jit(solution)/shard_map/ppermute | solution.py:1155
  147.4 40.8 %collective-permute-start.19 = (bf16[192,1536]{1,0:T(8,128)(2,1)}, bf16[192,1536]{1,0:T(8,128)(2,1)}, u32[]{:S(2)}, u32[]{:S(2)}) collective-permute-start(bf16[192,1536]{1,0:T(8,128)(2,1)} %get-tuple-element.106.refs_9_), channel_id=1, source_target_pairs={{8,0},{16,8},{24,16},{28,24},{20,28},{12,20},{4,12},{0,4},{9,1},{1... | collective-permute-start | bytes 1769480 | tf_op jit(solution)/shard_map/ppermute | solution.py:1156
  153.7 34.6 %collective-permute-start.21 = (bf16[384,384]{1,0:T(8,128)(2,1)}, bf16[384,384]{1,0:T(8,128)(2,1)}, u32[]{:S(2)}, u32[]{:S(2)}) collective-permute-start(bf16[384,384]{1,0:T(8,128)(2,1)} %get-tuple-element.232), channel_id=1, source_target_pairs={{0,1},{1,0},{2,3},{3,2},{4,5},{5,4},{6,7},{7,6},{8,9},{9,8},{10,11... | collective-permute-start | bytes 884744 | tf_op jit(solution)/shard_map/ppermute | solution.py:1016
  154.4 33.8 %collective-permute-start.22 = (bf16[384,384]{1,0:T(8,128)(2,1)}, bf16[384,384]{1,0:T(8,128)(2,1)}, u32[]{:S(2)}, u32[]{:S(2)}) collective-permute-start(bf16[384,384]{1,0:T(8,128)(2,1)} %get-tuple-element.231), channel_id=1, source_target_pairs={{0,2},{1,3},{2,0},{3,1},{4,6},{5,7},{6,4},{7,5},{8,10},{9,11},{10,... | collective-permute-start | bytes 884744 | tf_op jit(solution)/shard_map/ppermute | solution.py:1016
  155.7 32.6 %collective-permute-start.23 = (bf16[384,384]{1,0:T(8,128)(2,1)}, bf16[384,384]{1,0:T(8,128)(2,1)}, u32[]{:S(2)}, u32[]{:S(2)}) collective-permute-start(bf16[384,384]{1,0:T(8,128)(2,1)} %get-tuple-element.230), channel_id=1, source_target_pairs={{0,3},{1,2},{2,1},{3,0},{4,7},{5,6},{6,5},{7,4},{8,11},{9,10},{10,... | collective-permute-start | bytes 884744 | tf_op jit(solution)/shard_map/ppermute | solution.py:1016
  192.8 24.2 %collective-permute-start.24 = (bf16[9,32,1536]{2,1,0:T(8,128)(2,1)S(1)}, bf16[9,32,1536]{2,1,0:T(8,128)(2,1)S(1)}, u32[]{:S(2)}, u32[]{:S(2)}) collective-permute-start(bf16[9,32,1536]{2,1,0:T(8,128)(2,1)S(1)} %get-tuple-element.216), channel_id=1, source_target_pairs={{0,1},{1,0},{2,3},{3,2},{4,5},{5,4},{6,7},{7,6},{8,9},{9,8},{10,11... | collective-permute-start | bytes 2654216 | tf_op jit(solution)/shard_map/ppermute | solution.py:1016
  195.4 21.7 %collective-permute-start.26 = (bf16[9,32,1536]{2,1,0:T(8,128)(2,1)S(1)}, bf16[9,32,1536]{2,1,0:T(8,128)(2,1)S(1)}, u32[]{:S(2)}, u32[]{:S(2)}) collective-permute-start(bf16[9,32,1536]{2,1,0:T(8,128)(2,1)S(1)} %fusion.6), channel_id=1, source_target_pairs={{0,2},{1,3},{2,0},{3,1},{4,6},{5,7},{6,4},{7,5},{8,10},{9,11},{10,... | collective-permute-start | bytes 2654216 | tf_op jit(solution)/shard_map/ppermute | solution.py:1016
  196.6 17.2 %collective-permute-start.18 = (bf16[192,1536]{1,0:T(8,128)(2,1)}, bf16[192,1536]{1,0:T(8,128)(2,1)S(1)}, u32[]{:S(2)}, u32[]{:S(2)}) collective-permute-start(bf16[192,1536]{1,0:T(8,128)(2,1)} %collective-permute-done.15.refs_2_), channel_id=1, source_target_pairs={{0,8},{8,16},{16,24},{24,28},{28,20},{20,12},{12,4},{4,0},{1,9},{9... | collective-permute-start | bytes 1769480 | tf_op jit(solution)/shard_map/ppermute | solution.py:1155
  220.6 20.0 %collective-permute-start.28 = (bf16[9,32,1536]{2,1,0:T(8,128)(2,1)S(1)}, bf16[9,32,1536]{2,1,0:T(8,128)(2,1)S(1)}, u32[]{:S(2)}, u32[]{:S(2)}) collective-permute-start(bf16[9,32,1536]{2,1,0:T(8,128)(2,1)S(1)} %multiply_convert_fusion.refs_17_.refs_1_), channel_id=1, source_target_pairs={{0,2},{1,3},{2,0},{3,1},{4,6},{5,7},{6,4},{7,5},{8,10},{9,11},{10,... | collective-permute-start | bytes 2654216 | tf_op jit(solution)/shard_map/ppermute | solution.py:1016
  230.1 46.4 %collective-permute-start.33 = (bf16[9,32,1664]{2,1,0:T(8,128)(2,1)}, bf16[9,32,1664]{2,1,0:T(8,128)(2,1)}, u32[]{:S(2)}, u32[]{:S(2)}) collective-permute-start(bf16[9,32,1664]{2,1,0:T(8,128)(2,1)} %take_rows.3.refs_21_), channel_id=1, source_target_pairs={{0,2},{1,3},{2,0},{3,1},{4,6},{5,7},{6,4},{7,5},{8,10},{9,11},{10,... | collective-permute-start | bytes 2875400 | tf_op jit(solution)/shard_map/ppermute | solution.py:1016
  244.8 37.5 %collective-permute-start.27 = (bf16[9,32,1536]{2,1,0:T(8,128)(2,1)S(1)}, bf16[9,32,1536]{2,1,0:T(8,128)(2,1)S(1)}, u32[]{:S(2)}, u32[]{:S(2)}) collective-permute-start(bf16[9,32,1536]{2,1,0:T(8,128)(2,1)S(1)} %multiply_convert_fusion.refs_17_.refs_1_), channel_id=1, source_target_pairs={{0,1},{1,0},{2,3},{3,2},{4,5},{5,4},{6,7},{7,6},{8,9},{9,8},{10,11... | collective-permute-start | bytes 2654216 | tf_op jit(solution)/shard_map/ppermute | solution.py:1016
  253.5 26.1 %collective-permute-start.37 = (bf16[192,1536]{1,0:T(8,128)(2,1)S(1)}, bf16[192,1536]{1,0:T(8,128)(2,1)}, u32[]{:S(2)}, u32[]{:S(2)}) collective-permute-start(bf16[192,1536]{1,0:T(8,128)(2,1)S(1)} %collective-permute-done.36.refs_6_), channel_id=1, source_target_pairs={{0,8},{8,16},{16,24},{24,28},{28,20},{20,12},{12,4},{4,0},{1,9},{9... | collective-permute-start | bytes 1769480 | tf_op jit(solution)/shard_map/ppermute | solution.py:1155
  255.8 24.7 %collective-permute-start.41 = (bf16[192,1536]{1,0:T(8,128)(2,1)S(1)}, bf16[192,1536]{1,0:T(8,128)(2,1)}, u32[]{:S(2)}, u32[]{:S(2)}) collective-permute-start(bf16[192,1536]{1,0:T(8,128)(2,1)S(1)} %collective-permute-done.40.refs_14_), channel_id=1, source_target_pairs={{8,0},{16,8},{24,16},{28,24},{20,28},{12,20},{4,12},{0,4},{9,1},{1... | collective-permute-start | bytes 1769480 | tf_op jit(solution)/shard_map/ppermute | solution.py:1156
  280.5 35.9 %collective-permute-start.38 = (bf16[192,1536]{1,0:T(8,128)(2,1)}, bf16[192,1536]{1,0:T(8,128)(2,1)}, u32[]{:S(2)}, u32[]{:S(2)}) collective-permute-start(bf16[192,1536]{1,0:T(8,128)(2,1)} %collective-permute-done.37.refs_7_), channel_id=1, source_target_pairs={{0,8},{8,16},{16,24},{24,28},{28,20},{20,12},{12,4},{4,0},{1,9},{9... | collective-permute-start | bytes 1769480 | tf_op jit(solution)/shard_map/ppermute | solution.py:1155
  282.3 34.2 %collective-permute-start.42 = (bf16[192,1536]{1,0:T(8,128)(2,1)}, bf16[192,1536]{1,0:T(8,128)(2,1)}, u32[]{:S(2)}, u32[]{:S(2)}) collective-permute-start(bf16[192,1536]{1,0:T(8,128)(2,1)} %collective-permute-done.41.refs_15_), channel_id=1, source_target_pairs={{8,0},{16,8},{24,16},{28,24},{20,28},{12,20},{4,12},{0,4},{9,1},{1... | collective-permute-start | bytes 1769480 | tf_op jit(solution)/shard_map/ppermute | solution.py:1156
  380.0 19.4 %collective-permute-start.43 = (bf16[9,32,1664]{2,1,0:T(8,128)(2,1)S(1)}, bf16[9,32,1664]{2,1,0:T(8,128)(2,1)S(1)}, u32[]{:S(2)}, u32[]{:S(2)}) collective-permute-start(bf16[9,32,1664]{2,1,0:T(8,128)(2,1)S(1)} %get-tuple-element.210), channel_id=1, source_target_pairs={{0,1},{1,0},{2,3},{3,2},{4,5},{5,4},{6,7},{7,6},{8,9},{9,8},{10,11... | collective-permute-start | bytes 2875400 | tf_op jit(solution)/shard_map/ppermute | solution.py:1016
  386.3 21.6 %collective-permute-start.45 = (bf16[9,32,1664]{2,1,0:T(8,128)(2,1)S(1)}, bf16[9,32,1664]{2,1,0:T(8,128)(2,1)S(1)}, u32[]{:S(2)}, u32[]{:S(2)}) collective-permute-start(bf16[9,32,1664]{2,1,0:T(8,128)(2,1)S(1)} %fusion.1), channel_id=1, source_target_pairs={{0,2},{1,3},{2,0},{3,1},{4,6},{5,7},{6,4},{7,5},{8,10},{9,11},{10,... | collective-permute-start | bytes 2875400 | tf_op jit(solution)/shard_map/ppermute | solution.py:1016
  397.9 24.8 %collective-permute-start.51 = (bf16[192,1536]{1,0:T(8,128)(2,1)S(1)}, bf16[192,1536]{1,0:T(8,128)(2,1)S(1)}, u32[]{:S(2)}, u32[]{:S(2)}) collective-permute-start(bf16[192,1536]{1,0:T(8,128)(2,1)S(1)} %fusion.31), channel_id=1, source_target_pairs={{0,8},{8,16},{16,24},{24,28},{28,20},{20,12},{12,4},{4,0},{1,9},{9... | collective-permute-start | bytes 1769480 | tf_op jit(solution)/shard_map/ppermute | solution.py:1173
  398.0 33.3 %collective-permute-start.55 = (bf16[192,1536]{1,0:T(8,128)(2,1)S(1)}, bf16[192,1536]{1,0:T(8,128)(2,1)S(1)}, u32[]{:S(2)}, u32[]{:S(2)}) collective-permute-start(bf16[192,1536]{1,0:T(8,128)(2,1)S(1)} %fusion.27), channel_id=1, source_target_pairs={{8,0},{16,8},{24,16},{28,24},{20,28},{12,20},{4,12},{0,4},{9,1},{1... | collective-permute-start | bytes 1769480 | tf_op jit(solution)/shard_map/ppermute | solution.py:1174
  415.4 18.0 %collective-permute-start.47 = (bf16[9,32,1536]{2,1,0:T(8,128)(2,1)S(1)}, bf16[9,32,1536]{2,1,0:T(8,128)(2,1)S(1)}, u32[]{:S(2)}, u32[]{:S(2)}) collective-permute-start(bf16[9,32,1536]{2,1,0:T(8,128)(2,1)S(1)} %get-tuple-element.126), channel_id=1, source_target_pairs={{0,1},{1,0},{2,3},{3,2},{4,5},{5,4},{6,7},{7,6},{8,9},{9,8},{10,11... | collective-permute-start | bytes 2654216 | tf_op jit(solution)/shard_map/ppermute | solution.py:1016
  422.9 20.6 %collective-permute-start.48 = (bf16[9,32,1664]{2,1,0:T(8,128)(2,1)S(1)}, bf16[9,32,1664]{2,1,0:T(8,128)(2,1)S(1)}, u32[]{:S(2)}, u32[]{:S(2)}) collective-permute-start(bf16[9,32,1664]{2,1,0:T(8,128)(2,1)S(1)} %bitcast.218), channel_id=1, source_target_pairs={{0,2},{1,3},{2,0},{3,1},{4,6},{5,7},{6,4},{7,5},{8,10},{9,11},{10,... | collective-permute-start | bytes 2875400 | tf_op jit(solution)/shard_map/ppermute | solution.py:1016
  424.4 20.7 %collective-permute-start.52 = (bf16[192,1536]{1,0:T(8,128)(2,1)S(1)}, bf16[192,1536]{1,0:T(8,128)(2,1)S(1)}, u32[]{:S(2)}, u32[]{:S(2)}) collective-permute-start(bf16[192,1536]{1,0:T(8,128)(2,1)S(1)} %fusion.30), channel_id=1, source_target_pairs={{0,8},{8,16},{16,24},{24,28},{28,20},{20,12},{12,4},{4,0},{1,9},{9... | collective-permute-start | bytes 1769480 | tf_op jit(solution)/shard_map/ppermute | solution.py:1173
  432.5 54.1 %collective-permute-start.58 = (bf16[9,32,1664]{2,1,0:T(8,128)(2,1)S(1)}, bf16[9,32,1664]{2,1,0:T(8,128)(2,1)S(1)}, u32[]{:S(2)}, u32[]{:S(2)}) collective-permute-start(bf16[9,32,1664]{2,1,0:T(8,128)(2,1)S(1)} %bitcast.219), channel_id=1, source_target_pairs={{0,1},{1,0},{2,3},{3,2},{4,5},{5,4},{6,7},{7,6},{8,9},{9,8},{10,11... | collective-permute-start | bytes 2875400 | tf_op jit(solution)/shard_map/ppermute | solution.py:1016
  433.4 23.1 %collective-permute-start.46 = (bf16[9,32,1536]{2,1,0:T(8,128)(2,1)S(1)}, bf16[9,32,1536]{2,1,0:T(8,128)(2,1)S(1)}, u32[]{:S(2)}, u32[]{:S(2)}) collective-permute-start(bf16[9,32,1536]{2,1,0:T(8,128)(2,1)S(1)} %get-tuple-element.125), channel_id=1, source_target_pairs={{0,1},{1,0},{2,3},{3,2},{4,5},{5,4},{6,7},{7,6},{8,9},{9,8},{10,11... | collective-permute-start | bytes 2654216 | tf_op jit(solution)/shard_map/ppermute | solution.py:1016
  443.4 18.5 %collective-permute-start.49 = (bf16[9,32,1536]{2,1,0:T(8,128)(2,1)S(1)}, bf16[9,32,1536]{2,1,0:T(8,128)(2,1)S(1)}, u32[]{:S(2)}, u32[]{:S(2)}) collective-permute-start(bf16[9,32,1536]{2,1,0:T(8,128)(2,1)S(1)} %fusion.14), channel_id=1, source_target_pairs={{0,2},{1,3},{2,0},{3,1},{4,6},{5,7},{6,4},{7,5},{8,10},{9,11},{10,... | collective-permute-start | bytes 2654216 | tf_op jit(solution)/shard_map/ppermute | solution.py:1016
  451.3 30.8 %collective-permute-start.53 = (bf16[192,1536]{1,0:T(8,128)(2,1)S(1)}, bf16[192,1536]{1,0:T(8,128)(2,1)}, u32[]{:S(2)}, u32[]{:S(2)}) collective-permute-start(bf16[192,1536]{1,0:T(8,128)(2,1)S(1)} %fusion.29), channel_id=1, source_target_pairs={{0,8},{8,16},{16,24},{24,28},{28,20},{20,12},{12,4},{4,0},{1,9},{9... | collective-permute-start | bytes 1769480 | tf_op jit(solution)/shard_map/ppermute | solution.py:1173
  453.5 30.9 %collective-permute-start.57 = (bf16[192,1536]{1,0:T(8,128)(2,1)}, bf16[192,1536]{1,0:T(8,128)(2,1)}, u32[]{:S(2)}, u32[]{:S(2)}) collective-permute-start(bf16[192,1536]{1,0:T(8,128)(2,1)} %fusion.25), channel_id=1, source_target_pairs={{8,0},{16,8},{24,16},{28,24},{20,28},{12,20},{4,12},{0,4},{9,1},{1... | collective-permute-start | bytes 1769480 | tf_op jit(solution)/shard_map/ppermute | solution.py:1174
  456.5 30.0 %collective-permute-start.59 = (bf16[9,32,1664]{2,1,0:T(8,128)(2,1)S(1)}, bf16[9,32,1664]{2,1,0:T(8,128)(2,1)}, u32[]{:S(2)}, u32[]{:S(2)}) collective-permute-start(bf16[9,32,1664]{2,1,0:T(8,128)(2,1)S(1)} %collective-permute-done.48.refs_19_.refs_7_), channel_id=1, source_target_pairs={{0,1},{1,0},{2,3},{3,2},{4,5},{5,4},{6,7},{7,6},{8,9},{9,8},{10,11... | collective-permute-start | bytes 2875400 | tf_op jit(solution)/shard_map/ppermute | solution.py:1016
  467.6 78.5 %all-to-all-start.2 = ((bf16[16,32,1536]{2,1,0:T(8,128)(2,1)}), bf16[16,32,1536]{2,1,0:T(8,128)(2,1)}, u32[]{:S(2)}, u32[]{:S(2)}) async-start(bf16[16,32,1536]{2,1,0:T(8,128)(2,1)} %spread_rows.2), calls=%async_computation.2 | async-start | bytes 3145728 | tf_op jit(solution)/shard_map/all_to_all | solution.py:1318
  550.4 23.7 %collective-permute-start.60 = (bf16[9,32,1536]{2,1,0:T(8,128)(2,1)}, bf16[9,32,1536]{2,1,0:T(8,128)(2,1)S(1)}, u32[]{:S(2)}, u32[]{:S(2)}) collective-permute-start(bf16[9,32,1536]{2,1,0:T(8,128)(2,1)} %get-tuple-element.142), channel_id=1, source_target_pairs={{0,1},{1,0},{2,3},{3,2},{4,5},{5,4},{6,7},{7,6},{8,9},{9,8},{10,11... | collective-permute-start | bytes 2654216 | tf_op jit(solution)/shard_map/ppermute | solution.py:1016
  552.3 19.1 %collective-permute-start.75 = (bf16[192,1536]{1,0:T(8,128)(2,1)S(1)}, bf16[192,1536]{1,0:T(8,128)(2,1)S(1)}, u32[]{:S(2)}, u32[]{:S(2)}) collective-permute-start(bf16[192,1536]{1,0:T(8,128)(2,1)S(1)} %fusion.19), channel_id=1, source_target_pairs={{8,0},{16,8},{24,16},{28,24},{20,28},{12,20},{4,12},{0,4},{9,1},{1... | collective-permute-start | bytes 1769480 | tf_op jit(solution)/shard_map/ppermute | solution.py:1174
  574.0 74.7 %collective-permute-start.77 = (bf16[192,3072]{1,0:T(8,128)(2,1)S(1)}, bf16[192,3072]{1,0:T(8,128)(2,1)S(1)}, u32[]{:S(2)}, u32[]{:S(2)}) collective-permute-start(bf16[192,3072]{1,0:T(8,128)(2,1)S(1)} %pad_maximum_fusion.refs_1_), channel_id=1, source_target_pairs={{0,2},{1,3},{2,0},{3,1},{4,6},{5,7},{6,4},{7,5},{8,10},{9,11},{10,... | collective-permute-start | bytes 3538952 | tf_op jit(solution)/shard_map/ppermute | solution.py:1016
  579.5 23.5 %collective-permute-start.63 = (bf16[384,384]{1,0:T(8,128)(2,1)}, bf16[384,384]{1,0:T(8,128)(2,1)}, u32[]{:S(2)}, u32[]{:S(2)}) collective-permute-start(bf16[384,384]{1,0:T(8,128)(2,1)} %get-tuple-element.228), channel_id=1, source_target_pairs={{0,1},{1,0},{2,3},{3,2},{4,5},{5,4},{6,7},{7,6},{8,9},{9,8},{10,11... | collective-permute-start | bytes 884744 | tf_op jit(solution)/shard_map/ppermute | solution.py:1016
  588.7 19.0 %collective-permute-start.64 = (bf16[384,384]{1,0:T(8,128)(2,1)}, bf16[384,384]{1,0:T(8,128)(2,1)}, u32[]{:S(2)}, u32[]{:S(2)}) collective-permute-start(bf16[384,384]{1,0:T(8,128)(2,1)} %get-tuple-element.227), channel_id=1, source_target_pairs={{0,2},{1,3},{2,0},{3,1},{4,6},{5,7},{6,4},{7,5},{8,10},{9,11},{10,... | collective-permute-start | bytes 884744 | tf_op jit(solution)/shard_map/ppermute | solution.py:1016
  590.9 30.1 %collective-permute-start.65 = (bf16[384,384]{1,0:T(8,128)(2,1)}, bf16[384,384]{1,0:T(8,128)(2,1)}, u32[]{:S(2)}, u32[]{:S(2)}) collective-permute-start(bf16[384,384]{1,0:T(8,128)(2,1)} %get-tuple-element.226), channel_id=1, source_target_pairs={{0,3},{1,2},{2,1},{3,0},{4,7},{5,6},{6,5},{7,4},{8,11},{9,10},{10,... | collective-permute-start | bytes 884744 | tf_op jit(solution)/shard_map/ppermute | solution.py:1016
  596.4 87.7 %all-to-all-start.3 = ((bf16[16,32,1536]{2,1,0:T(8,128)(2,1)}), bf16[16,32,1536]{2,1,0:T(8,128)(2,1)}, u32[]{:S(2)}, u32[]{:S(2)}) async-start(bf16[16,32,1536]{2,1,0:T(8,128)(2,1)} %spread_rows.3), calls=%async_computation.4 | async-start | bytes 3145728 | tf_op jit(solution)/shard_map/all_to_all | solution.py:1345
  601.4 44.2 %collective-permute-start.80 = (bf16[192,1536]{1,0:T(8,128)(2,1)S(1)}, bf16[192,1536]{1,0:T(8,128)(2,1)S(1)}, u32[]{:S(2)}, u32[]{:S(2)}) collective-permute-start(bf16[192,1536]{1,0:T(8,128)(2,1)S(1)} %copy-done.36), channel_id=1, source_target_pairs={{0,2},{1,3},{2,0},{3,1},{4,6},{5,7},{6,4},{7,5},{8,10},{9,11},{10,... | collective-permute-start | bytes 1769480 | tf_op jit(solution)/shard_map/ppermute | solution.py:1016
  644.7 19.5 %collective-permute-start.79 = (bf16[192,1536]{1,0:T(8,128)(2,1)S(1)}, bf16[192,1536]{1,0:T(8,128)(2,1)S(1)}, u32[]{:S(2)}, u32[]{:S(2)}) collective-permute-start(bf16[192,1536]{1,0:T(8,128)(2,1)S(1)} %copy-done.36), channel_id=1, source_target_pairs={{0,1},{1,0},{2,3},{3,2},{4,5},{5,4},{6,7},{7,6},{8,9},{9,8},{10,11... | collective-permute-start | bytes 1769480 | tf_op jit(solution)/shard_map/ppermute | solution.py:1016
  645.5 19.6 %collective-permute-start.81 = (bf16[192,1536]{1,0:T(8,128)(2,1)S(1)}, bf16[192,1536]{1,0:T(8,128)(2,1)S(1)}, u32[]{:S(2)}, u32[]{:S(2)}) collective-permute-start(bf16[192,1536]{1,0:T(8,128)(2,1)S(1)} %collective-permute-done.80.refs_3_), channel_id=1, source_target_pairs={{0,1},{1,0},{2,3},{3,2},{4,5},{5,4},{6,7},{7,6},{8,9},{9,8},{10,11... | collective-permute-start | bytes 1769480 | tf_op jit(solution)/shard_map/ppermute | solution.py:1016
  647.3 23.6 %collective-permute-start.76 = (bf16[192,3072]{1,0:T(8,128)(2,1)S(1)}, bf16[192,3072]{1,0:T(8,128)(2,1)S(1)}, u32[]{:S(2)}, u32[]{:S(2)}) collective-permute-start(bf16[192,3072]{1,0:T(8,128)(2,1)S(1)} %pad_maximum_fusion.refs_1_), channel_id=1, source_target_pairs={{0,1},{1,0},{2,3},{3,2},{4,5},{5,4},{6,7},{7,6},{8,9},{9,8},{10,11... | collective-permute-start | bytes 3538952 | tf_op jit(solution)/shard_map/ppermute | solution.py:1016
  648.6 22.2 %collective-permute-start.78 = (bf16[192,3072]{1,0:T(8,128)(2,1)S(1)}, bf16[192,3072]{1,0:T(8,128)(2,1)S(1)}, u32[]{:S(2)}, u32[]{:S(2)}) collective-permute-start(bf16[192,3072]{1,0:T(8,128)(2,1)S(1)} %collective-permute-done.77.refs_3_), channel_id=1, source_target_pairs={{0,1},{1,0},{2,3},{3,2},{4,5},{5,4},{6,7},{7,6},{8,9},{9,8},{10,11... | collective-permute-start | bytes 3538952 | tf_op jit(solution)/shard_map/ppermute | solution.py:1016
  (144 other events, 2562.0 us)
Sparse Core Ops, SparseCore 0:
  316.6 115.1 reduce-scatter.1

commit v4 on v3

--- a/solution.py
+++ b/solution.py
@@ -1323,12 +1323,12 @@
         table, base, ring_fs, ring_bs, rows_m, wout, q, k, v, cosine, sine, width
     )
     shed.step(da)
+    half_f, half_b, gout = attention_grads(
+        table, base, a_all, rows_b, rows_m, heads, dqkv, width, n
+    )
     da_part = scatter_parts([da])
-    da_near, da_hop = scatter_near(da_part, back_out)
+    da_near, da_hop = scatter_near(da_part, back_out, gout)
     da_cross = swap(da_hop, 2)
-    half_f, half_b, gout = attention_grads(
-        table, base, a_all, rows_b, rows_m, after(heads, da_hop), dqkv, width, n
-    )
     gout = after(gout, da_cross)
     pieces = [gout[0]] + [swap(gout[kk], kk) for kk in range(1, MEMBERS)]
     full_f, full_b = pack_out_grads(table, base, pieces, half_f, half_b)

time: 744 us -> 737 us (level)
  starting transfers between devices: 204 us -> 186 us
  waiting for transfers between devices: 196 us -> 209 us
    ppermute x14, starting transfers between devices: 17.4 us -> 3.35 us  [step(): self.bs.append(lax.ppermute(after(self.bs[-1], *deps), 'dp', back))]
    ppermute x14, waiting for transfers between devices: 28.7 us -> 38 us  [step(): b = lax.ppermute(after(self.sums[1], *deps), 'dp', back)]
  transfers between devices with their start and end apart: 100 -> 100, of which waited for: 37 -> 40; matrix products, arithmetic and copies ran while one was open for 12% -> 12% of each run, Pallas kernels for 27% -> 27%
where the time goes in v4:
time: 737 us; the launch traced here: 729 us
  Pallas kernels  209 us (28%)
  waiting for transfers between devices  209 us (28%)
  starting transfers between devices  186 us (25%)
  other arithmetic  69.4 us (9%)
  local copies, waits for them, and re-layouts  34 us (5%)
  between operations  20.3 us (3%)
    ppermute x14, waiting for transfers between devices, step(): self.fs.append(lax.ppermute(after(self.fs[-1], *deps), 'dp', ahead))  88.4 us
    pallas_call x2, Pallas kernels, expert_kernel(): pl.pallas_call(kernel, grid=(tiles + cuts,), out_shape=(jax.ShapeDtypeStr...  85 us
    ppermute x39, starting transfers between devices, swap(): return lax.ppermute(values, 'seq', [(i, i ^ bits) for i in range(MEMBERS)])  71.6 us
    ppermute x39, waiting for transfers between devices, swap(): return lax.ppermute(values, 'seq', [(i, i ^ bits) for i in range(MEMBERS)])  44.8 us
    ppermute x14, starting transfers between devices, step(): self.fs.append(lax.ppermute(after(self.fs[-1], *deps), 'dp', ahead))  40.2 us
    pallas_call x1, Pallas kernels, attention_backward(): pl.pallas_call(kernel, out_shape=(jax.ShapeDtypeStruct((MEMBERS, nt, 32,...  39.1 us
    ppermute x14, waiting for transfers between devices, step(): b = lax.ppermute(after(self.sums[1], *deps), 'dp', back)  38 us
    convert_element_type x28, other arithmetic, step(): (got.astype(F32) + mine.astype(F32)).astype(BF)  32.3 us
  transfers between devices with their start and end apart: 100, of which 40 were waited for; matrix products, arithmetic and copies ran while one was open for 12% of the time, Pallas kernels for 27%

profile of v4, /device:TPU:1, one launch (start us, length us, event | category | flops | bytes accessed | tf_op | source)
XLA Modules:
  0.0 729.2 jit_solution(6236046069820019538)
XLA Ops:
  7.2 3.4 pick.1
  10.6 6.5 all-to-all-start
  25.8 4.2 pick_marked.1
  30.1 24.3 %collective-permute-done.refs_2_ = bf16[192,1408]{1,0:T(8,128)(2,1)S(1)} collective-permute-done((bf16[192,1408]{1,0:T(8,128)(2,1)S(1)}, bf16[192,1408]{1,0:T(8,128)(2,1)S(1)}, u32[]{:S(2)}, u32[]{:S(2)}) %collective-permute-start) | collective-permute-done | bytes 540704 | tf_op jit(solution)/shard_map/ppermute | solution.py:1155
  54.4 10.8 %collective-permute-start.1 = (bf16[192,1408]{1,0:T(8,128)(2,1)S(1)}, bf16[192,1408]{1,0:T(8,128)(2,1)S(1)}, u32[]{:S(2)}, u32[]{:S(2)}) collective-permute-start(bf16[192,1408]{1,0:T(8,128)(2,1)S(1)} %collective-permute-done.refs_2_), channel_id=1, source_target_pairs={{0,8},{8,16},{16,24},{24,28},{28,20},{20,12},{12,4},{4,0},{1,9},{9... | collective-permute-start | bytes 1622024 | tf_op jit(solution)/shard_map/ppermute | solution.py:1155
  82.7 6.0 collective-permute-done.2.refs_4_
  94.6 5.6 collective-permute-done.3.refs_5_
  102.5 8.5 %collective-permute-done.5.refs_6_ = bf16[192,1408]{1,0:T(8,128)(2,1)S(1)} collective-permute-done((bf16[192,1408]{1,0:T(8,128)(2,1)S(1)}, bf16[192,1408]{1,0:T(8,128)(2,1)S(1)}, u32[]{:S(2)}, u32[]{:S(2)}) %collective-permute-start.5) | collective-permute-done | bytes 540704 | tf_op jit(solution)/shard_map/ppermute | solution.py:1155
  113.2 8.5 %collective-permute-done.6.refs_7_ = bf16[192,1408]{1,0:T(8,128)(2,1)S(1)} collective-permute-done((bf16[192,1408]{1,0:T(8,128)(2,1)S(1)}, bf16[192,1408]{1,0:T(8,128)(2,1)S(1)}, u32[]{:S(2)}, u32[]{:S(2)}) %collective-permute-start.6) | collective-permute-done | bytes 540704 | tf_op jit(solution)/shard_map/ppermute | solution.py:1155
  125.2 7.6 %collective-permute-done.14.refs_16_ = bf16[192,1280]{1,0:T(8,128)(2,1)S(1)} collective-permute-done((bf16[192,1280]{1,0:T(8,128)(2,1)S(1)}, bf16[192,1280]{1,0:T(8,128)(2,1)S(1)}, u32[]{:S(2)}, u32[]{:S(2)}) %collective-permute-start.14) | collective-permute-done | bytes 491552 | tf_op jit(solution)/shard_map/ppermute | solution.py:1156
  132.8 6.7 all-to-all-start.1
  139.5 5.5 collective-permute-start.16
  162.2 23.6 %attention_forward.1 = (bf16[9,128,1536]{2,1,0:T(8,128)(2,1)}, bf16[2,9,384,64]{3,2,1,0:T(8,128)(2,1)}, bf16[2,1152,64]{2,1,0:T(8,128)(2,1)}, bf16[2,1152,64]{2,...) custom-call(s32[42]{0:T(128)S(1)} %concatenate.46.refs_0_.tab, ...), custom_call_target="tpu_custom_call" | custom-call | flops 120000000 | bytes 146800 | tf_op jit(solution)/shard_map/attention_forward/pallas_call | solution.py:423
  188.4 4.1 project_out.1
  196.7 4.8 collective-permute-start.18
  201.6 12.3 %collective-permute-done.18.refs_3_ = bf16[192,1536]{1,0:T(8,128)(2,1)S(1)} collective-permute-done((bf16[192,1536]{1,0:T(8,128)(2,1)}, bf16[192,1536]{1,0:T(8,128)(2,1)S(1)}, u32[]{:S(2)}, u32[]{:S(2)}) %collective-permute-start.18) | collective-permute-done | bytes 589856 | tf_op jit(solution)/shard_map/ppermute | solution.py:1155
  221.4 7.2 collective-permute-done.30.refs_4_
  230.3 10.3 %collective-permute-done.35.refs_5_ = bf16[192,1536]{1,0:T(8,128)(2,1)S(1)} collective-permute-done((bf16[192,1536]{1,0:T(8,128)(2,1)S(1)}, bf16[192,1536]{1,0:T(8,128)(2,1)S(1)}, u32[]{:S(2)}, u32[]{:S(2)}) %collective-permute-start.35) | collective-permute-done | bytes 589856 | tf_op jit(solution)/shard_map/ppermute | solution.py:1155
  240.6 4.0 collective-permute-start.36
  244.8 4.2 collective-permute-start.27
  249.0 4.5 collective-permute-done.36.refs_6_
  256.0 6.5 collective-permute-start.32
  266.4 4.4 collective-permute-start.29
  277.1 30.8 %expert.2 = (bf16[4,9,32,1664]{3,2,1,0:T(8,128)(2,1)}, bf16[4,9,32,1536]{3,2,1,0:T(8,128)(2,1)}, bf16[1536,1536]{1,0:T(8,128)(2,1)}) custom-call(s32[42]{0:T(128)} %copy-done.39, bf16[192,1408]{1,0:T(8,128)(2,1)} %copy-done.2, bf16[192,1408]{1,0:T(8,128)(2,1)} %copy-done.6, bf16[192,1408]{1,0:T(8,128)(2,1)} %copy-done.8, bf16[192,1408]{1,0:T(8,128)(2,1)} %copy-done.44, ...), custom_call_target="tpu_custom_call" | custom-call | flops 170000000 | bytes 272629 | tf_op jit(solution)/shard_map/expert/pallas_call | solution.py:917
  307.9 54.2 %expert.3 = (bf16[4,9,32,1664]{3,2,1,0:T(8,128)(2,1)}, bf16[4,9,32,1536]{3,2,1,0:T(8,128)(2,1)}, bf16[8,192,1536]{2,1,0:T(8,128)(2,1)}, bf16[8,192,1536]{2,1,0:T(8,128)(2,1)}) custom-call(s32[42]{0:T(128)} %copy-done.39, bf16[192,1536]{1,0:T(8,128)(2,1)} %get-tuple-element.101.refs_1_, bf16[192,1536]{1,0:T(8,128)(2,1)} %collective-permute-done.15.refs_2_, ...), custom_call_target="tpu_custom_call" | custom-call | flops 340000000 | bytes 419430 | tf_op jit(solution)/shard_map/expert/pallas_call | solution.py:917
  373.9 8.9 %collective-permute-done.50 = bf16[192,1536]{1,0:T(8,128)(2,1)S(1)} collective-permute-done((bf16[192,1536]{1,0:T(8,128)(2,1)S(1)}, bf16[192,1536]{1,0:T(8,128)(2,1)S(1)}, u32[]{:S(2)}, u32[]{:S(2)}) %collective-permute-start.50) | collective-permute-done | bytes 589856 | tf_op jit(solution)/shard_map/ppermute | solution.py:1173
  385.6 8.6 %collective-permute-done.45 = bf16[9,32,1664]{2,1,0:T(8,128)(2,1)S(1)} collective-permute-done((bf16[9,32,1664]{2,1,0:T(8,128)(2,1)S(1)}, bf16[9,32,1664]{2,1,0:T(8,128)(2,1)S(1)}, u32[]{:S(2)}, u32[]{:S(2)}) %collective-permute-start.45) | collective-permute-done | bytes 958496 | tf_op jit(solution)/shard_map/ppermute | solution.py:1016
  403.9 4.9 collective-permute-done.51
  413.5 3.9 collective-permute-done.55
  422.8 6.1 collective-permute-done.48.refs_19_.refs_7_
  431.6 4.3 collective-permute-done.56
  452.9 15.5 %all-to-all-start.2 = ((bf16[16,32,1536]{2,1,0:T(8,128)(2,1)}), bf16[16,32,1536]{2,1,0:T(8,128)(2,1)}, u32[]{:S(2)}, u32[]{:S(2)}) async-start(bf16[16,32,1536]{2,1,0:T(8,128)(2,1)} %spread_rows.2), calls=%async_computation.2 | async-start | bytes 3145728 | tf_op jit(solution)/shard_map/all_to_all | solution.py:1318
  473.8 39.1 %attention_backward.1 = (bf16[4,9,32,1536]{3,2,1,0:T(8,128)(2,1)}, bf16[1152,640]{1,0:T(8,128)(2,1)}) custom-call(s32[42]{0:T(128)} %copy-done.39, bf16[192,1408]{1,0:T(8,128)(2,1)} %copy-done.2, bf16[192,1408]{1,0:T(8,128)(2,1)} %copy-done.6, bf16[192,1408]{1,0:T(8,128)(2,1)} %copy-done.8, bf16[192,1408]{1,0:T(8,128)(2,1)} %copy-done.44, ...), custom_call_target="tpu_custom_call" | custom-call | flops 200000000 | bytes 167772 | tf_op jit(solution)/shard_map/attention_backward/pallas_call | solution.py:573
  514.8 10.3 %collective-permute-done.73 = bf16[192,1536]{1,0:T(8,128)(2,1)} collective-permute-done((bf16[192,1536]{1,0:T(8,128)(2,1)S(1)}, bf16[192,1536]{1,0:T(8,128)(2,1)}, u32[]{:S(2)}, u32[]{:S(2)}) %collective-permute-start.73) | collective-permute-done | bytes 589856 | tf_op jit(solution)/shard_map/ppermute | solution.py:1174
  533.3 12.1 %attention_grads.1 = (bf16[8,192,512]{2,1,0:T(8,128)(2,1)}, bf16[8,192,640]{2,1,0:T(8,128)(2,1)}, bf16[4,384,384]{2,1,0:T(8,128)(2,1)}) custom-call(s32[42]{0:T(128)S(1)} %copy-done.40, bf16[9,32,1536]{2,1,0:T(8,128)(2,1)S(1)} %copy-done.1, bf16[9,32,1536]{2,1,0:T(8,128)(2,1)S(1)} %copy-done.15, bf16[9,32,1536]{2,1,0:T(8,128)(2,1)S(1)} %copy-done.13, ...), custom_call_target="tpu_custom_call" | custom-call | flops 40000000 | bytes 167772 | tf_op jit(solution)/shard_map/attention_grads/pallas_call | solution.py:638
  545.4 4.3 collective-permute-start.61
  555.7 10.0 %collective-permute-done.75 = bf16[192,1536]{1,0:T(8,128)(2,1)S(1)} collective-permute-done((bf16[192,1536]{1,0:T(8,128)(2,1)S(1)}, bf16[192,1536]{1,0:T(8,128)(2,1)S(1)}, u32[]{:S(2)}, u32[]{:S(2)}) %collective-permute-start.75) | collective-permute-done | bytes 589856 | tf_op jit(solution)/shard_map/ppermute | solution.py:1174
  570.6 4.0 collective-permute-done.62
  578.9 3.6 collective-permute-start.63
  589.6 5.3 all-to-all-start.3
  596.1 10.2 %collective-permute-done.64.refs_3_ = bf16[384,384]{1,0:T(8,128)(2,1)} collective-permute-done((bf16[384,384]{1,0:T(8,128)(2,1)}, bf16[384,384]{1,0:T(8,128)(2,1)}, u32[]{:S(2)}, u32[]{:S(2)}) %collective-permute-start.64) | collective-permute-done | bytes 294944 | tf_op jit(solution)/shard_map/ppermute | solution.py:1016
  606.3 9.5 %collective-permute-done.65.refs_4_ = bf16[384,384]{1,0:T(8,128)(2,1)} collective-permute-done((bf16[384,384]{1,0:T(8,128)(2,1)}, bf16[384,384]{1,0:T(8,128)(2,1)}, u32[]{:S(2)}, u32[]{:S(2)}) %collective-permute-start.65) | collective-permute-done | bytes 294944 | tf_op jit(solution)/shard_map/ppermute | solution.py:1016
  628.1 9.0 %collective-permute-start.70 = (bf16[192,512]{1,0:T(8,128)(2,1)S(1)}, bf16[192,512]{1,0:T(8,128)(2,1)S(1)}, u32[]{:S(2)}, u32[]{:S(2)}) collective-permute-start(bf16[192,512]{1,0:T(8,128)(2,1)S(1)} %fusion.49), channel_id=1, source_target_pairs={{0,8},{8,16},{16,24},{24,28},{28,20},{20,12},{12,4},{4,0},{1,9},{9... | collective-permute-start | bytes 589832 | tf_op jit(solution)/shard_map/ppermute | solution.py:1173
  658.7 4.7 place_experts.2
  664.5 7.6 %place_experts.3 = (f32[12,192,1536]{2,1,0:T(8,128)}, f32[192,128]{1,0:T(8,128)S(1)}) custom-call(s32[4]{0:T(128)S(1)} %iota_xor_fusion.refs_0_, bf16[192,3072]{1,0:T(8,128)(2,1)S(1)} %pad_maximum_fusion.refs_1_, bf16[192,3072]{1,0:T(8,128)(2,1)S(1)} %collective-permute-done.76.refs_2_, ...), custom_call_target="tpu_custom_call", output_to_operand_aliasing={{0}: (6, {})} | custom-call | bytes 141557 | tf_op jit(solution)/shard_map/place_experts/pallas_call | solution.py:246
  689.6 3.8 collective-permute-done.84
  698.8 8.3 %collective-permute-start.92 = (bf16[192,1024]{1,0:T(8,128)(2,1)S(1)}, bf16[192,1024]{1,0:T(8,128)(2,1)S(1)}, u32[]{:S(2)}, u32[]{:S(2)}) collective-permute-start(bf16[192,1024]{1,0:T(8,128)(2,1)S(1)} %pad_maximum_fusion.7.refs_1_), channel_id=1, source_target_pairs={{0,1},{1,0},{2,3},{3,2},{4,5},{5,4},{6,7},{7,6},{8,9},{9,8},{10,11... | collective-permute-start | bytes 1179656 | tf_op jit(solution)/shard_map/ppermute | solution.py:1016
  707.1 6.2 collective-permute-start.94
  (470 shorter events, 240.1 us)
Async XLA Ops:
  10.6 61.0 %all-to-all-start = ((bf16[16,32,1536]{2,1,0:T(8,128)(2,1)}), bf16[16,32,1536]{2,1,0:T(8,128)(2,1)}, u32[]{:S(2)}, u32[]{:S(2)}) async-start(bf16[16,32,1536]{2,1,0:T(8,128)(2,1)} %pick.1), calls=%async_computation | async-start | bytes 3145728 | tf_op jit(solution)/shard_map/all_to_all | solution.py:1083
  22.3 32.1 %collective-permute-start = (bf16[192,1408]{1,0:T(8,128)(2,1)S(1)}, bf16[192,1408]{1,0:T(8,128)(2,1)S(1)}, u32[]{:S(2)}, u32[]{:S(2)}) collective-permute-start(bf16[192,1408]{1,0:T(8,128)(2,1)S(1)} %concatenate.41.refs_1_), channel_id=1, source_target_pairs={{0,8},{8,16},{16,24},{24,28},{28,20},{20,12},{12,4},{4,0},{1,9},{9... | collective-permute-start | bytes 1622024 | tf_op jit(solution)/shard_map/ppermute | solution.py:1155
  24.8 40.4 %collective-permute-start.8 = (bf16[192,1280]{1,0:T(8,128)(2,1)S(1)}, bf16[192,1280]{1,0:T(8,128)(2,1)S(1)}, u32[]{:S(2)}, u32[]{:S(2)}) collective-permute-start(bf16[192,1280]{1,0:T(8,128)(2,1)S(1)} %pad_maximum_fusion.6.refs_9_), channel_id=1, source_target_pairs={{8,0},{16,8},{24,16},{28,24},{20,28},{12,20},{4,12},{0,4},{9,1},{1... | collective-permute-start | bytes 1474568 | tf_op jit(solution)/shard_map/ppermute | solution.py:1156
  54.4 21.9 %collective-permute-start.1 = (bf16[192,1408]{1,0:T(8,128)(2,1)S(1)}, bf16[192,1408]{1,0:T(8,128)(2,1)S(1)}, u32[]{:S(2)}, u32[]{:S(2)}) collective-permute-start(bf16[192,1408]{1,0:T(8,128)(2,1)S(1)} %collective-permute-done.refs_2_), channel_id=1, source_target_pairs={{0,8},{8,16},{16,24},{24,28},{28,20},{20,12},{12,4},{4,0},{1,9},{9... | collective-permute-start | bytes 1622024 | tf_op jit(solution)/shard_map/ppermute | solution.py:1155
  73.9 20.7 %collective-permute-start.4 = (bf16[9,32,1536]{2,1,0:T(8,128)(2,1)}, bf16[9,32,1536]{2,1,0:T(8,128)(2,1)S(1)}, u32[]{:S(2)}, u32[]{:S(2)}) collective-permute-start(bf16[9,32,1536]{2,1,0:T(8,128)(2,1)} %take_rows.2.refs_17_), channel_id=1, source_target_pairs={{0,2},{1,3},{2,0},{3,1},{4,6},{5,7},{6,4},{7,5},{8,10},{9,11},{10,... | collective-permute-start | bytes 2654216 | tf_op jit(solution)/shard_map/ppermute | solution.py:1016
  132.8 53.0 %all-to-all-start.1 = ((bf16[16,32,1664]{2,1,0:T(8,128)(2,1)}), bf16[16,32,1664]{2,1,0:T(8,128)(2,1)}, u32[]{:S(2)}, u32[]{:S(2)}) async-start(bf16[16,32,1664]{2,1,0:T(8,128)(2,1)} %pick_marked.1), calls=%async_computation.1 | async-start | bytes 3407872 | tf_op jit(solution)/shard_map/all_to_all | solution.py:1213
  139.5 333.3 %reduce-scatter.2.cloned.1.call-start = ((), (), s32[]{:S(2)}) async-start(), calls=%async_computation.5 | async-start | bytes 5308416 | tf_op jit(solution)/shard_map/reduce_scatter | solution.py:1264
  145.8 42.5 %collective-permute-start.15 = (bf16[192,1536]{1,0:T(8,128)(2,1)}, bf16[192,1536]{1,0:T(8,128)(2,1)}, u32[]{:S(2)}, u32[]{:S(2)}) collective-permute-start(bf16[192,1536]{1,0:T(8,128)(2,1)} %get-tuple-element.101.refs_1_), channel_id=1, source_target_pairs={{0,8},{8,16},{16,24},{24,28},{28,20},{20,12},{12,4},{4,0},{1,9},{9... | collective-permute-start | bytes 1769480 | tf_op jit(solution)/shard_map/ppermute | solution.py:1155
  147.4 40.9 %collective-permute-start.19 = (bf16[192,1536]{1,0:T(8,128)(2,1)}, bf16[192,1536]{1,0:T(8,128)(2,1)}, u32[]{:S(2)}, u32[]{:S(2)}) collective-permute-start(bf16[192,1536]{1,0:T(8,128)(2,1)} %get-tuple-element.105.refs_9_), channel_id=1, source_target_pairs={{8,0},{16,8},{24,16},{28,24},{20,28},{12,20},{4,12},{0,4},{9,1},{1... | collective-permute-start | bytes 1769480 | tf_op jit(solution)/shard_map/ppermute | solution.py:1156
  153.7 34.6 %collective-permute-start.21 = (bf16[384,384]{1,0:T(8,128)(2,1)}, bf16[384,384]{1,0:T(8,128)(2,1)}, u32[]{:S(2)}, u32[]{:S(2)}) collective-permute-start(bf16[384,384]{1,0:T(8,128)(2,1)} %get-tuple-element.230), channel_id=1, source_target_pairs={{0,1},{1,0},{2,3},{3,2},{4,5},{5,4},{6,7},{7,6},{8,9},{9,8},{10,11... | collective-permute-start | bytes 884744 | tf_op jit(solution)/shard_map/ppermute | solution.py:1016
  154.5 33.8 %collective-permute-start.22 = (bf16[384,384]{1,0:T(8,128)(2,1)}, bf16[384,384]{1,0:T(8,128)(2,1)}, u32[]{:S(2)}, u32[]{:S(2)}) collective-permute-start(bf16[384,384]{1,0:T(8,128)(2,1)} %get-tuple-element.229), channel_id=1, source_target_pairs={{0,2},{1,3},{2,0},{3,1},{4,6},{5,7},{6,4},{7,5},{8,10},{9,11},{10,... | collective-permute-start | bytes 884744 | tf_op jit(solution)/shard_map/ppermute | solution.py:1016
  155.7 32.6 %collective-permute-start.23 = (bf16[384,384]{1,0:T(8,128)(2,1)}, bf16[384,384]{1,0:T(8,128)(2,1)}, u32[]{:S(2)}, u32[]{:S(2)}) collective-permute-start(bf16[384,384]{1,0:T(8,128)(2,1)} %get-tuple-element.228), channel_id=1, source_target_pairs={{0,3},{1,2},{2,1},{3,0},{4,7},{5,6},{6,5},{7,4},{8,11},{9,10},{10,... | collective-permute-start | bytes 884744 | tf_op jit(solution)/shard_map/ppermute | solution.py:1016
  192.9 24.1 %collective-permute-start.24 = (bf16[9,32,1536]{2,1,0:T(8,128)(2,1)S(1)}, bf16[9,32,1536]{2,1,0:T(8,128)(2,1)S(1)}, u32[]{:S(2)}, u32[]{:S(2)}) collective-permute-start(bf16[9,32,1536]{2,1,0:T(8,128)(2,1)S(1)} %get-tuple-element.214), channel_id=1, source_target_pairs={{0,1},{1,0},{2,3},{3,2},{4,5},{5,4},{6,7},{7,6},{8,9},{9,8},{10,11... | collective-permute-start | bytes 2654216 | tf_op jit(solution)/shard_map/ppermute | solution.py:1016
  195.4 21.6 %collective-permute-start.26 = (bf16[9,32,1536]{2,1,0:T(8,128)(2,1)S(1)}, bf16[9,32,1536]{2,1,0:T(8,128)(2,1)S(1)}, u32[]{:S(2)}, u32[]{:S(2)}) collective-permute-start(bf16[9,32,1536]{2,1,0:T(8,128)(2,1)S(1)} %fusion.6), channel_id=1, source_target_pairs={{0,2},{1,3},{2,0},{3,1},{4,6},{5,7},{6,4},{7,5},{8,10},{9,11},{10,... | collective-permute-start | bytes 2654216 | tf_op jit(solution)/shard_map/ppermute | solution.py:1016
  220.6 20.0 %collective-permute-start.28 = (bf16[9,32,1536]{2,1,0:T(8,128)(2,1)S(1)}, bf16[9,32,1536]{2,1,0:T(8,128)(2,1)S(1)}, u32[]{:S(2)}, u32[]{:S(2)}) collective-permute-start(bf16[9,32,1536]{2,1,0:T(8,128)(2,1)S(1)} %multiply_convert_fusion.refs_17_.refs_1_), channel_id=1, source_target_pairs={{0,2},{1,3},{2,0},{3,1},{4,6},{5,7},{6,4},{7,5},{8,10},{9,11},{10,... | collective-permute-start | bytes 2654216 | tf_op jit(solution)/shard_map/ppermute | solution.py:1016
  230.1 32.4 %collective-permute-start.33 = (bf16[9,32,1664]{2,1,0:T(8,128)(2,1)}, bf16[9,32,1664]{2,1,0:T(8,128)(2,1)}, u32[]{:S(2)}, u32[]{:S(2)}) collective-permute-start(bf16[9,32,1664]{2,1,0:T(8,128)(2,1)} %take_rows.3.refs_21_), channel_id=1, source_target_pairs={{0,2},{1,3},{2,0},{3,1},{4,6},{5,7},{6,4},{7,5},{8,10},{9,11},{10,... | collective-permute-start | bytes 2875400 | tf_op jit(solution)/shard_map/ppermute | solution.py:1016
  244.8 29.0 %collective-permute-start.27 = (bf16[9,32,1536]{2,1,0:T(8,128)(2,1)S(1)}, bf16[9,32,1536]{2,1,0:T(8,128)(2,1)S(1)}, u32[]{:S(2)}, u32[]{:S(2)}) collective-permute-start(bf16[9,32,1536]{2,1,0:T(8,128)(2,1)S(1)} %multiply_convert_fusion.refs_17_.refs_1_), channel_id=1, source_target_pairs={{0,1},{1,0},{2,3},{3,2},{4,5},{5,4},{6,7},{7,6},{8,9},{9,8},{10,11... | collective-permute-start | bytes 2654216 | tf_op jit(solution)/shard_map/ppermute | solution.py:1016
  256.0 21.0 %collective-permute-start.32 = (bf16[9,32,1664]{2,1,0:T(8,128)(2,1)}, bf16[9,32,1664]{2,1,0:T(8,128)(2,1)}, u32[]{:S(2)}, u32[]{:S(2)}) collective-permute-start(bf16[9,32,1664]{2,1,0:T(8,128)(2,1)} %take_rows.3.refs_21_), channel_id=1, source_target_pairs={{0,1},{1,0},{2,3},{3,2},{4,5},{5,4},{6,7},{7,6},{8,9},{9,8},{10,11... | collective-permute-start | bytes 2875400 | tf_op jit(solution)/shard_map/ppermute | solution.py:1016
  271.4 36.5 %collective-permute-start.38 = (bf16[192,1536]{1,0:T(8,128)(2,1)}, bf16[192,1536]{1,0:T(8,128)(2,1)}, u32[]{:S(2)}, u32[]{:S(2)}) collective-permute-start(bf16[192,1536]{1,0:T(8,128)(2,1)} %collective-permute-done.37.refs_7_), channel_id=1, source_target_pairs={{0,8},{8,16},{16,24},{24,28},{28,20},{20,12},{12,4},{4,0},{1,9},{9... | collective-permute-start | bytes 1769480 | tf_op jit(solution)/shard_map/ppermute | solution.py:1155
  273.8 34.2 %collective-permute-start.42 = (bf16[192,1536]{1,0:T(8,128)(2,1)}, bf16[192,1536]{1,0:T(8,128)(2,1)}, u32[]{:S(2)}, u32[]{:S(2)}) collective-permute-start(bf16[192,1536]{1,0:T(8,128)(2,1)} %collective-permute-done.41.refs_15_), channel_id=1, source_target_pairs={{8,0},{16,8},{24,16},{28,24},{20,28},{12,20},{4,12},{0,4},{9,1},{1... | collective-permute-start | bytes 1769480 | tf_op jit(solution)/shard_map/ppermute | solution.py:1156
  366.2 19.4 %collective-permute-start.43 = (bf16[9,32,1664]{2,1,0:T(8,128)(2,1)S(1)}, bf16[9,32,1664]{2,1,0:T(8,128)(2,1)S(1)}, u32[]{:S(2)}, u32[]{:S(2)}) collective-permute-start(bf16[9,32,1664]{2,1,0:T(8,128)(2,1)S(1)} %get-tuple-element.208), channel_id=1, source_target_pairs={{0,1},{1,0},{2,3},{3,2},{4,5},{5,4},{6,7},{7,6},{8,9},{9,8},{10,11... | collective-permute-start | bytes 2875400 | tf_op jit(solution)/shard_map/ppermute | solution.py:1016
  372.6 21.6 %collective-permute-start.45 = (bf16[9,32,1664]{2,1,0:T(8,128)(2,1)S(1)}, bf16[9,32,1664]{2,1,0:T(8,128)(2,1)S(1)}, u32[]{:S(2)}, u32[]{:S(2)}) collective-permute-start(bf16[9,32,1664]{2,1,0:T(8,128)(2,1)S(1)} %fusion.1), channel_id=1, source_target_pairs={{0,2},{1,3},{2,0},{3,1},{4,6},{5,7},{6,4},{7,5},{8,10},{9,11},{10,... | collective-permute-start | bytes 2875400 | tf_op jit(solution)/shard_map/ppermute | solution.py:1016
  384.1 24.7 %collective-permute-start.51 = (bf16[192,1536]{1,0:T(8,128)(2,1)S(1)}, bf16[192,1536]{1,0:T(8,128)(2,1)S(1)}, u32[]{:S(2)}, u32[]{:S(2)}) collective-permute-start(bf16[192,1536]{1,0:T(8,128)(2,1)S(1)} %fusion.31), channel_id=1, source_target_pairs={{0,8},{8,16},{16,24},{24,28},{28,20},{20,12},{12,4},{4,0},{1,9},{9... | collective-permute-start | bytes 1769480 | tf_op jit(solution)/shard_map/ppermute | solution.py:1173
  384.2 33.3 %collective-permute-start.55 = (bf16[192,1536]{1,0:T(8,128)(2,1)S(1)}, bf16[192,1536]{1,0:T(8,128)(2,1)S(1)}, u32[]{:S(2)}, u32[]{:S(2)}) collective-permute-start(bf16[192,1536]{1,0:T(8,128)(2,1)S(1)} %fusion.27), channel_id=1, source_target_pairs={{8,0},{16,8},{24,16},{28,24},{20,28},{12,20},{4,12},{0,4},{9,1},{1... | collective-permute-start | bytes 1769480 | tf_op jit(solution)/shard_map/ppermute | solution.py:1174
  401.7 18.1 %collective-permute-start.47 = (bf16[9,32,1536]{2,1,0:T(8,128)(2,1)S(1)}, bf16[9,32,1536]{2,1,0:T(8,128)(2,1)S(1)}, u32[]{:S(2)}, u32[]{:S(2)}) collective-permute-start(bf16[9,32,1536]{2,1,0:T(8,128)(2,1)S(1)} %get-tuple-element.125), channel_id=1, source_target_pairs={{0,1},{1,0},{2,3},{3,2},{4,5},{5,4},{6,7},{7,6},{8,9},{9,8},{10,11... | collective-permute-start | bytes 2654216 | tf_op jit(solution)/shard_map/ppermute | solution.py:1016
  408.9 20.0 %collective-permute-start.48 = (bf16[9,32,1664]{2,1,0:T(8,128)(2,1)S(1)}, bf16[9,32,1664]{2,1,0:T(8,128)(2,1)S(1)}, u32[]{:S(2)}, u32[]{:S(2)}) collective-permute-start(bf16[9,32,1664]{2,1,0:T(8,128)(2,1)S(1)} %bitcast.218), channel_id=1, source_target_pairs={{0,2},{1,3},{2,0},{3,1},{4,6},{5,7},{6,4},{7,5},{8,10},{9,11},{10,... | collective-permute-start | bytes 2875400 | tf_op jit(solution)/shard_map/ppermute | solution.py:1016
  410.4 21.1 %collective-permute-start.52 = (bf16[192,1536]{1,0:T(8,128)(2,1)S(1)}, bf16[192,1536]{1,0:T(8,128)(2,1)S(1)}, u32[]{:S(2)}, u32[]{:S(2)}) collective-permute-start(bf16[192,1536]{1,0:T(8,128)(2,1)S(1)} %fusion.30), channel_id=1, source_target_pairs={{0,8},{8,16},{16,24},{24,28},{28,20},{20,12},{12,4},{4,0},{1,9},{9... | collective-permute-start | bytes 1769480 | tf_op jit(solution)/shard_map/ppermute | solution.py:1173
  418.7 54.2 %collective-permute-start.58 = (bf16[9,32,1664]{2,1,0:T(8,128)(2,1)S(1)}, bf16[9,32,1664]{2,1,0:T(8,128)(2,1)S(1)}, u32[]{:S(2)}, u32[]{:S(2)}) collective-permute-start(bf16[9,32,1664]{2,1,0:T(8,128)(2,1)S(1)} %bitcast.219), channel_id=1, source_target_pairs={{0,1},{1,0},{2,3},{3,2},{4,5},{5,4},{6,7},{7,6},{8,9},{9,8},{10,11... | collective-permute-start | bytes 2875400 | tf_op jit(solution)/shard_map/ppermute | solution.py:1016
  419.7 23.0 %collective-permute-start.46 = (bf16[9,32,1536]{2,1,0:T(8,128)(2,1)S(1)}, bf16[9,32,1536]{2,1,0:T(8,128)(2,1)S(1)}, u32[]{:S(2)}, u32[]{:S(2)}) collective-permute-start(bf16[9,32,1536]{2,1,0:T(8,128)(2,1)S(1)} %get-tuple-element.124), channel_id=1, source_target_pairs={{0,1},{1,0},{2,3},{3,2},{4,5},{5,4},{6,7},{7,6},{8,9},{9,8},{10,11... | collective-permute-start | bytes 2654216 | tf_op jit(solution)/shard_map/ppermute | solution.py:1016
  428.9 18.3 %collective-permute-start.49 = (bf16[9,32,1536]{2,1,0:T(8,128)(2,1)S(1)}, bf16[9,32,1536]{2,1,0:T(8,128)(2,1)S(1)}, u32[]{:S(2)}, u32[]{:S(2)}) collective-permute-start(bf16[9,32,1536]{2,1,0:T(8,128)(2,1)S(1)} %fusion.14), channel_id=1, source_target_pairs={{0,2},{1,3},{2,0},{3,1},{4,6},{5,7},{6,4},{7,5},{8,10},{9,11},{10,... | collective-permute-start | bytes 2654216 | tf_op jit(solution)/shard_map/ppermute | solution.py:1016
  437.9 30.4 %collective-permute-start.53 = (bf16[192,1536]{1,0:T(8,128)(2,1)S(1)}, bf16[192,1536]{1,0:T(8,128)(2,1)}, u32[]{:S(2)}, u32[]{:S(2)}) collective-permute-start(bf16[192,1536]{1,0:T(8,128)(2,1)S(1)} %fusion.29), channel_id=1, source_target_pairs={{0,8},{8,16},{16,24},{24,28},{28,20},{20,12},{12,4},{4,0},{1,9},{9... | collective-permute-start | bytes 1769480 | tf_op jit(solution)/shard_map/ppermute | solution.py:1173
  440.1 30.5 %collective-permute-start.57 = (bf16[192,1536]{1,0:T(8,128)(2,1)}, bf16[192,1536]{1,0:T(8,128)(2,1)}, u32[]{:S(2)}, u32[]{:S(2)}) collective-permute-start(bf16[192,1536]{1,0:T(8,128)(2,1)} %fusion.25), channel_id=1, source_target_pairs={{8,0},{16,8},{24,16},{28,24},{20,28},{12,20},{4,12},{0,4},{9,1},{1... | collective-permute-start | bytes 1769480 | tf_op jit(solution)/shard_map/ppermute | solution.py:1174
  442.7 30.2 %collective-permute-start.59 = (bf16[9,32,1664]{2,1,0:T(8,128)(2,1)S(1)}, bf16[9,32,1664]{2,1,0:T(8,128)(2,1)}, u32[]{:S(2)}, u32[]{:S(2)}) collective-permute-start(bf16[9,32,1664]{2,1,0:T(8,128)(2,1)S(1)} %collective-permute-done.48.refs_19_.refs_7_), channel_id=1, source_target_pairs={{0,1},{1,0},{2,3},{3,2},{4,5},{5,4},{6,7},{7,6},{8,9},{9,8},{10,11... | collective-permute-start | bytes 2875400 | tf_op jit(solution)/shard_map/ppermute | solution.py:1016
  452.9 92.4 %all-to-all-start.2 = ((bf16[16,32,1536]{2,1,0:T(8,128)(2,1)}), bf16[16,32,1536]{2,1,0:T(8,128)(2,1)}, u32[]{:S(2)}, u32[]{:S(2)}) async-start(bf16[16,32,1536]{2,1,0:T(8,128)(2,1)} %spread_rows.2), calls=%async_computation.2 | async-start | bytes 3145728 | tf_op jit(solution)/shard_map/all_to_all | solution.py:1318
  526.6 23.1 %collective-permute-start.74 = (bf16[192,1536]{1,0:T(8,128)(2,1)S(1)}, bf16[192,1536]{1,0:T(8,128)(2,1)}, u32[]{:S(2)}, u32[]{:S(2)}) collective-permute-start(bf16[192,1536]{1,0:T(8,128)(2,1)S(1)} %fusion.20), channel_id=1, source_target_pairs={{8,0},{16,8},{24,16},{28,24},{20,28},{12,20},{4,12},{0,4},{9,1},{1... | collective-permute-start | bytes 1769480 | tf_op jit(solution)/shard_map/ppermute | solution.py:1174
  529.9 22.6 %collective-permute-start.67 = (bf16[192,1536]{1,0:T(8,128)(2,1)}, bf16[192,1536]{1,0:T(8,128)(2,1)}, u32[]{:S(2)}, u32[]{:S(2)}) collective-permute-start(bf16[192,1536]{1,0:T(8,128)(2,1)} %fusion.23), channel_id=1, source_target_pairs={{0,8},{8,16},{16,24},{24,28},{28,20},{20,12},{12,4},{4,0},{1,9},{9... | collective-permute-start | bytes 1769480 | tf_op jit(solution)/shard_map/ppermute | solution.py:1173
  549.6 21.0 %collective-permute-start.60 = (bf16[9,32,1536]{2,1,0:T(8,128)(2,1)}, bf16[9,32,1536]{2,1,0:T(8,128)(2,1)S(1)}, u32[]{:S(2)}, u32[]{:S(2)}) collective-permute-start(bf16[9,32,1536]{2,1,0:T(8,128)(2,1)} %get-tuple-element.144), channel_id=1, source_target_pairs={{0,1},{1,0},{2,3},{3,2},{4,5},{5,4},{6,7},{7,6},{8,9},{9,8},{10,11... | collective-permute-start | bytes 2654216 | tf_op jit(solution)/shard_map/ppermute | solution.py:1016
  554.5 20.1 %collective-permute-start.62 = (bf16[9,32,1536]{2,1,0:T(8,128)(2,1)S(1)}, bf16[9,32,1536]{2,1,0:T(8,128)(2,1)S(1)}, u32[]{:S(2)}, u32[]{:S(2)}) collective-permute-start(bf16[9,32,1536]{2,1,0:T(8,128)(2,1)S(1)} %fusion.4), channel_id=1, source_target_pairs={{0,2},{1,3},{2,0},{3,1},{4,6},{5,7},{6,4},{7,5},{8,10},{9,11},{10,... | collective-permute-start | bytes 2654216 | tf_op jit(solution)/shard_map/ppermute | solution.py:1016
  569.4 72.8 %collective-permute-start.77 = (bf16[192,3072]{1,0:T(8,128)(2,1)S(1)}, bf16[192,3072]{1,0:T(8,128)(2,1)S(1)}, u32[]{:S(2)}, u32[]{:S(2)}) collective-permute-start(bf16[192,3072]{1,0:T(8,128)(2,1)S(1)} %pad_maximum_fusion.refs_1_), channel_id=1, source_target_pairs={{0,2},{1,3},{2,0},{3,1},{4,6},{5,7},{6,4},{7,5},{8,10},{9,11},{10,... | collective-permute-start | bytes 3538952 | tf_op jit(solution)/shard_map/ppermute | solution.py:1016
  578.9 17.2 %collective-permute-start.63 = (bf16[384,384]{1,0:T(8,128)(2,1)}, bf16[384,384]{1,0:T(8,128)(2,1)}, u32[]{:S(2)}, u32[]{:S(2)}) collective-permute-start(bf16[384,384]{1,0:T(8,128)(2,1)} %get-tuple-element.226), channel_id=1, source_target_pairs={{0,1},{1,0},{2,3},{3,2},{4,5},{5,4},{6,7},{7,6},{8,9},{9,8},{10,11... | collective-permute-start | bytes 884744 | tf_op jit(solution)/shard_map/ppermute | solution.py:1016
  582.5 23.8 %collective-permute-start.64 = (bf16[384,384]{1,0:T(8,128)(2,1)}, bf16[384,384]{1,0:T(8,128)(2,1)}, u32[]{:S(2)}, u32[]{:S(2)}) collective-permute-start(bf16[384,384]{1,0:T(8,128)(2,1)} %get-tuple-element.225), channel_id=1, source_target_pairs={{0,2},{1,3},{2,0},{3,1},{4,6},{5,7},{6,4},{7,5},{8,10},{9,11},{10,... | collective-permute-start | bytes 884744 | tf_op jit(solution)/shard_map/ppermute | solution.py:1016
  583.6 32.2 %collective-permute-start.65 = (bf16[384,384]{1,0:T(8,128)(2,1)}, bf16[384,384]{1,0:T(8,128)(2,1)}, u32[]{:S(2)}, u32[]{:S(2)}) collective-permute-start(bf16[384,384]{1,0:T(8,128)(2,1)} %get-tuple-element.224), channel_id=1, source_target_pairs={{0,3},{1,2},{2,1},{3,0},{4,7},{5,6},{6,5},{7,4},{8,11},{9,10},{10,... | collective-permute-start | bytes 884744 | tf_op jit(solution)/shard_map/ppermute | solution.py:1016
  589.6 88.1 %all-to-all-start.3 = ((bf16[16,32,1536]{2,1,0:T(8,128)(2,1)}), bf16[16,32,1536]{2,1,0:T(8,128)(2,1)}, u32[]{:S(2)}, u32[]{:S(2)}) async-start(bf16[16,32,1536]{2,1,0:T(8,128)(2,1)} %spread_rows.3), calls=%async_computation.4 | async-start | bytes 3145728 | tf_op jit(solution)/shard_map/all_to_all | solution.py:1345
  594.9 44.6 %collective-permute-start.80 = (bf16[192,1536]{1,0:T(8,128)(2,1)S(1)}, bf16[192,1536]{1,0:T(8,128)(2,1)S(1)}, u32[]{:S(2)}, u32[]{:S(2)}) collective-permute-start(bf16[192,1536]{1,0:T(8,128)(2,1)S(1)} %copy-done.36), channel_id=1, source_target_pairs={{0,2},{1,3},{2,0},{3,1},{4,6},{5,7},{6,4},{7,5},{8,10},{9,11},{10,... | collective-permute-start | bytes 1769480 | tf_op jit(solution)/shard_map/ppermute | solution.py:1016
  639.0 18.7 %collective-permute-start.79 = (bf16[192,1536]{1,0:T(8,128)(2,1)S(1)}, bf16[192,1536]{1,0:T(8,128)(2,1)S(1)}, u32[]{:S(2)}, u32[]{:S(2)}) collective-permute-start(bf16[192,1536]{1,0:T(8,128)(2,1)S(1)} %copy-done.36), channel_id=1, source_target_pairs={{0,1},{1,0},{2,3},{3,2},{4,5},{5,4},{6,7},{7,6},{8,9},{9,8},{10,11... | collective-permute-start | bytes 1769480 | tf_op jit(solution)/shard_map/ppermute | solution.py:1016
  639.5 19.2 %collective-permute-start.81 = (bf16[192,1536]{1,0:T(8,128)(2,1)S(1)}, bf16[192,1536]{1,0:T(8,128)(2,1)S(1)}, u32[]{:S(2)}, u32[]{:S(2)}) collective-permute-start(bf16[192,1536]{1,0:T(8,128)(2,1)S(1)} %collective-permute-done.80.refs_3_), channel_id=1, source_target_pairs={{0,1},{1,0},{2,3},{3,2},{4,5},{5,4},{6,7},{7,6},{8,9},{9,8},{10,11... | collective-permute-start | bytes 1769480 | tf_op jit(solution)/shard_map/ppermute | solution.py:1016
  640.8 23.6 %collective-permute-start.76 = (bf16[192,3072]{1,0:T(8,128)(2,1)S(1)}, bf16[192,3072]{1,0:T(8,128)(2,1)S(1)}, u32[]{:S(2)}, u32[]{:S(2)}) collective-permute-start(bf16[192,3072]{1,0:T(8,128)(2,1)S(1)} %pad_maximum_fusion.refs_1_), channel_id=1, source_target_pairs={{0,1},{1,0},{2,3},{3,2},{4,5},{5,4},{6,7},{7,6},{8,9},{9,8},{10,11... | collective-permute-start | bytes 3538952 | tf_op jit(solution)/shard_map/ppermute | solution.py:1016
  642.2 22.3 %collective-permute-start.78 = (bf16[192,3072]{1,0:T(8,128)(2,1)S(1)}, bf16[192,3072]{1,0:T(8,128)(2,1)S(1)}, u32[]{:S(2)}, u32[]{:S(2)}) collective-permute-start(bf16[192,3072]{1,0:T(8,128)(2,1)S(1)} %collective-permute-done.77.refs_3_), channel_id=1, source_target_pairs={{0,1},{1,0},{2,3},{3,2},{4,5},{5,4},{6,7},{7,6},{8,9},{9,8},{10,11... | collective-permute-start | bytes 3538952 | tf_op jit(solution)/shard_map/ppermute | solution.py:1016
  (145 other events, 2491.5 us)
Sparse Core Ops, SparseCore 0:
  308.0 109.7 reduce-scatter.1

commit v5 on v4

--- a/solution.py
+++ b/solution.py
@@ -400,11 +400,11 @@
             return carry
 
         lax.fori_loop(0, tiles, project, 0)
-        for c in range(tiles):
-            extent = (c + 1) * TILE
-
-            def attend(i, carry, c=c, extent=extent):
-                t = c * per + i
+        for low_t in range(0, nt, 2):
+            high_t = min(low_t + 2, nt)
+            extent = high_t * KEYROWS
+
+            def attend(t, carry, extent=extent):
                 bias = bias_for(t, extent, first_len)
                 mixed = []
                 for j in range(KVH):
@@ -418,7 +418,7 @@
                 heads[rows, :] = jnp.concatenate(mixed, 1).astype(BF)
                 return carry
 
-            lax.fori_loop(0, per, attend, 0)
+            lax.fori_loop(low_t, high_t, attend, 0)
 
     return pl.pallas_call(
         kernel,
@@ -518,11 +518,11 @@
             return carry
 
         lax.fori_loop(0, tiles, heads_back, 0)
-        for c in range(tiles):
-            extent = (c + 1) * TILE
-
-            def attend(i, carry, c=c, extent=extent):
-                t = c * per + i
+        for low_t in range(0, nt, 2):
+            high_t = min(low_t + 2, nt)
+            extent = high_t * KEYROWS
+
+            def attend(t, carry, extent=extent):
                 bias = bias_for(t, extent, first_len)
                 for j in range(KVH):
                     qb = q_ref[j, t]
@@ -541,7 +541,7 @@
                     dv_s[j, :extent, :] += dot_tn(p.astype(BF), db)
                 return carry
 
-            lax.fori_loop(0, per, attend, 0)
+            lax.fori_loop(low_t, high_t, attend, 0)
         wait_all(cw)
 
         def inputs_back(i, carry):

time: 737 us -> 735 us (level)
  transfers between devices with their start and end apart: 100 -> 100, of which waited for: 40 -> 41; matrix products, arithmetic and copies ran while one was open for 12% -> 12% of each run, Pallas kernels for 27% -> 27%
where the time goes in v5:
time: 735 us; the launch traced here: 727 us
  waiting for transfers between devices  208 us (28%)
  Pallas kernels  206 us (28%)
  starting transfers between devices  189 us (26%)
  other arithmetic  69.4 us (9%)
  local copies, waits for them, and re-layouts  33.9 us (5%)
  between operations  20.3 us (3%)
    ppermute x14, waiting for transfers between devices, step(): self.fs.append(lax.ppermute(after(self.fs[-1], *deps), 'dp', ahead))  88.4 us
    pallas_call x2, Pallas kernels, expert_kernel(): pl.pallas_call(kernel, grid=(tiles + cuts,), out_shape=(jax.ShapeDtypeStr...  85.2 us
    ppermute x39, starting transfers between devices, swap(): return lax.ppermute(values, 'seq', [(i, i ^ bits) for i in range(MEMBERS)])  71.1 us
    ppermute x39, waiting for transfers between devices, swap(): return lax.ppermute(values, 'seq', [(i, i ^ bits) for i in range(MEMBERS)])  44.8 us
    ppermute x14, starting transfers between devices, step(): self.fs.append(lax.ppermute(after(self.fs[-1], *deps), 'dp', ahead))  42.2 us
    pallas_call x1, Pallas kernels, attention_backward(): pl.pallas_call(kernel, out_shape=(jax.ShapeDtypeStruct((MEMBERS, nt, 32,...  37.3 us
    ppermute x14, waiting for transfers between devices, step(): b = lax.ppermute(after(self.sums[1], *deps), 'dp', back)  36.6 us
    convert_element_type x28, other arithmetic, step(): (got.astype(F32) + mine.astype(F32)).astype(BF)  32.3 us
  transfers between devices with their start and end apart: 100, of which 41 were waited for; matrix products, arithmetic and copies ran while one was open for 12% of the time, Pallas kernels for 27%

profile of v5, /device:TPU:1, one launch (start us, length us, event | category | flops | bytes accessed | tf_op | source)
XLA Modules:
  0.0 727.0 jit_solution(9407793614944729374)
XLA Ops:
  7.2 3.4 pick.1
  10.6 6.5 all-to-all-start
  25.8 4.2 pick_marked.1
  30.1 24.3 %collective-permute-done.refs_2_ = bf16[192,1408]{1,0:T(8,128)(2,1)S(1)} collective-permute-done((bf16[192,1408]{1,0:T(8,128)(2,1)S(1)}, bf16[192,1408]{1,0:T(8,128)(2,1)S(1)}, u32[]{:S(2)}, u32[]{:S(2)}) %collective-permute-start) | collective-permute-done | bytes 540704 | tf_op jit(solution)/shard_map/ppermute | solution.py:1155
  54.4 10.8 %collective-permute-start.1 = (bf16[192,1408]{1,0:T(8,128)(2,1)S(1)}, bf16[192,1408]{1,0:T(8,128)(2,1)S(1)}, u32[]{:S(2)}, u32[]{:S(2)}) collective-permute-start(bf16[192,1408]{1,0:T(8,128)(2,1)S(1)} %collective-permute-done.refs_2_), channel_id=1, source_target_pairs={{0,8},{8,16},{16,24},{24,28},{28,20},{20,12},{12,4},{4,0},{1,9},{9... | collective-permute-start | bytes 1622024 | tf_op jit(solution)/shard_map/ppermute | solution.py:1155
  82.7 6.0 collective-permute-done.2.refs_4_
  94.6 5.6 collective-permute-done.3.refs_5_
  102.5 8.5 %collective-permute-done.5.refs_6_ = bf16[192,1408]{1,0:T(8,128)(2,1)S(1)} collective-permute-done((bf16[192,1408]{1,0:T(8,128)(2,1)S(1)}, bf16[192,1408]{1,0:T(8,128)(2,1)S(1)}, u32[]{:S(2)}, u32[]{:S(2)}) %collective-permute-start.5) | collective-permute-done | bytes 540704 | tf_op jit(solution)/shard_map/ppermute | solution.py:1155
  113.2 8.5 %collective-permute-done.6.refs_7_ = bf16[192,1408]{1,0:T(8,128)(2,1)S(1)} collective-permute-done((bf16[192,1408]{1,0:T(8,128)(2,1)S(1)}, bf16[192,1408]{1,0:T(8,128)(2,1)S(1)}, u32[]{:S(2)}, u32[]{:S(2)}) %collective-permute-start.6) | collective-permute-done | bytes 540704 | tf_op jit(solution)/shard_map/ppermute | solution.py:1155
  125.2 7.6 %collective-permute-done.14.refs_16_ = bf16[192,1280]{1,0:T(8,128)(2,1)S(1)} collective-permute-done((bf16[192,1280]{1,0:T(8,128)(2,1)S(1)}, bf16[192,1280]{1,0:T(8,128)(2,1)S(1)}, u32[]{:S(2)}, u32[]{:S(2)}) %collective-permute-start.14) | collective-permute-done | bytes 491552 | tf_op jit(solution)/shard_map/ppermute | solution.py:1156
  132.8 6.7 all-to-all-start.1
  139.5 5.5 collective-permute-start.16
  161.9 21.9 %attention_forward.1 = (bf16[9,128,1536]{2,1,0:T(8,128)(2,1)}, bf16[2,9,384,64]{3,2,1,0:T(8,128)(2,1)}, bf16[2,1152,64]{2,1,0:T(8,128)(2,1)}, bf16[2,1152,64]{2,...) custom-call(s32[42]{0:T(128)S(1)} %concatenate.46.refs_0_.tab, ...), custom_call_target="tpu_custom_call" | custom-call | flops 120000000 | bytes 146800 | tf_op jit(solution)/shard_map/attention_forward/pallas_call | solution.py:423
  186.4 4.1 project_out.1
  194.7 6.8 collective-permute-start.18
  201.6 12.3 %collective-permute-done.18.refs_3_ = bf16[192,1536]{1,0:T(8,128)(2,1)S(1)} collective-permute-done((bf16[192,1536]{1,0:T(8,128)(2,1)}, bf16[192,1536]{1,0:T(8,128)(2,1)S(1)}, u32[]{:S(2)}, u32[]{:S(2)}) %collective-permute-start.18) | collective-permute-done | bytes 589856 | tf_op jit(solution)/shard_map/ppermute | solution.py:1155
  221.3 7.3 collective-permute-done.30.refs_4_
  230.4 10.2 %collective-permute-done.35.refs_5_ = bf16[192,1536]{1,0:T(8,128)(2,1)S(1)} collective-permute-done((bf16[192,1536]{1,0:T(8,128)(2,1)S(1)}, bf16[192,1536]{1,0:T(8,128)(2,1)S(1)}, u32[]{:S(2)}, u32[]{:S(2)}) %collective-permute-start.35) | collective-permute-done | bytes 589856 | tf_op jit(solution)/shard_map/ppermute | solution.py:1155
  240.6 4.1 collective-permute-start.36
  244.8 4.2 collective-permute-start.27
  249.0 4.5 collective-permute-done.36.refs_6_
  255.8 6.4 collective-permute-start.32
  266.8 4.1 collective-permute-start.29
  277.1 30.8 %expert.2 = (bf16[4,9,32,1664]{3,2,1,0:T(8,128)(2,1)}, bf16[4,9,32,1536]{3,2,1,0:T(8,128)(2,1)}, bf16[1536,1536]{1,0:T(8,128)(2,1)}) custom-call(s32[42]{0:T(128)} %copy-done.39, bf16[192,1408]{1,0:T(8,128)(2,1)} %copy-done.2, bf16[192,1408]{1,0:T(8,128)(2,1)} %copy-done.6, bf16[192,1408]{1,0:T(8,128)(2,1)} %copy-done.8, bf16[192,1408]{1,0:T(8,128)(2,1)} %copy-done.44, ...), custom_call_target="tpu_custom_call" | custom-call | flops 170000000 | bytes 272629 | tf_op jit(solution)/shard_map/expert/pallas_call | solution.py:917
  307.9 54.4 %expert.3 = (bf16[4,9,32,1664]{3,2,1,0:T(8,128)(2,1)}, bf16[4,9,32,1536]{3,2,1,0:T(8,128)(2,1)}, bf16[8,192,1536]{2,1,0:T(8,128)(2,1)}, bf16[8,192,1536]{2,1,0:T(8,128)(2,1)}) custom-call(s32[42]{0:T(128)} %copy-done.39, bf16[192,1536]{1,0:T(8,128)(2,1)} %get-tuple-element.101.refs_1_, bf16[192,1536]{1,0:T(8,128)(2,1)} %collective-permute-done.15.refs_2_, ...), custom_call_target="tpu_custom_call" | custom-call | flops 340000000 | bytes 419430 | tf_op jit(solution)/shard_map/expert/pallas_call | solution.py:917
  374.1 8.7 %collective-permute-done.50 = bf16[192,1536]{1,0:T(8,128)(2,1)S(1)} collective-permute-done((bf16[192,1536]{1,0:T(8,128)(2,1)S(1)}, bf16[192,1536]{1,0:T(8,128)(2,1)S(1)}, u32[]{:S(2)}, u32[]{:S(2)}) %collective-permute-start.50) | collective-permute-done | bytes 589856 | tf_op jit(solution)/shard_map/ppermute | solution.py:1173
  385.6 8.8 %collective-permute-done.45 = bf16[9,32,1664]{2,1,0:T(8,128)(2,1)S(1)} collective-permute-done((bf16[9,32,1664]{2,1,0:T(8,128)(2,1)S(1)}, bf16[9,32,1664]{2,1,0:T(8,128)(2,1)S(1)}, u32[]{:S(2)}, u32[]{:S(2)}) %collective-permute-start.45) | collective-permute-done | bytes 958496 | tf_op jit(solution)/shard_map/ppermute | solution.py:1016
  404.1 4.7 collective-permute-done.51
  410.4 4.1 collective-permute-start.52
  422.8 6.1 collective-permute-done.48.refs_19_.refs_7_
  431.6 4.2 collective-permute-done.56
  452.8 15.4 %all-to-all-start.2 = ((bf16[16,32,1536]{2,1,0:T(8,128)(2,1)}), bf16[16,32,1536]{2,1,0:T(8,128)(2,1)}, u32[]{:S(2)}, u32[]{:S(2)}) async-start(bf16[16,32,1536]{2,1,0:T(8,128)(2,1)} %spread_rows.2), calls=%async_computation.2 | async-start | bytes 3145728 | tf_op jit(solution)/shard_map/all_to_all | solution.py:1318
  473.6 37.3 %attention_backward.1 = (bf16[4,9,32,1536]{3,2,1,0:T(8,128)(2,1)}, bf16[1152,640]{1,0:T(8,128)(2,1)}) custom-call(s32[42]{0:T(128)} %copy-done.39, bf16[192,1408]{1,0:T(8,128)(2,1)} %copy-done.2, bf16[192,1408]{1,0:T(8,128)(2,1)} %copy-done.6, bf16[192,1408]{1,0:T(8,128)(2,1)} %copy-done.8, bf16[192,1408]{1,0:T(8,128)(2,1)} %copy-done.44, ...), custom_call_target="tpu_custom_call" | custom-call | flops 200000000 | bytes 167772 | tf_op jit(solution)/shard_map/attention_backward/pallas_call | solution.py:573
  512.8 10.2 %collective-permute-done.73 = bf16[192,1536]{1,0:T(8,128)(2,1)} collective-permute-done((bf16[192,1536]{1,0:T(8,128)(2,1)S(1)}, bf16[192,1536]{1,0:T(8,128)(2,1)}, u32[]{:S(2)}, u32[]{:S(2)}) %collective-permute-start.73) | collective-permute-done | bytes 589856 | tf_op jit(solution)/shard_map/ppermute | solution.py:1174
  530.8 12.1 %attention_grads.1 = (bf16[8,192,512]{2,1,0:T(8,128)(2,1)}, bf16[8,192,640]{2,1,0:T(8,128)(2,1)}, bf16[4,384,384]{2,1,0:T(8,128)(2,1)}) custom-call(s32[42]{0:T(128)S(1)} %copy-done.40, bf16[9,32,1536]{2,1,0:T(8,128)(2,1)S(1)} %copy-done.1, bf16[9,32,1536]{2,1,0:T(8,128)(2,1)S(1)} %copy-done.15, bf16[9,32,1536]{2,1,0:T(8,128)(2,1)S(1)} %copy-done.13, ...), custom_call_target="tpu_custom_call" | custom-call | flops 40000000 | bytes 167772 | tf_op jit(solution)/shard_map/attention_grads/pallas_call | solution.py:638
  542.9 4.4 collective-permute-start.61
  553.3 10.1 %collective-permute-done.75 = bf16[192,1536]{1,0:T(8,128)(2,1)S(1)} collective-permute-done((bf16[192,1536]{1,0:T(8,128)(2,1)S(1)}, bf16[192,1536]{1,0:T(8,128)(2,1)S(1)}, u32[]{:S(2)}, u32[]{:S(2)}) %collective-permute-start.75) | collective-permute-done | bytes 589856 | tf_op jit(solution)/shard_map/ppermute | solution.py:1174
  568.4 4.0 collective-permute-done.62
  576.7 3.5 collective-permute-start.63
  587.3 5.4 all-to-all-start.3
  593.8 10.3 %collective-permute-done.64.refs_3_ = bf16[384,384]{1,0:T(8,128)(2,1)} collective-permute-done((bf16[384,384]{1,0:T(8,128)(2,1)}, bf16[384,384]{1,0:T(8,128)(2,1)}, u32[]{:S(2)}, u32[]{:S(2)}) %collective-permute-start.64) | collective-permute-done | bytes 294944 | tf_op jit(solution)/shard_map/ppermute | solution.py:1016
  604.1 9.4 %collective-permute-done.65.refs_4_ = bf16[384,384]{1,0:T(8,128)(2,1)} collective-permute-done((bf16[384,384]{1,0:T(8,128)(2,1)}, bf16[384,384]{1,0:T(8,128)(2,1)}, u32[]{:S(2)}, u32[]{:S(2)}) %collective-permute-start.65) | collective-permute-done | bytes 294944 | tf_op jit(solution)/shard_map/ppermute | solution.py:1016
  625.7 9.1 %collective-permute-start.70 = (bf16[192,512]{1,0:T(8,128)(2,1)S(1)}, bf16[192,512]{1,0:T(8,128)(2,1)S(1)}, u32[]{:S(2)}, u32[]{:S(2)}) collective-permute-start(bf16[192,512]{1,0:T(8,128)(2,1)S(1)} %fusion.49), channel_id=1, source_target_pairs={{0,8},{8,16},{16,24},{24,28},{28,20},{20,12},{12,4},{4,0},{1,9},{9... | collective-permute-start | bytes 589832 | tf_op jit(solution)/shard_map/ppermute | solution.py:1173
  656.6 4.7 place_experts.2
  662.3 7.6 %place_experts.3 = (f32[12,192,1536]{2,1,0:T(8,128)}, f32[192,128]{1,0:T(8,128)S(1)}) custom-call(s32[4]{0:T(128)S(1)} %iota_xor_fusion.refs_0_, bf16[192,3072]{1,0:T(8,128)(2,1)S(1)} %pad_maximum_fusion.refs_1_, bf16[192,3072]{1,0:T(8,128)(2,1)S(1)} %collective-permute-done.76.refs_2_, ...), custom_call_target="tpu_custom_call", output_to_operand_aliasing={{0}: (6, {})} | custom-call | bytes 141557 | tf_op jit(solution)/shard_map/place_experts/pallas_call | solution.py:246
  687.4 3.8 collective-permute-done.84
  696.5 8.3 %collective-permute-start.92 = (bf16[192,1024]{1,0:T(8,128)(2,1)S(1)}, bf16[192,1024]{1,0:T(8,128)(2,1)S(1)}, u32[]{:S(2)}, u32[]{:S(2)}) collective-permute-start(bf16[192,1024]{1,0:T(8,128)(2,1)S(1)} %pad_maximum_fusion.7.refs_1_), channel_id=1, source_target_pairs={{0,1},{1,0},{2,3},{3,2},{4,5},{5,4},{6,7},{7,6},{8,9},{9,8},{10,11... | collective-permute-start | bytes 1179656 | tf_op jit(solution)/shard_map/ppermute | solution.py:1016
  704.8 6.3 collective-permute-start.94
  (470 shorter events, 239.6 us)
Async XLA Ops:
  10.6 61.0 %all-to-all-start = ((bf16[16,32,1536]{2,1,0:T(8,128)(2,1)}), bf16[16,32,1536]{2,1,0:T(8,128)(2,1)}, u32[]{:S(2)}, u32[]{:S(2)}) async-start(bf16[16,32,1536]{2,1,0:T(8,128)(2,1)} %pick.1), calls=%async_computation | async-start | bytes 3145728 | tf_op jit(solution)/shard_map/all_to_all | solution.py:1083
  22.3 32.1 %collective-permute-start = (bf16[192,1408]{1,0:T(8,128)(2,1)S(1)}, bf16[192,1408]{1,0:T(8,128)(2,1)S(1)}, u32[]{:S(2)}, u32[]{:S(2)}) collective-permute-start(bf16[192,1408]{1,0:T(8,128)(2,1)S(1)} %concatenate.41.refs_1_), channel_id=1, source_target_pairs={{0,8},{8,16},{16,24},{24,28},{28,20},{20,12},{12,4},{4,0},{1,9},{9... | collective-permute-start | bytes 1622024 | tf_op jit(solution)/shard_map/ppermute | solution.py:1155
  24.8 40.4 %collective-permute-start.8 = (bf16[192,1280]{1,0:T(8,128)(2,1)S(1)}, bf16[192,1280]{1,0:T(8,128)(2,1)S(1)}, u32[]{:S(2)}, u32[]{:S(2)}) collective-permute-start(bf16[192,1280]{1,0:T(8,128)(2,1)S(1)} %pad_maximum_fusion.6.refs_9_), channel_id=1, source_target_pairs={{8,0},{16,8},{24,16},{28,24},{20,28},{12,20},{4,12},{0,4},{9,1},{1... | collective-permute-start | bytes 1474568 | tf_op jit(solution)/shard_map/ppermute | solution.py:1156
  54.4 21.9 %collective-permute-start.1 = (bf16[192,1408]{1,0:T(8,128)(2,1)S(1)}, bf16[192,1408]{1,0:T(8,128)(2,1)S(1)}, u32[]{:S(2)}, u32[]{:S(2)}) collective-permute-start(bf16[192,1408]{1,0:T(8,128)(2,1)S(1)} %collective-permute-done.refs_2_), channel_id=1, source_target_pairs={{0,8},{8,16},{16,24},{24,28},{28,20},{20,12},{12,4},{4,0},{1,9},{9... | collective-permute-start | bytes 1622024 | tf_op jit(solution)/shard_map/ppermute | solution.py:1155
  73.9 20.7 %collective-permute-start.4 = (bf16[9,32,1536]{2,1,0:T(8,128)(2,1)}, bf16[9,32,1536]{2,1,0:T(8,128)(2,1)S(1)}, u32[]{:S(2)}, u32[]{:S(2)}) collective-permute-start(bf16[9,32,1536]{2,1,0:T(8,128)(2,1)} %take_rows.2.refs_17_), channel_id=1, source_target_pairs={{0,2},{1,3},{2,0},{3,1},{4,6},{5,7},{6,4},{7,5},{8,10},{9,11},{10,... | collective-permute-start | bytes 2654216 | tf_op jit(solution)/shard_map/ppermute | solution.py:1016
  132.8 51.0 %all-to-all-start.1 = ((bf16[16,32,1664]{2,1,0:T(8,128)(2,1)}), bf16[16,32,1664]{2,1,0:T(8,128)(2,1)}, u32[]{:S(2)}, u32[]{:S(2)}) async-start(bf16[16,32,1664]{2,1,0:T(8,128)(2,1)} %pick_marked.1), calls=%async_computation.1 | async-start | bytes 3407872 | tf_op jit(solution)/shard_map/all_to_all | solution.py:1213
  139.5 333.1 %reduce-scatter.2.cloned.1.call-start = ((), (), s32[]{:S(2)}) async-start(), calls=%async_computation.5 | async-start | bytes 5308416 | tf_op jit(solution)/shard_map/reduce_scatter | solution.py:1264
  145.8 40.5 %collective-permute-start.15 = (bf16[192,1536]{1,0:T(8,128)(2,1)}, bf16[192,1536]{1,0:T(8,128)(2,1)}, u32[]{:S(2)}, u32[]{:S(2)}) collective-permute-start(bf16[192,1536]{1,0:T(8,128)(2,1)} %get-tuple-element.101.refs_1_), channel_id=1, source_target_pairs={{0,8},{8,16},{16,24},{24,28},{28,20},{20,12},{12,4},{4,0},{1,9},{9... | collective-permute-start | bytes 1769480 | tf_op jit(solution)/shard_map/ppermute | solution.py:1155
  147.4 38.9 %collective-permute-start.19 = (bf16[192,1536]{1,0:T(8,128)(2,1)}, bf16[192,1536]{1,0:T(8,128)(2,1)}, u32[]{:S(2)}, u32[]{:S(2)}) collective-permute-start(bf16[192,1536]{1,0:T(8,128)(2,1)} %get-tuple-element.105.refs_9_), channel_id=1, source_target_pairs={{8,0},{16,8},{24,16},{28,24},{20,28},{12,20},{4,12},{0,4},{9,1},{1... | collective-permute-start | bytes 1769480 | tf_op jit(solution)/shard_map/ppermute | solution.py:1156
  153.5 32.9 %collective-permute-start.21 = (bf16[384,384]{1,0:T(8,128)(2,1)}, bf16[384,384]{1,0:T(8,128)(2,1)}, u32[]{:S(2)}, u32[]{:S(2)}) collective-permute-start(bf16[384,384]{1,0:T(8,128)(2,1)} %get-tuple-element.230), channel_id=1, source_target_pairs={{0,1},{1,0},{2,3},{3,2},{4,5},{5,4},{6,7},{7,6},{8,9},{9,8},{10,11... | collective-permute-start | bytes 884744 | tf_op jit(solution)/shard_map/ppermute | solution.py:1016
  154.3 32.1 %collective-permute-start.22 = (bf16[384,384]{1,0:T(8,128)(2,1)}, bf16[384,384]{1,0:T(8,128)(2,1)}, u32[]{:S(2)}, u32[]{:S(2)}) collective-permute-start(bf16[384,384]{1,0:T(8,128)(2,1)} %get-tuple-element.229), channel_id=1, source_target_pairs={{0,2},{1,3},{2,0},{3,1},{4,6},{5,7},{6,4},{7,5},{8,10},{9,11},{10,... | collective-permute-start | bytes 884744 | tf_op jit(solution)/shard_map/ppermute | solution.py:1016
  155.5 30.9 %collective-permute-start.23 = (bf16[384,384]{1,0:T(8,128)(2,1)}, bf16[384,384]{1,0:T(8,128)(2,1)}, u32[]{:S(2)}, u32[]{:S(2)}) collective-permute-start(bf16[384,384]{1,0:T(8,128)(2,1)} %get-tuple-element.228), channel_id=1, source_target_pairs={{0,3},{1,2},{2,1},{3,0},{4,7},{5,6},{6,5},{7,4},{8,11},{9,10},{10,... | collective-permute-start | bytes 884744 | tf_op jit(solution)/shard_map/ppermute | solution.py:1016
  190.9 26.5 %collective-permute-start.24 = (bf16[9,32,1536]{2,1,0:T(8,128)(2,1)S(1)}, bf16[9,32,1536]{2,1,0:T(8,128)(2,1)S(1)}, u32[]{:S(2)}, u32[]{:S(2)}) collective-permute-start(bf16[9,32,1536]{2,1,0:T(8,128)(2,1)S(1)} %get-tuple-element.214), channel_id=1, source_target_pairs={{0,1},{1,0},{2,3},{3,2},{4,5},{5,4},{6,7},{7,6},{8,9},{9,8},{10,11... | collective-permute-start | bytes 2654216 | tf_op jit(solution)/shard_map/ppermute | solution.py:1016
  193.4 24.0 %collective-permute-start.26 = (bf16[9,32,1536]{2,1,0:T(8,128)(2,1)S(1)}, bf16[9,32,1536]{2,1,0:T(8,128)(2,1)S(1)}, u32[]{:S(2)}, u32[]{:S(2)}) collective-permute-start(bf16[9,32,1536]{2,1,0:T(8,128)(2,1)S(1)} %fusion.6), channel_id=1, source_target_pairs={{0,2},{1,3},{2,0},{3,1},{4,6},{5,7},{6,4},{7,5},{8,10},{9,11},{10,... | collective-permute-start | bytes 2654216 | tf_op jit(solution)/shard_map/ppermute | solution.py:1016
  194.7 19.1 %collective-permute-start.18 = (bf16[192,1536]{1,0:T(8,128)(2,1)}, bf16[192,1536]{1,0:T(8,128)(2,1)S(1)}, u32[]{:S(2)}, u32[]{:S(2)}) collective-permute-start(bf16[192,1536]{1,0:T(8,128)(2,1)} %collective-permute-done.15.refs_2_), channel_id=1, source_target_pairs={{0,8},{8,16},{16,24},{24,28},{28,20},{20,12},{12,4},{4,0},{1,9},{9... | collective-permute-start | bytes 1769480 | tf_op jit(solution)/shard_map/ppermute | solution.py:1155
  221.0 19.6 %collective-permute-start.28 = (bf16[9,32,1536]{2,1,0:T(8,128)(2,1)S(1)}, bf16[9,32,1536]{2,1,0:T(8,128)(2,1)S(1)}, u32[]{:S(2)}, u32[]{:S(2)}) collective-permute-start(bf16[9,32,1536]{2,1,0:T(8,128)(2,1)S(1)} %multiply_convert_fusion.refs_17_.refs_1_), channel_id=1, source_target_pairs={{0,2},{1,3},{2,0},{3,1},{4,6},{5,7},{6,4},{7,5},{8,10},{9,11},{10,... | collective-permute-start | bytes 2654216 | tf_op jit(solution)/shard_map/ppermute | solution.py:1016
  230.2 32.1 %collective-permute-start.33 = (bf16[9,32,1664]{2,1,0:T(8,128)(2,1)}, bf16[9,32,1664]{2,1,0:T(8,128)(2,1)}, u32[]{:S(2)}, u32[]{:S(2)}) collective-permute-start(bf16[9,32,1664]{2,1,0:T(8,128)(2,1)} %take_rows.3.refs_21_), channel_id=1, source_target_pairs={{0,2},{1,3},{2,0},{3,1},{4,6},{5,7},{6,4},{7,5},{8,10},{9,11},{10,... | collective-permute-start | bytes 2875400 | tf_op jit(solution)/shard_map/ppermute | solution.py:1016
  244.8 29.0 %collective-permute-start.27 = (bf16[9,32,1536]{2,1,0:T(8,128)(2,1)S(1)}, bf16[9,32,1536]{2,1,0:T(8,128)(2,1)S(1)}, u32[]{:S(2)}, u32[]{:S(2)}) collective-permute-start(bf16[9,32,1536]{2,1,0:T(8,128)(2,1)S(1)} %multiply_convert_fusion.refs_17_.refs_1_), channel_id=1, source_target_pairs={{0,1},{1,0},{2,3},{3,2},{4,5},{5,4},{6,7},{7,6},{8,9},{9,8},{10,11... | collective-permute-start | bytes 2654216 | tf_op jit(solution)/shard_map/ppermute | solution.py:1016
  255.8 21.2 %collective-permute-start.32 = (bf16[9,32,1664]{2,1,0:T(8,128)(2,1)}, bf16[9,32,1664]{2,1,0:T(8,128)(2,1)}, u32[]{:S(2)}, u32[]{:S(2)}) collective-permute-start(bf16[9,32,1664]{2,1,0:T(8,128)(2,1)} %take_rows.3.refs_21_), channel_id=1, source_target_pairs={{0,1},{1,0},{2,3},{3,2},{4,5},{5,4},{6,7},{7,6},{8,9},{9,8},{10,11... | collective-permute-start | bytes 2875400 | tf_op jit(solution)/shard_map/ppermute | solution.py:1016
  271.4 36.5 %collective-permute-start.38 = (bf16[192,1536]{1,0:T(8,128)(2,1)}, bf16[192,1536]{1,0:T(8,128)(2,1)}, u32[]{:S(2)}, u32[]{:S(2)}) collective-permute-start(bf16[192,1536]{1,0:T(8,128)(2,1)} %collective-permute-done.37.refs_7_), channel_id=1, source_target_pairs={{0,8},{8,16},{16,24},{24,28},{28,20},{20,12},{12,4},{4,0},{1,9},{9... | collective-permute-start | bytes 1769480 | tf_op jit(solution)/shard_map/ppermute | solution.py:1155
  273.8 34.2 %collective-permute-start.42 = (bf16[192,1536]{1,0:T(8,128)(2,1)}, bf16[192,1536]{1,0:T(8,128)(2,1)}, u32[]{:S(2)}, u32[]{:S(2)}) collective-permute-start(bf16[192,1536]{1,0:T(8,128)(2,1)} %collective-permute-done.41.refs_15_), channel_id=1, source_target_pairs={{8,0},{16,8},{24,16},{28,24},{20,28},{12,20},{4,12},{0,4},{9,1},{1... | collective-permute-start | bytes 1769480 | tf_op jit(solution)/shard_map/ppermute | solution.py:1156
  366.4 19.2 %collective-permute-start.43 = (bf16[9,32,1664]{2,1,0:T(8,128)(2,1)S(1)}, bf16[9,32,1664]{2,1,0:T(8,128)(2,1)S(1)}, u32[]{:S(2)}, u32[]{:S(2)}) collective-permute-start(bf16[9,32,1664]{2,1,0:T(8,128)(2,1)S(1)} %get-tuple-element.208), channel_id=1, source_target_pairs={{0,1},{1,0},{2,3},{3,2},{4,5},{5,4},{6,7},{7,6},{8,9},{9,8},{10,11... | collective-permute-start | bytes 2875400 | tf_op jit(solution)/shard_map/ppermute | solution.py:1016
  372.8 21.6 %collective-permute-start.45 = (bf16[9,32,1664]{2,1,0:T(8,128)(2,1)S(1)}, bf16[9,32,1664]{2,1,0:T(8,128)(2,1)S(1)}, u32[]{:S(2)}, u32[]{:S(2)}) collective-permute-start(bf16[9,32,1664]{2,1,0:T(8,128)(2,1)S(1)} %fusion.1), channel_id=1, source_target_pairs={{0,2},{1,3},{2,0},{3,1},{4,6},{5,7},{6,4},{7,5},{8,10},{9,11},{10,... | collective-permute-start | bytes 2875400 | tf_op jit(solution)/shard_map/ppermute | solution.py:1016
  384.1 24.7 %collective-permute-start.51 = (bf16[192,1536]{1,0:T(8,128)(2,1)S(1)}, bf16[192,1536]{1,0:T(8,128)(2,1)S(1)}, u32[]{:S(2)}, u32[]{:S(2)}) collective-permute-start(bf16[192,1536]{1,0:T(8,128)(2,1)S(1)} %fusion.31), channel_id=1, source_target_pairs={{0,8},{8,16},{16,24},{24,28},{28,20},{20,12},{12,4},{4,0},{1,9},{9... | collective-permute-start | bytes 1769480 | tf_op jit(solution)/shard_map/ppermute | solution.py:1173
  384.2 32.9 %collective-permute-start.55 = (bf16[192,1536]{1,0:T(8,128)(2,1)S(1)}, bf16[192,1536]{1,0:T(8,128)(2,1)S(1)}, u32[]{:S(2)}, u32[]{:S(2)}) collective-permute-start(bf16[192,1536]{1,0:T(8,128)(2,1)S(1)} %fusion.27), channel_id=1, source_target_pairs={{8,0},{16,8},{24,16},{28,24},{20,28},{12,20},{4,12},{0,4},{9,1},{1... | collective-permute-start | bytes 1769480 | tf_op jit(solution)/shard_map/ppermute | solution.py:1174
  402.0 17.9 %collective-permute-start.47 = (bf16[9,32,1536]{2,1,0:T(8,128)(2,1)S(1)}, bf16[9,32,1536]{2,1,0:T(8,128)(2,1)S(1)}, u32[]{:S(2)}, u32[]{:S(2)}) collective-permute-start(bf16[9,32,1536]{2,1,0:T(8,128)(2,1)S(1)} %get-tuple-element.125), channel_id=1, source_target_pairs={{0,1},{1,0},{2,3},{3,2},{4,5},{5,4},{6,7},{7,6},{8,9},{9,8},{10,11... | collective-permute-start | bytes 2654216 | tf_op jit(solution)/shard_map/ppermute | solution.py:1016
  408.9 19.9 %collective-permute-start.48 = (bf16[9,32,1664]{2,1,0:T(8,128)(2,1)S(1)}, bf16[9,32,1664]{2,1,0:T(8,128)(2,1)S(1)}, u32[]{:S(2)}, u32[]{:S(2)}) collective-permute-start(bf16[9,32,1664]{2,1,0:T(8,128)(2,1)S(1)} %bitcast.218), channel_id=1, source_target_pairs={{0,2},{1,3},{2,0},{3,1},{4,6},{5,7},{6,4},{7,5},{8,10},{9,11},{10,... | collective-permute-start | bytes 2875400 | tf_op jit(solution)/shard_map/ppermute | solution.py:1016
  410.4 21.1 %collective-permute-start.52 = (bf16[192,1536]{1,0:T(8,128)(2,1)S(1)}, bf16[192,1536]{1,0:T(8,128)(2,1)S(1)}, u32[]{:S(2)}, u32[]{:S(2)}) collective-permute-start(bf16[192,1536]{1,0:T(8,128)(2,1)S(1)} %fusion.30), channel_id=1, source_target_pairs={{0,8},{8,16},{16,24},{24,28},{28,20},{20,12},{12,4},{4,0},{1,9},{9... | collective-permute-start | bytes 1769480 | tf_op jit(solution)/shard_map/ppermute | solution.py:1173
  418.4 54.3 %collective-permute-start.58 = (bf16[9,32,1664]{2,1,0:T(8,128)(2,1)S(1)}, bf16[9,32,1664]{2,1,0:T(8,128)(2,1)S(1)}, u32[]{:S(2)}, u32[]{:S(2)}) collective-permute-start(bf16[9,32,1664]{2,1,0:T(8,128)(2,1)S(1)} %bitcast.219), channel_id=1, source_target_pairs={{0,1},{1,0},{2,3},{3,2},{4,5},{5,4},{6,7},{7,6},{8,9},{9,8},{10,11... | collective-permute-start | bytes 2875400 | tf_op jit(solution)/shard_map/ppermute | solution.py:1016
  419.8 22.9 %collective-permute-start.46 = (bf16[9,32,1536]{2,1,0:T(8,128)(2,1)S(1)}, bf16[9,32,1536]{2,1,0:T(8,128)(2,1)S(1)}, u32[]{:S(2)}, u32[]{:S(2)}) collective-permute-start(bf16[9,32,1536]{2,1,0:T(8,128)(2,1)S(1)} %get-tuple-element.124), channel_id=1, source_target_pairs={{0,1},{1,0},{2,3},{3,2},{4,5},{5,4},{6,7},{7,6},{8,9},{9,8},{10,11... | collective-permute-start | bytes 2654216 | tf_op jit(solution)/shard_map/ppermute | solution.py:1016
  428.8 18.3 %collective-permute-start.49 = (bf16[9,32,1536]{2,1,0:T(8,128)(2,1)S(1)}, bf16[9,32,1536]{2,1,0:T(8,128)(2,1)S(1)}, u32[]{:S(2)}, u32[]{:S(2)}) collective-permute-start(bf16[9,32,1536]{2,1,0:T(8,128)(2,1)S(1)} %fusion.14), channel_id=1, source_target_pairs={{0,2},{1,3},{2,0},{3,1},{4,6},{5,7},{6,4},{7,5},{8,10},{9,11},{10,... | collective-permute-start | bytes 2654216 | tf_op jit(solution)/shard_map/ppermute | solution.py:1016
  437.9 30.3 %collective-permute-start.53 = (bf16[192,1536]{1,0:T(8,128)(2,1)S(1)}, bf16[192,1536]{1,0:T(8,128)(2,1)}, u32[]{:S(2)}, u32[]{:S(2)}) collective-permute-start(bf16[192,1536]{1,0:T(8,128)(2,1)S(1)} %fusion.29), channel_id=1, source_target_pairs={{0,8},{8,16},{16,24},{24,28},{28,20},{20,12},{12,4},{4,0},{1,9},{9... | collective-permute-start | bytes 1769480 | tf_op jit(solution)/shard_map/ppermute | solution.py:1173
  439.9 30.5 %collective-permute-start.57 = (bf16[192,1536]{1,0:T(8,128)(2,1)}, bf16[192,1536]{1,0:T(8,128)(2,1)}, u32[]{:S(2)}, u32[]{:S(2)}) collective-permute-start(bf16[192,1536]{1,0:T(8,128)(2,1)} %fusion.25), channel_id=1, source_target_pairs={{8,0},{16,8},{24,16},{28,24},{20,28},{12,20},{4,12},{0,4},{9,1},{1... | collective-permute-start | bytes 1769480 | tf_op jit(solution)/shard_map/ppermute | solution.py:1174
  442.7 30.0 %collective-permute-start.59 = (bf16[9,32,1664]{2,1,0:T(8,128)(2,1)S(1)}, bf16[9,32,1664]{2,1,0:T(8,128)(2,1)}, u32[]{:S(2)}, u32[]{:S(2)}) collective-permute-start(bf16[9,32,1664]{2,1,0:T(8,128)(2,1)S(1)} %collective-permute-done.48.refs_19_.refs_7_), channel_id=1, source_target_pairs={{0,1},{1,0},{2,3},{3,2},{4,5},{5,4},{6,7},{7,6},{8,9},{9,8},{10,11... | collective-permute-start | bytes 2875400 | tf_op jit(solution)/shard_map/ppermute | solution.py:1016
  452.8 90.1 %all-to-all-start.2 = ((bf16[16,32,1536]{2,1,0:T(8,128)(2,1)}), bf16[16,32,1536]{2,1,0:T(8,128)(2,1)}, u32[]{:S(2)}, u32[]{:S(2)}) async-start(bf16[16,32,1536]{2,1,0:T(8,128)(2,1)} %spread_rows.2), calls=%async_computation.2 | async-start | bytes 3145728 | tf_op jit(solution)/shard_map/all_to_all | solution.py:1318
  524.4 23.0 %collective-permute-start.74 = (bf16[192,1536]{1,0:T(8,128)(2,1)S(1)}, bf16[192,1536]{1,0:T(8,128)(2,1)}, u32[]{:S(2)}, u32[]{:S(2)}) collective-permute-start(bf16[192,1536]{1,0:T(8,128)(2,1)S(1)} %fusion.20), channel_id=1, source_target_pairs={{8,0},{16,8},{24,16},{28,24},{20,28},{12,20},{4,12},{0,4},{9,1},{1... | collective-permute-start | bytes 1769480 | tf_op jit(solution)/shard_map/ppermute | solution.py:1174
  527.8 22.7 %collective-permute-start.67 = (bf16[192,1536]{1,0:T(8,128)(2,1)}, bf16[192,1536]{1,0:T(8,128)(2,1)}, u32[]{:S(2)}, u32[]{:S(2)}) collective-permute-start(bf16[192,1536]{1,0:T(8,128)(2,1)} %fusion.23), channel_id=1, source_target_pairs={{0,8},{8,16},{16,24},{24,28},{28,20},{20,12},{12,4},{4,0},{1,9},{9... | collective-permute-start | bytes 1769480 | tf_op jit(solution)/shard_map/ppermute | solution.py:1173
  547.3 21.1 %collective-permute-start.60 = (bf16[9,32,1536]{2,1,0:T(8,128)(2,1)}, bf16[9,32,1536]{2,1,0:T(8,128)(2,1)S(1)}, u32[]{:S(2)}, u32[]{:S(2)}) collective-permute-start(bf16[9,32,1536]{2,1,0:T(8,128)(2,1)} %get-tuple-element.144), channel_id=1, source_target_pairs={{0,1},{1,0},{2,3},{3,2},{4,5},{5,4},{6,7},{7,6},{8,9},{9,8},{10,11... | collective-permute-start | bytes 2654216 | tf_op jit(solution)/shard_map/ppermute | solution.py:1016
  552.2 20.2 %collective-permute-start.62 = (bf16[9,32,1536]{2,1,0:T(8,128)(2,1)S(1)}, bf16[9,32,1536]{2,1,0:T(8,128)(2,1)S(1)}, u32[]{:S(2)}, u32[]{:S(2)}) collective-permute-start(bf16[9,32,1536]{2,1,0:T(8,128)(2,1)S(1)} %fusion.4), channel_id=1, source_target_pairs={{0,2},{1,3},{2,0},{3,1},{4,6},{5,7},{6,4},{7,5},{8,10},{9,11},{10,... | collective-permute-start | bytes 2654216 | tf_op jit(solution)/shard_map/ppermute | solution.py:1016
  567.3 72.6 %collective-permute-start.77 = (bf16[192,3072]{1,0:T(8,128)(2,1)S(1)}, bf16[192,3072]{1,0:T(8,128)(2,1)S(1)}, u32[]{:S(2)}, u32[]{:S(2)}) collective-permute-start(bf16[192,3072]{1,0:T(8,128)(2,1)S(1)} %pad_maximum_fusion.refs_1_), channel_id=1, source_target_pairs={{0,2},{1,3},{2,0},{3,1},{4,6},{5,7},{6,4},{7,5},{8,10},{9,11},{10,... | collective-permute-start | bytes 3538952 | tf_op jit(solution)/shard_map/ppermute | solution.py:1016
  580.2 23.9 %collective-permute-start.64 = (bf16[384,384]{1,0:T(8,128)(2,1)}, bf16[384,384]{1,0:T(8,128)(2,1)}, u32[]{:S(2)}, u32[]{:S(2)}) collective-permute-start(bf16[384,384]{1,0:T(8,128)(2,1)} %get-tuple-element.225), channel_id=1, source_target_pairs={{0,2},{1,3},{2,0},{3,1},{4,6},{5,7},{6,4},{7,5},{8,10},{9,11},{10,... | collective-permute-start | bytes 884744 | tf_op jit(solution)/shard_map/ppermute | solution.py:1016
  581.2 32.4 %collective-permute-start.65 = (bf16[384,384]{1,0:T(8,128)(2,1)}, bf16[384,384]{1,0:T(8,128)(2,1)}, u32[]{:S(2)}, u32[]{:S(2)}) collective-permute-start(bf16[384,384]{1,0:T(8,128)(2,1)} %get-tuple-element.224), channel_id=1, source_target_pairs={{0,3},{1,2},{2,1},{3,0},{4,7},{5,6},{6,5},{7,4},{8,11},{9,10},{10,... | collective-permute-start | bytes 884744 | tf_op jit(solution)/shard_map/ppermute | solution.py:1016
  587.3 88.2 %all-to-all-start.3 = ((bf16[16,32,1536]{2,1,0:T(8,128)(2,1)}), bf16[16,32,1536]{2,1,0:T(8,128)(2,1)}, u32[]{:S(2)}, u32[]{:S(2)}) async-start(bf16[16,32,1536]{2,1,0:T(8,128)(2,1)} %spread_rows.3), calls=%async_computation.4 | async-start | bytes 3145728 | tf_op jit(solution)/shard_map/all_to_all | solution.py:1345
  592.7 44.6 %collective-permute-start.80 = (bf16[192,1536]{1,0:T(8,128)(2,1)S(1)}, bf16[192,1536]{1,0:T(8,128)(2,1)S(1)}, u32[]{:S(2)}, u32[]{:S(2)}) collective-permute-start(bf16[192,1536]{1,0:T(8,128)(2,1)S(1)} %copy-done.36), channel_id=1, source_target_pairs={{0,2},{1,3},{2,0},{3,1},{4,6},{5,7},{6,4},{7,5},{8,10},{9,11},{10,... | collective-permute-start | bytes 1769480 | tf_op jit(solution)/shard_map/ppermute | solution.py:1016
  636.8 18.7 %collective-permute-start.79 = (bf16[192,1536]{1,0:T(8,128)(2,1)S(1)}, bf16[192,1536]{1,0:T(8,128)(2,1)S(1)}, u32[]{:S(2)}, u32[]{:S(2)}) collective-permute-start(bf16[192,1536]{1,0:T(8,128)(2,1)S(1)} %copy-done.36), channel_id=1, source_target_pairs={{0,1},{1,0},{2,3},{3,2},{4,5},{5,4},{6,7},{7,6},{8,9},{9,8},{10,11... | collective-permute-start | bytes 1769480 | tf_op jit(solution)/shard_map/ppermute | solution.py:1016
  637.3 19.3 %collective-permute-start.81 = (bf16[192,1536]{1,0:T(8,128)(2,1)S(1)}, bf16[192,1536]{1,0:T(8,128)(2,1)S(1)}, u32[]{:S(2)}, u32[]{:S(2)}) collective-permute-start(bf16[192,1536]{1,0:T(8,128)(2,1)S(1)} %collective-permute-done.80.refs_3_), channel_id=1, source_target_pairs={{0,1},{1,0},{2,3},{3,2},{4,5},{5,4},{6,7},{7,6},{8,9},{9,8},{10,11... | collective-permute-start | bytes 1769480 | tf_op jit(solution)/shard_map/ppermute | solution.py:1016
  638.6 23.7 %collective-permute-start.76 = (bf16[192,3072]{1,0:T(8,128)(2,1)S(1)}, bf16[192,3072]{1,0:T(8,128)(2,1)S(1)}, u32[]{:S(2)}, u32[]{:S(2)}) collective-permute-start(bf16[192,3072]{1,0:T(8,128)(2,1)S(1)} %pad_maximum_fusion.refs_1_), channel_id=1, source_target_pairs={{0,1},{1,0},{2,3},{3,2},{4,5},{5,4},{6,7},{7,6},{8,9},{9,8},{10,11... | collective-permute-start | bytes 3538952 | tf_op jit(solution)/shard_map/ppermute | solution.py:1016
  640.0 22.3 %collective-permute-start.78 = (bf16[192,3072]{1,0:T(8,128)(2,1)S(1)}, bf16[192,3072]{1,0:T(8,128)(2,1)S(1)}, u32[]{:S(2)}, u32[]{:S(2)}) collective-permute-start(bf16[192,3072]{1,0:T(8,128)(2,1)S(1)} %collective-permute-done.77.refs_3_), channel_id=1, source_target_pairs={{0,1},{1,0},{2,3},{3,2},{4,5},{5,4},{6,7},{7,6},{8,9},{9,8},{10,11... | collective-permute-start | bytes 3538952 | tf_op jit(solution)/shard_map/ppermute | solution.py:1016
  (145 other events, 2480.8 us)
Sparse Core Ops, SparseCore 0:
  308.0 108.9 reduce-scatter.1
